TPU v7x, 512 devices: a whole 4x8x8 slice. The times are simulated.
512 devices in a mesh: dp: 2 (over core), section: 8 (over z), mp: 32 (over x, y).
Axes of the slice: x: 4, y: 8, z: 8, core: 2. Of those that a mesh axis runs over, the one named last changes fastest.
Arguments:
- activations: bfloat16 [2, 8, 128, 128, 384], P('dp', 'section', 'mp'), may hold values from -8 to 8
- out_grads: bfloat16 [2, 8, 128, 128, 384], P('dp', 'section', 'mp'), may hold values from -6 to 6
- layer_weights: bfloat16 [8, 4, 384, 384], P('section'), may hold values from -1.5 to 1.5
Outputs:
- received: bfloat16 [2, 8, 128, 128, 384], P('dp', 'section', 'mp')
- weight_grads: float32 [8, 4, 384, 384], P('section', 'dp', 'mp')
All inputs are finite; a program needn't handle non-finite values.
Results may differ from a plain program's by a relative error of at most 0.011.
Values may be sent and summed in bfloat16 or wider, within the bound.
No kernel may reach another device: no remote copies, remote signals or barrier semaphores. Data moves between devices by JAX's collectives and lax.ppermute only.
A program may use at most 64 MiB of HBM per device.

v0:
```python
import jax
import jax.numpy as jnp
from jax import lax
from jax.sharding import PartitionSpec as P

HEAD_DIM = 64


EPS = 1e-05


def passed_along(array, axis, by):
    peers = lax.axis_size(axis)
    pairs = [(i, i + by) for i in range(peers) if 0 <= i + by < peers]
    return lax.ppermute(array, axis, pairs)


def normalize(values):
    mean_value = jnp.mean(values, axis=-1, keepdims=True)
    centred = values - mean_value
    inverse = lax.rsqrt(jnp.mean(centred * centred, axis=-1, keepdims=True) + EPS)
    return (centred * inverse, inverse)


def norm_backward(grad_in, standard, inverse):
    grad_mean = jnp.mean(grad_in, axis=-1, keepdims=True)
    grad_proj = jnp.mean(grad_in * standard, axis=-1, keepdims=True)
    return inverse * (grad_in - grad_mean - standard * grad_proj)


def attend(queries, key_rows, values_in, out_delta):
    seq_count, res_count, head_width = queries.shape
    head_shape = (seq_count, res_count, head_width // HEAD_DIM, HEAD_DIM)
    query_heads = queries.reshape(head_shape)
    key_heads = key_rows.reshape(head_shape)
    value_heads = values_in.reshape(head_shape)
    delta_heads = out_delta.reshape(head_shape)
    scaling = HEAD_DIM ** (-0.5)
    scores = (
        jnp.einsum("srhe,trhe->rhst", query_heads, key_heads, preferred_element_type=jnp.float32)
        * scaling
    )
    row_max = jnp.max(scores, axis=-1, keepdims=True)
    exponent = jnp.exp(scores - row_max)
    probs = exponent / jnp.sum(exponent, axis=-1, keepdims=True)
    soft = probs.astype(jnp.bfloat16)
    attn_out = jnp.einsum(
        "rhst,trhe->srhe", soft, value_heads, preferred_element_type=jnp.float32
    ).astype(jnp.bfloat16)
    dprobs = jnp.einsum(
        "srhe,trhe->rhst", delta_heads, value_heads, preferred_element_type=jnp.float32
    )
    row_delta = jnp.sum(probs * dprobs, axis=-1, keepdims=True)
    dscores = (probs * (dprobs - row_delta)).astype(jnp.bfloat16)
    query_grad = (
        jnp.einsum("rhst,trhe->srhe", dscores, key_heads, preferred_element_type=jnp.float32)
        * scaling
    ).astype(jnp.bfloat16)
    key_grad = (
        jnp.einsum("rhst,srhe->trhe", dscores, query_heads, preferred_element_type=jnp.float32)
        * scaling
    ).astype(jnp.bfloat16)
    value_grad = jnp.einsum(
        "rhst,srhe->trhe", soft, delta_heads, preferred_element_type=jnp.float32
    ).astype(jnp.bfloat16)
    flat_shape = (seq_count, res_count, head_width)
    return (
        attn_out.reshape(flat_shape),
        jnp.stack(
            [
                query_grad.reshape(flat_shape),
                key_grad.reshape(flat_shape),
                value_grad.reshape(flat_shape),
            ]
        ),
    )


def input_gradient(dprojected, weight, standard, inverse, out_flat):
    normed_grad = jnp.einsum(
        "nth,ndh->td", dprojected, weight[:3], preferred_element_type=jnp.float32
    )
    branch = lax.optimization_barrier(
        norm_backward(normed_grad, standard, inverse).astype(jnp.bfloat16)
    )
    return (out_flat.astype(jnp.float32) + branch.astype(jnp.float32)).astype(jnp.bfloat16)


def per_device(activations, out_grads, layer_weights):
    weight = layer_weights[0]
    model_width = activations.shape[4]
    head_width = weight.shape[2]
    row_count, res_total = (activations.shape[2], activations.shape[3])
    tokens = row_count * res_total
    standard, inverse = normalize(activations.reshape(tokens, model_width).astype(jnp.float32))
    normed = standard.astype(jnp.bfloat16)
    out_flat = out_grads.reshape(tokens, model_width)
    projected = jnp.einsum(
        "td,ndh->nth", normed, weight[:3], preferred_element_type=jnp.float32
    ).astype(jnp.bfloat16)
    attn_grad = jnp.dot(out_flat, weight[3], preferred_element_type=jnp.float32).astype(
        jnp.bfloat16
    )
    col_proj, col_attn_grad = (
        lax.all_to_all(
            projected.reshape(3, row_count, res_total, head_width),
            "mp",
            split_axis=2,
            concat_axis=1,
            tiled=True,
        ),
        lax.all_to_all(
            attn_grad.reshape(1, row_count, res_total, head_width),
            "mp",
            split_axis=2,
            concat_axis=1,
            tiled=True,
        ),
    )
    attn_out, stacked_grads = attend(col_proj[0], col_proj[1], col_proj[2], col_attn_grad[0])
    back_grads, back_out = (
        lax.all_to_all(stacked_grads, "mp", split_axis=1, concat_axis=2, tiled=True),
        lax.all_to_all(attn_out[None], "mp", split_axis=1, concat_axis=2, tiled=True),
    )
    dprojected = back_grads.reshape(3, tokens, head_width)
    attn_flat = back_out.reshape(tokens, head_width)
    input_grad = input_gradient(dprojected, weight, standard, inverse, out_flat)
    row_grads = input_grad.reshape(activations.shape)
    received = passed_along(row_grads, "section", -1)
    projection_terms = jnp.einsum(
        "td,nth->ndh", normed, dprojected, preferred_element_type=jnp.float32
    )
    output_term = jnp.einsum("td,th->dh", out_flat, attn_flat, preferred_element_type=jnp.float32)
    grad_term = jnp.concatenate([projection_terms, output_term[None]], axis=0)[None]
    model_part = lax.psum_scatter(grad_term, "mp", scatter_dimension=2, tiled=True)
    replica_part = lax.psum_scatter(model_part, "dp", scatter_dimension=1, tiled=True)
    return (received, replica_part)


def solution(mesh):
    in_specs = (
        P("dp", "section", "mp", None, None),
        P("dp", "section", "mp", None, None),
        P("section", None, None, None),
    )
    out_specs = (P("dp", "section", "mp", None, None), P("section", "dp", "mp", None))
    return jax.shard_map(
        per_device, mesh=mesh, in_specs=in_specs, out_specs=out_specs, check_vma=False
    )
```

profile of v0, /device:TPU:1, one launch (start us, length us, event | category | flops | bytes accessed | tf_op | source)
XLA Modules:
  0.0 356.2 jit_solution(5089881661219460919)
XLA Ops:
  7.2 1.5 convolution_convert_fusion.3
  8.7 1.1 copy.108
  9.8 10.5 %all-to-all-start.1 = ((bf16[1,4,128,384]{3,1,0,2:T(4,128)(2,1)}), bf16[1,4,128,384]{3,1,0,2:T(4,128)(2,1)S(1)}, u32[]{:S(2)}, u32[]{:S(2)}) async-start(bf16[1,4,128,384]{3,1,0,2:T(4,128)(2,1)} %copy.108), calls=%async_computation.1 | async-start | bytes 786432 | tf_op jit(solution)/shard_map/all_to_all | solution.py:112
  20.4 0.6 fusion.15
  21.0 0.3 multiply_reduce_fusion.2
  21.3 0.6 fusion.16
  21.9 0.2 multiply_convert_fusion.2
  22.1 0.8 convolution_convert_fusion
  22.9 1.9 copy.102
  24.9 7.1 %all-to-all-done.1 = bf16[1,4,128,384]{3,1,0,2:T(4,128)(2,1)S(1)} async-done(((bf16[1,4,128,384]{3,1,0,2:T(4,128)(2,1)}), bf16[1,4,128,384]{3,1,0,2:T(4,128)(2,1)S(1)}, u32[]{:S(2)}, u32[]{:S(2)}) %all-to-all-start.1) | async-done | bytes 393248 | tf_op jit(solution)/shard_map/all_to_all | solution.py:112
  32.0 7.6 %all-to-all-start = ((bf16[3,4,128,384]{3,1,0,2:T(4,128)(2,1)}), bf16[3,4,128,384]{3,1,0,2:T(4,128)(2,1)S(1)}, u32[]{:S(2)}, u32[]{:S(2)}) async-start(bf16[3,4,128,384]{3,1,0,2:T(4,128)(2,1)} %copy.102), calls=%async_computation | async-start | bytes 2359296 | tf_op jit(solution)/shard_map/all_to_all | solution.py:105
  39.6 0.9 copy.109
  40.5 1.7 reshape_squeeze.14
  42.2 1.6 copy.111
  43.8 23.5 %all-to-all-done = bf16[3,4,128,384]{3,1,0,2:T(4,128)(2,1)S(1)} async-done(((bf16[3,4,128,384]{3,1,0,2:T(4,128)(2,1)}), bf16[3,4,128,384]{3,1,0,2:T(4,128)(2,1)S(1)}, u32[]{:S(2)}, u32[]{:S(2)}) %all-to-all-start) | async-done | bytes 1179680 | tf_op jit(solution)/shard_map/all_to_all | solution.py:105
  67.2 0.4 copy.103
  67.7 1.1 fusion.18
  68.8 0.2 copy.105
  69.0 0.5 reshape_squeeze.13
  69.5 0.9 copy.106
  70.4 0.2 copy.104
  70.5 0.5 reshape_squeeze.12
  71.0 0.9 copy.113
  71.9 0.2 copy.110
  72.1 0.5 reshape_squeeze.15
  72.6 1.6 copy.112
  74.2 0.7 fusion.19
  75.0 1.7 convolution_convert_fusion.1
  76.7 2.2 multiply_reduce_fusion
  78.9 1.0 copy.129
  79.9 8.4 %all-to-all-start.3 = ((bf16[1,128,4,384]{3,2,0,1:T(4,128)(2,1)}), bf16[1,128,4,384]{3,2,0,1:T(4,128)(2,1)S(1)}, u32[]{:S(2)}, u32[]{:S(2)}) async-start(bf16[1,128,4,384]{3,2,0,1:T(4,128)(2,1)} %copy.129), calls=%async_computation.3 | async-start | bytes 786432 | tf_op jit(solution)/shard_map/all_to_all | solution.py:123
  88.3 2.2 multiply_convert_fusion
  90.5 0.3 fusion.3
  90.9 0.3 copy.119
  91.1 0.6 fusion.4
  91.8 0.3 copy.120
  92.0 2.2 convolution_convert_fusion.2
  94.2 0.3 copy.121
  94.5 1.9 pad_maximum_fusion
  96.4 2.5 all-to-all-done.3
  98.9 7.9 %all-to-all-start.2 = ((bf16[3,128,4,384]{3,2,0,1:T(4,128)(2,1)}), bf16[3,128,4,384]{3,2,0,1:T(4,128)(2,1)S(1)}, u32[]{:S(2)}, u32[]{:S(2)}) async-start(bf16[3,128,4,384]{3,2,0,1:T(4,128)(2,1)} %pad_maximum_fusion), calls=%async_computation.2 | async-start | bytes 2359296 | tf_op jit(solution)/shard_map/all_to_all | solution.py:122
  107.0 1.2 convolution_bitcast_fusion.2
  108.3 26.1 %all-to-all-done.2 = bf16[3,128,4,384]{3,2,0,1:T(4,128)(2,1)S(1)} async-done(((bf16[3,128,4,384]{3,2,0,1:T(4,128)(2,1)}), bf16[3,128,4,384]{3,2,0,1:T(4,128)(2,1)S(1)}, u32[]{:S(2)}, u32[]{:S(2)}) %all-to-all-start.2) | async-done | bytes 1179680 | tf_op jit(solution)/shard_map/all_to_all | solution.py:122
  134.3 0.5 copy.123
  134.9 0.3 reshape.115
  135.2 1.1 copy-done.1
  136.2 0.8 convolution_bitcast_fusion
  137.1 0.3 copy-done.4
  137.3 0.2 maximum_bitcast_fusion
  137.5 2.5 copy.131
  140.0 0.2 copy.138
  140.2 0.2 copy.140
  140.4 0.8 copy-done.2
  141.2 1.9 fusion.17
  143.1 0.2 multiply_convert_fusion.1
  143.4 0.2 copy.141
  143.7 1.3 collective-permute-start
  145.0 1.3 dynamic-slice
  146.9 158.8 %all-reduce.5.cloned.1.call-done = f32[1,4,384,384]{3,1,0,2:T(4,128)} async-done(((f32[1,4,384,384]{3,1,0,2:T(4,128)}), f32[1,4,384,384]{3,1,0,2:T(4,128)}) %all-reduce.5.cloned.1.call-update) | async-done | bytes 2359312
  305.7 1.5 constant_dynamic-slice_fusion
  307.3 1.3 dynamic-slice.2
  309.2 37.8 %all-reduce.7.cloned.1.call-done = f32[1,4,12,384]{3,1,0,2:T(4,128)} async-done(((f32[1,4,12,384]{3,1,0,2:T(4,128)}), f32[1,4,12,384]{3,1,0,2:T(4,128)}) %all-reduce.7.cloned.1.call-update) | async-done | bytes 73744
  347.1 1.5 dynamic-slice_bitcast_fusion
  348.6 0.7 copy.147
  (33 shorter events, 0.7 us)
Async XLA Ops:
  7.2 13.1 %copy-start = (bf16[1,1,4,128,384]{4,3,2,1,0:T(8,128)(2,1)S(1)}, bf16[1,1,4,128,384]{4,3,2,1,0:T(8,128)(2,1)}, u32[]{:S(2)}) copy-start(bf16[1,1,4,128,384]{4,3,2,1,0:T(8,128)(2,1)} %param.3) | copy-start | bytes 1179652
  8.7 13.4 %copy-start.9 = (bf16[1,4,384,384]{3,2,1,0:T(8,128)(2,1)S(1)}, bf16[1,4,384,384]{3,2,1,0:T(8,128)(2,1)}, u32[]{:S(2)}) copy-start(bf16[1,4,384,384]{3,2,1,0:T(8,128)(2,1)} %param.5) | copy-start | bytes 3538948
  9.8 22.2 %all-to-all-start.1 = ((bf16[1,4,128,384]{3,1,0,2:T(4,128)(2,1)}), bf16[1,4,128,384]{3,1,0,2:T(4,128)(2,1)S(1)}, u32[]{:S(2)}, u32[]{:S(2)}) async-start(bf16[1,4,128,384]{3,1,0,2:T(4,128)(2,1)} %copy.108), calls=%async_computation.1 | async-start | bytes 786432 | tf_op jit(solution)/shard_map/all_to_all | solution.py:112
  32.0 35.3 %all-to-all-start = ((bf16[3,4,128,384]{3,1,0,2:T(4,128)(2,1)}), bf16[3,4,128,384]{3,1,0,2:T(4,128)(2,1)S(1)}, u32[]{:S(2)}, u32[]{:S(2)}) async-start(bf16[3,4,128,384]{3,1,0,2:T(4,128)(2,1)} %copy.102), calls=%async_computation | async-start | bytes 2359296 | tf_op jit(solution)/shard_map/all_to_all | solution.py:105
  69.0 1.4 copy-start.5
  74.9 4.0 %copy-start.6 = (f32[4,6,128,128]{2,3,1,0:T(8,128)}, f32[4,6,128,128]{2,3,1,0:T(8,128)S(1)}, u32[]{:S(2)}) copy-start(f32[4,6,128,128]{2,3,1,0:T(8,128)S(1)} %get-tuple-element.22) | copy-start | bytes 4718596
  74.9 1.7 copy-start.7
  74.9 1.8 copy-start.8
  78.9 9.4 %copy-start.10 = (f32[4,6,128]{2,1,0:T(8,128)S(1)}, f32[4,6,128]{2,1,0:T(8,128)}, u32[]{:S(2)}) copy-start(f32[4,6,128]{2,1,0:T(8,128)} %get-tuple-element.23) | copy-start | bytes 36868
  79.9 19.0 %all-to-all-start.3 = ((bf16[1,128,4,384]{3,2,0,1:T(4,128)(2,1)}), bf16[1,128,4,384]{3,2,0,1:T(4,128)(2,1)S(1)}, u32[]{:S(2)}, u32[]{:S(2)}) async-start(bf16[1,128,4,384]{3,2,0,1:T(4,128)(2,1)} %copy.129), calls=%async_computation.3 | async-start | bytes 786432 | tf_op jit(solution)/shard_map/all_to_all | solution.py:123
  96.4 10.6 %copy-start.3 = (bf16[1,1,4,128,384]{4,3,2,1,0:T(8,128)(2,1)S(1)}, bf16[1,1,4,128,384]{4,3,2,1,0:T(8,128)(2,1)}, u32[]{:S(2)}) copy-start(bf16[1,1,4,128,384]{4,3,2,1,0:T(8,128)(2,1)} %param.4) | copy-start | bytes 1179652
  98.9 35.5 %all-to-all-start.2 = ((bf16[3,128,4,384]{3,2,0,1:T(4,128)(2,1)}), bf16[3,128,4,384]{3,2,0,1:T(4,128)(2,1)S(1)}, u32[]{:S(2)}, u32[]{:S(2)}) async-start(bf16[3,128,4,384]{3,2,0,1:T(4,128)(2,1)} %pad_maximum_fusion), calls=%async_computation.2 | async-start | bytes 2359296 | tf_op jit(solution)/shard_map/all_to_all | solution.py:122
  106.7 199.0 %all-reduce.5.cloned.1.call-start = ((), (), s32[]{:S(2)}) async-start(), calls=%async_computation.4 | async-start | bytes 4718592
  135.2 1.1 copy-start.1
  136.2 1.1 copy-start.4
  139.9 1.3 copy-start.2
  139.9 1.3 copy-start.11
  140.0 1.3 copy-start.12
  140.0 207.1 %all-reduce.7.cloned.1.call-start = ((), (), s32[]{:S(2)}) async-start(), calls=%async_computation.5 | async-start | bytes 147456
  143.7 165.5 %collective-permute-start = (bf16[1,1,4,128,384]{4,3,2,1,0:T(8,128)(2,1)S(1)}, bf16[1,1,4,128,384]{4,3,2,1,0:T(8,128)(2,1)S(1)}, u32[]{:S(2)}, u32[]{:S(2)}) collective-permute-start(bf16[1,1,4,128,384]{4,3,2,1,0:T(8,128)(2,1)S(1)} %bitcast.96), channel_id=1, source_target_pairs={{32,0},{64,32},{96,64},{128,96},{160,128},{192,160},{224,192},{33,... | collective-permute-start | bytes 1179656 | tf_op jit(solution)/shard_map/ppermute | solution.py:15
Sparse Core Ops, SparseCore 0:
  140.1 165.6 all-reduce.4
  309.1 37.8 all-reduce.6
where the time goes:
time: 357 us; the launch traced here: 356 us
  waiting for transfers between devices  256 us (72%)
  starting transfers between devices  35.7 us (10%)
  local copies, waits for them, and re-layouts  28.5 us (8%)
  between operations  15.7 us (4%)
  matrix products  14 us (4%)
  other arithmetic  6.4 us (2%)
    unnamed x4, waiting for transfers between devices  197 us
    all_to_all x1, waiting for transfers between devices, per_device(): lax.all_to_all(stacked_grads, 'mp', split_axis=1, concat_axis=2, tiled=True)  26.1 us
    all_to_all x1, waiting for transfers between devices, per_device(): lax.all_to_all(projected.reshape(3, row_count, res_total, head_width), 'm...  23.5 us
    all_to_all x1, starting transfers between devices, per_device(): lax.all_to_all(attn_grad.reshape(1, row_count, res_total, head_width), 'm...  10.5 us
    unnamed x31, local copies, waits for them, and re-layouts  8.55 us
    all_to_all x1, starting transfers between devices, per_device(): lax.all_to_all(attn_out[None], 'mp', split_axis=1, concat_axis=2, tiled=T...  8.39 us
    all_to_all x1, starting transfers between devices, per_device(): lax.all_to_all(stacked_grads, 'mp', split_axis=1, concat_axis=2, tiled=True)  7.87 us
    all_to_all x1, starting transfers between devices, per_device(): lax.all_to_all(projected.reshape(3, row_count, res_total, head_width), 'm...  7.59 us
  transfers between devices with their start and end apart: 7, of which 6 were waited for; matrix products, arithmetic and copies ran while one was open for 7% of the time, Pallas kernels for 0%

commit v1 on v0

v1 whole, which is shorter than its diff:
```python
import functools

import jax
import jax.numpy as jnp
from jax import lax
from jax.experimental import pallas as pl
from jax.experimental.pallas import tpu as pltpu
from jax.sharding import PartitionSpec as P

HEAD_DIM = 64
EPS = 1e-05
F32 = jnp.float32
BF16 = jnp.bfloat16
LANES = 128
ROWS = 4
COLS = 4
CELL = ROWS * COLS
GROUP = 16
BLOCK = GROUP * CELL
VMEM = pl.BlockSpec(memory_space=pltpu.VMEM)
SMEM = pl.BlockSpec(memory_space=pltpu.SMEM)


def dot(a, b, dims=((1,), (0,))):
    return lax.dot_general(a, b, (dims, ((), ())), preferred_element_type=F32)


def selection(size, source_of):
    out = lax.broadcasted_iota(jnp.int32, (size, size), 0)
    source = lax.broadcasted_iota(jnp.int32, (size, size), 1)
    return jnp.where(source_of(out) == source, 1.0, 0.0).astype(BF16)


def reorder(matrix, rows):
    return dot(matrix, rows).astype(BF16)


def pack_kernel(act_ref, grad_ref, out_ref):
    order = selection(BLOCK, lambda o: ((o >> 2) & 3) * 64 + (o >> 4) * 4 + (o & 3))
    groups = out_ref.shape[0] // GROUP
    residues = act_ref.shape[0] // ROWS
    span = GROUP * COLS
    for slot, ref in enumerate((act_ref, grad_ref)):
        for g in range(groups):
            rows = jnp.concatenate(
                [ref[i * residues + g * span : i * residues + (g + 1) * span] for i in range(ROWS)]
            )
            moved = reorder(order, rows).reshape(GROUP, CELL, -1)
            out_ref[g * GROUP : (g + 1) * GROUP, slot * CELL : (slot + 1) * CELL] = moved


def main_kernel(
    in_ref,
    weight_ref,
    back_ref,
    normed_ref,
    grads_ref,
    attn_ref,
    delta_ref,
    standard_ref,
    inverse_ref,
    proj_ref,
):
    peers = in_ref.shape[0]
    groups = peers // GROUP
    width = in_ref.shape[2]
    seqs = peers * ROWS
    tokens = seqs * COLS
    span = GROUP * ROWS
    order = selection(BLOCK, lambda o: ((o >> 2) & 15) * 16 + (o & 3) * 4 + (o >> 6))
    for g in range(groups):
        peers_of = slice(g * GROUP, (g + 1) * GROUP)
        acts = dot(order, in_ref[peers_of, :CELL].reshape(BLOCK, width))
        outs = reorder(order, in_ref[peers_of, CELL : 2 * CELL].reshape(BLOCK, width))
        for j in range(COLS):
            to = slice(j * seqs + g * span, j * seqs + (g + 1) * span)
            standard_ref[to] = acts[j * span : (j + 1) * span]
            delta_ref[to] = outs[j * span : (j + 1) * span]
    values = standard_ref[...]
    mean_value = jnp.mean(values, axis=-1, keepdims=True)
    centred = values - mean_value
    inverse = lax.rsqrt(jnp.mean(centred * centred, axis=-1, keepdims=True) + EPS)
    standard = centred * inverse
    standard_ref[...] = standard
    inverse_ref[...] = jnp.broadcast_to(inverse, inverse_ref.shape)
    normed = standard.astype(BF16)
    normed_ref[...] = normed
    for n in range(3):
        proj_ref[n] = dot(normed, weight_ref[n]).astype(BF16)
    proj_ref[3] = dot(delta_ref[...], weight_ref[3]).astype(BF16)

    scaling = HEAD_DIM ** (-0.5)
    low = lax.broadcasted_iota(jnp.int32, (seqs, LANES), 1) < HEAD_DIM

    def apart(pair):
        zero = jnp.zeros_like(pair)
        return jnp.concatenate([jnp.where(low, pair, zero), jnp.where(low, zero, pair)])

    def joined(rows):
        return jnp.where(low, rows[:seqs], rows[seqs:])

    def halves(rows, function):
        return jnp.concatenate([function(rows[:, :seqs]), function(rows[:, seqs:])], axis=1)

    def column(j, carry):
        here = pl.ds(pl.multiple_of(j * seqs, seqs), seqs)
        for pair in range(width // LANES):
            lanes = slice(pair * LANES, (pair + 1) * LANES)
            query, key, value, delta = (proj_ref[n, here, lanes] for n in range(4))
            keys, vals = apart(key), apart(value)
            scores = dot(query, keys, ((1,), (1,))) * scaling
            dprobs = dot(delta, vals, ((1,), (1,)))
            probs, soft, dscores = [], [], []
            for h in range(2):
                part = scores[:, h * seqs : (h + 1) * seqs]
                exponent = jnp.exp(part - jnp.max(part, axis=-1, keepdims=True))
                prob = exponent / jnp.sum(exponent, axis=-1, keepdims=True)
                dprob = dprobs[:, h * seqs : (h + 1) * seqs]
                row_delta = jnp.sum(prob * dprob, axis=-1, keepdims=True)
                soft.append(prob.astype(BF16))
                dscores.append((prob * (dprob - row_delta)).astype(BF16))
            soft = jnp.concatenate(soft, axis=1)
            dscores = jnp.concatenate(dscores, axis=1)
            attn_ref[here, lanes] = dot(soft, vals).astype(BF16)
            grads_ref[0, here, lanes] = (dot(dscores, keys) * scaling).astype(BF16)
            key_grad = joined(dot(dscores, query, ((0,), (0,))))
            grads_ref[1, here, lanes] = (key_grad * scaling).astype(BF16)
            grads_ref[2, here, lanes] = joined(dot(soft, delta, ((0,), (0,)))).astype(BF16)
        return carry

    lax.fori_loop(0, COLS, column, 0)

    grad_in = dot(grads_ref[0], weight_ref[0], ((1,), (1,)))
    grad_in += dot(grads_ref[1], weight_ref[1], ((1,), (1,)))
    grad_in += dot(grads_ref[2], weight_ref[2], ((1,), (1,)))
    standard = standard_ref[...]
    grad_mean = jnp.mean(grad_in, axis=-1, keepdims=True)
    grad_proj = jnp.mean(grad_in * standard, axis=-1, keepdims=True)
    branch = inverse_ref[:, :1] * (grad_in - grad_mean - standard * grad_proj)
    branch = branch.astype(BF16).astype(F32)
    input_grad = (delta_ref[...].astype(F32) + branch).astype(BF16)
    order = selection(BLOCK, lambda o: (o & 3) * 64 + (o >> 4) * 4 + ((o >> 2) & 3))
    for g in range(groups):
        rows = jnp.concatenate(
            [input_grad[j * seqs + g * span : j * seqs + (g + 1) * span] for j in range(COLS)]
        )
        back_ref[g * GROUP : (g + 1) * GROUP] = reorder(order, rows).reshape(GROUP, CELL, width)


def weight_kernel(replica_ref, normed_ref, grads_ref, attn_ref, delta_ref, keep_ref, give_ref):
    replica = replica_ref[0]
    for n in range(4):
        if n < 3:
            term = dot(normed_ref[...], grads_ref[n], ((0,), (0,)))
        else:
            term = dot(delta_ref[...], attn_ref[...], ((0,), (0,)))

        @pl.when(replica == n // 2)
        def _():
            keep_ref[n % 2] = term

        @pl.when(replica != n // 2)
        def _():
            give_ref[n % 2] = term.astype(BF16)


def combine_kernel(keep_ref, got_ref, back_ref, out_ref):
    peers, cells, width = back_ref.shape
    part = width // peers
    out_ref[:, :cells] = back_ref[...]
    size = 8 * part

    def source_of(o):
        device = o // (2 * part)
        inside = o - device * (2 * part)
        matrix = inside // part
        return matrix * size + device * part + inside - matrix * part

    order = selection(2 * size, source_of)
    for g in range(peers // 8):
        here = slice(g * size, (g + 1) * size)
        rows = [(keep_ref[m, here] + got_ref[m, here].astype(F32)).astype(BF16) for m in range(2)]
        moved = reorder(order, jnp.concatenate(rows)).reshape(8, 2 * part, width)
        out_ref[g * 8 : (g + 1) * 8, cells:] = moved


def final_kernel(in_ref, received_ref, grads_ref):
    peers, _, width = in_ref.shape
    groups = peers // GROUP
    residues = peers * COLS
    span = GROUP * COLS
    order = selection(BLOCK, lambda o: ((o >> 2) & 15) * 16 + (o >> 6) * 4 + (o & 3))
    for g in range(groups):
        rows = in_ref[g * GROUP : (g + 1) * GROUP, :CELL].reshape(BLOCK, width)
        moved = reorder(order, rows)
        for i in range(ROWS):
            to = slice(i * residues + g * span, i * residues + (g + 1) * span)
            received_ref[to] = moved[i * span : (i + 1) * span]
    grads_ref[...] = jnp.sum(in_ref[:, CELL:].astype(F32), axis=0)


def shape(dims, dtype=BF16):
    return jax.ShapeDtypeStruct(dims, dtype)


def call(kernel, in_specs, out_shape, scratch=()):
    return pl.pallas_call(
        kernel,
        in_specs=in_specs,
        out_specs=jax.tree.map(lambda _: VMEM, out_shape),
        out_shape=out_shape,
        scratch_shapes=scratch,
        compiler_params=pltpu.CompilerParams(vmem_limit_bytes=56 * 1024 * 1024),
    )


def exchange(array):
    return lax.all_to_all(array, "mp", split_axis=0, concat_axis=0, tiled=True)


def per_device(activations, out_grads, layer_weights):
    rows, residues, width = activations.shape[2:]
    peers = lax.axis_size("mp")
    tokens = rows * residues
    part = width // peers
    packed = call(pack_kernel, [VMEM] * 2, shape((peers, 2 * CELL, width)))(
        activations.reshape(tokens, width), out_grads.reshape(tokens, width)
    )
    arrived = exchange(packed)
    back, normed, grads, attn, delta = call(
        main_kernel,
        [VMEM] * 2,
        (
            shape((peers, CELL, width)),
            shape((tokens, width)),
            shape((3, tokens, width)),
            shape((tokens, width)),
            shape((tokens, width)),
        ),
        [
            pltpu.VMEM((tokens, width), F32),
            pltpu.VMEM((tokens, LANES), F32),
            pltpu.VMEM((4, tokens, width), BF16),
        ],
    )(arrived, layer_weights[0])
    sections = lax.axis_size("section")
    back = lax.ppermute(back, "section", [(i + 1, i) for i in range(sections - 1)])
    replica = lax.axis_index("dp").astype(jnp.int32).reshape(1)
    keep, give = call(
        weight_kernel,
        [SMEM] + [VMEM] * 4,
        (shape((2, width, width), F32), shape((2, width, width))),
    )(replica, normed, grads, attn, delta)
    got = lax.ppermute(give, "dp", [(0, 1), (1, 0)])
    leaving = call(combine_kernel, [VMEM] * 3, shape((peers, CELL + 2 * part, width)))(
        keep, got, back
    )
    landed = exchange(leaving)
    received, weight_grads = call(
        final_kernel, [VMEM], (shape((tokens, width)), shape((2 * part, width), F32))
    )(landed)
    return (received.reshape(activations.shape), weight_grads.reshape(1, 2, part, width))


def solution(mesh):
    in_specs = (
        P("dp", "section", "mp", None, None),
        P("dp", "section", "mp", None, None),
        P("section", None, None, None),
    )
    out_specs = (P("dp", "section", "mp", None, None), P("section", "dp", "mp", None))
    return jax.shard_map(
        per_device, mesh=mesh, in_specs=in_specs, out_specs=out_specs, check_vma=False
    )
```

time: 357 us -> 111 us (0.31)
  the two profiles are of different devices: /device:TPU:1 before, /device:TPU:200 now
where the time goes in v1:
time: 111 us
  waiting for transfers between devices  36.5 us (33%)
  blocking collectives  32.3 us (29%)
  Pallas kernels  24.2 us (22%)
  starting transfers between devices  14 us (13%)
  local copies, waits for them, and re-layouts  3.25 us (3%)
    all_to_all x1, blocking collectives, exchange(): return lax.all_to_all(array, 'mp', split_axis=0, concat_axis=0, tiled=True)  32.3 us
    all_to_all x1, waiting for transfers between devices, exchange(): return lax.all_to_all(array, 'mp', split_axis=0, concat_axis=0, tiled=True)  23.2 us
    ppermute x1, waiting for transfers between devices, per_device(): lax.ppermute(back, 'section', [(i + 1, i) for i in range(sections - 1)])  13.4 us
    pallas_call x1, Pallas kernels, per_device(): call(main_kernel, [VMEM] * 2, (shape((peers, CELL, width)), shape((tokens...  11.9 us
    all_to_all x1, starting transfers between devices, exchange(): return lax.all_to_all(array, 'mp', split_axis=0, concat_axis=0, tiled=True)  10.2 us
    pallas_call x1, Pallas kernels, per_device(): call(weight_kernel, [SMEM] + [VMEM] * 4, (shape((2, width, width), F32),...  4.58 us
    pallas_call x1, Pallas kernels, per_device(): call(combine_kernel, [VMEM] * 3, shape((peers, CELL + 2 * part, width)))  3.01 us
    unnamed x9, local copies, waits for them, and re-layouts  2.47 us
  transfers between devices with their start and end apart: 3, of which 2 were waited for; matrix products, arithmetic and copies ran while one was open for 0% of the time, Pallas kernels for 0%

profile of v1, /device:TPU:200, one launch (start us, length us, event | category | flops | bytes accessed | tf_op | source)
XLA Modules:
  0.0 110.9 jit_solution(672862951496466188)
XLA Ops:
  0.6 2.4 %shard_map.50 = bf16[32,32,384]{2,1,0:T(8,128)(2,1)} custom-call(bf16[512,384]{1,0:T(8,128)(2,1)} %bitcast.6, bf16[512,384]{1,0:T(8,128)(2,1)} %bitcast.7), custom_call_target="tpu_custom_call" | custom-call | tf_op jit(solution)/shard_map/pallas_call | solution.py:226
  3.1 10.2 %all-to-all-start = ((bf16[32,32,384]{2,1,0:T(8,128)(2,1)}), bf16[32,32,384]{2,1,0:T(8,128)(2,1)S(1)}, u32[]{:S(2)}, u32[]{:S(2)}) async-start(bf16[32,32,384]{2,1,0:T(8,128)(2,1)} %shard_map.50), calls=%async_computation | async-start | bytes 1572864 | tf_op jit(solution)/shard_map/all_to_all | solution.py:218
  13.2 23.2 %all-to-all-done.in_ref = bf16[32,32,384]{2,1,0:T(8,128)(2,1)S(1)} async-done(((bf16[32,32,384]{2,1,0:T(8,128)(2,1)}), bf16[32,32,384]{2,1,0:T(8,128)(2,1)S(1)}, u32[]{:S(2)}, u32[]{:S(2)}) %all-to-all-start) | async-done | bytes 786464 | tf_op jit(solution)/shard_map/all_to_all | solution.py:218
  36.4 0.0 copy-start
  36.4 0.9 copy-done
  37.3 11.9 %shard_map.51 = (bf16[32,16,384]{2,1,0:T(8,128)(2,1)}, bf16[512,384]{1,0:T(8,128)(2,1)}, bf16[3,512,384]{2,1,0:T(8,128)(2,1)}, bf16[512,384]{1,0:T(8,128)(2,1)}, bf16[512,384]{1,0:T(8,128)(2,1)}) custom-call(bf16[32,32,384]{2,1,0:T(8,128)(2,1)} %copy-done, bf16[4,384,384]{2,1,0:T(8,128)(2,1)} %bitcast.5), custom_call_target="tpu_custom_call" | custom-call | tf_op jit(solution)/shard_map/pallas_call | solution.py:230
  49.2 0.0 copy-start.3
  49.2 4.6 %shard_map.52 = (f32[2,384,384]{2,1,0:T(8,128)}, bf16[2,384,384]{2,1,0:T(8,128)(2,1)}) custom-call(s32[1]{0:T(128)} %bitcast.replica_ref, bf16[512,384]{1,0:T(8,128)(2,1)} %get-tuple-element.11.normed_ref, bf16[3,512,384]{2,1,0:T(8,128)(2,1)} %get-tuple-element.12.grads_ref, bf16[512,384]{1,0:T(8,128)(2,1)} %get-tuple-element.13.attn_ref, ...), custom_call_target="tpu_custom_call" | custom-call | tf_op jit(solution)/shard_map/pallas_call | solution.py:249
  53.7 1.9 %collective-permute-start = (bf16[2,384,384]{2,1,0:T(8,128)(2,1)}, bf16[2,384,384]{2,1,0:T(8,128)(2,1)S(1)}, u32[]{:S(2)}, u32[]{:S(2)}) collective-permute-start(bf16[2,384,384]{2,1,0:T(8,128)(2,1)} %get-tuple-element.16), channel_id=1, source_target_pairs={{0,256},{256,0},{1,257},{257,1},{2,258},{258,2},{3,259},{259,3},{4... | collective-permute-start | bytes 1769480 | tf_op jit(solution)/shard_map/ppermute | solution.py:254
  55.7 0.0 copy-done.3
  55.7 1.9 %collective-permute-start.1 = (bf16[32,16,384]{2,1,0:T(8,128)(2,1)S(1)}, bf16[32,16,384]{2,1,0:T(8,128)(2,1)S(1)}, u32[]{:S(2)}, u32[]{:S(2)}) collective-permute-start(bf16[32,16,384]{2,1,0:T(8,128)(2,1)S(1)} %copy-done.3), channel_id=1, source_target_pairs={{32,0},{64,32},{96,64},{128,96},{160,128},{192,160},{224,192},{33,... | collective-permute-start | bytes 1179656 | tf_op jit(solution)/shard_map/ppermute | solution.py:247
  57.6 13.4 %collective-permute-done.1.back_ref = bf16[32,16,384]{2,1,0:T(8,128)(2,1)S(1)} collective-permute-done((bf16[32,16,384]{2,1,0:T(8,128)(2,1)S(1)}, bf16[32,16,384]{2,1,0:T(8,128)(2,1)S(1)}, u32[]{:S(2)}, u32[]{:S(2)}) %collective-permute-start.1) | collective-permute-done | bytes 393248 | tf_op jit(solution)/shard_map/ppermute | solution.py:247
  71.0 0.0 copy-start.2
  71.0 0.0 collective-permute-done.got_ref
  71.0 0.0 copy-start.1
  71.0 0.7 copy-done.2
  71.7 0.2 copy-done.1
  71.9 3.0 %shard_map.53 = bf16[32,40,384]{2,1,0:T(8,128)(2,1)} custom-call(f32[2,384,384]{2,1,0:T(8,128)} %get-tuple-element.15.keep_ref, bf16[2,384,384]{2,1,0:T(8,128)(2,1)} %copy-done.1, bf16[32,16,384]{2,1,0:T(8,128)(2,1)} %copy-done.2), custom_call_target="tpu_custom_call" | custom-call | tf_op jit(solution)/shard_map/pallas_call | solution.py:255
  74.9 32.3 %all_to_all.10.in_ref = bf16[32,40,384]{2,1,0:T(8,128)(2,1)} all-to-all(bf16[32,40,384]{2,1,0:T(8,128)(2,1)} %shard_map.53), channel_id=1, replica_groups=mesh['dp'=2,'section'=8,'mp'=32] {'mp'}, dimensions={0} | all-to-all | bytes 1966080 | tf_op jit(solution)/shard_map/all_to_all | solution.py:218
  107.3 2.3 %shard_map.54 = (bf16[512,384]{1,0:T(8,128)(2,1)}, f32[24,384]{1,0:T(8,128)}) custom-call(bf16[32,40,384]{2,1,0:T(8,128)(2,1)} %all_to_all.10.in_ref), custom_call_target="tpu_custom_call" | custom-call | tf_op jit(solution)/shard_map/pallas_call | solution.py:259
  109.5 0.8 reshape.23
  110.3 0.6 copy.6
Async XLA Ops:
  3.1 33.3 %all-to-all-start = ((bf16[32,32,384]{2,1,0:T(8,128)(2,1)}), bf16[32,32,384]{2,1,0:T(8,128)(2,1)S(1)}, u32[]{:S(2)}, u32[]{:S(2)}) async-start(bf16[32,32,384]{2,1,0:T(8,128)(2,1)} %shard_map.50), calls=%async_computation | async-start | bytes 1572864 | tf_op jit(solution)/shard_map/all_to_all | solution.py:218
  36.4 0.9 copy-start
  49.2 6.5 %copy-start.3 = (bf16[32,16,384]{2,1,0:T(8,128)(2,1)S(1)}, bf16[32,16,384]{2,1,0:T(8,128)(2,1)}, u32[]{:S(2)}) copy-start(bf16[32,16,384]{2,1,0:T(8,128)(2,1)} %get-tuple-element.17) | copy-start | bytes 1179652
  53.7 17.2 %collective-permute-start = (bf16[2,384,384]{2,1,0:T(8,128)(2,1)}, bf16[2,384,384]{2,1,0:T(8,128)(2,1)S(1)}, u32[]{:S(2)}, u32[]{:S(2)}) collective-permute-start(bf16[2,384,384]{2,1,0:T(8,128)(2,1)} %get-tuple-element.16), channel_id=1, source_target_pairs={{0,256},{256,0},{1,257},{257,1},{2,258},{258,2},{3,259},{259,3},{4... | collective-permute-start | bytes 1769480 | tf_op jit(solution)/shard_map/ppermute | solution.py:254
  55.7 15.3 %collective-permute-start.1 = (bf16[32,16,384]{2,1,0:T(8,128)(2,1)S(1)}, bf16[32,16,384]{2,1,0:T(8,128)(2,1)S(1)}, u32[]{:S(2)}, u32[]{:S(2)}) collective-permute-start(bf16[32,16,384]{2,1,0:T(8,128)(2,1)S(1)} %copy-done.3), channel_id=1, source_target_pairs={{32,0},{64,32},{96,64},{128,96},{160,128},{192,160},{224,192},{33,... | collective-permute-start | bytes 1179656 | tf_op jit(solution)/shard_map/ppermute | solution.py:247
  71.0 0.7 copy-start.2
  71.0 1.0 copy-start.1

commit v2 on v1

--- a/solution.py
+++ b/solution.py
@@ -1,11 +1,10 @@
-import functools
-
 import jax
 import jax.numpy as jnp
 from jax import lax
 from jax.experimental import pallas as pl
 from jax.experimental.pallas import tpu as pltpu
 from jax.sharding import PartitionSpec as P
+
 
 HEAD_DIM = 64
 EPS = 1e-05
@@ -17,6 +16,8 @@
 CELL = ROWS * COLS
 GROUP = 16
 BLOCK = GROUP * CELL
+NX = 4
+PAD = 8
 VMEM = pl.BlockSpec(memory_space=pltpu.VMEM)
 SMEM = pl.BlockSpec(memory_space=pltpu.SMEM)
 
@@ -49,23 +50,24 @@
             out_ref[g * GROUP : (g + 1) * GROUP, slot * CELL : (slot + 1) * CELL] = moved
 
 
-def main_kernel(
+def attend_kernel(
+    replica_ref,
     in_ref,
     weight_ref,
-    back_ref,
-    normed_ref,
     grads_ref,
-    attn_ref,
     delta_ref,
     standard_ref,
     inverse_ref,
+    keep_ref,
+    give_ref,
+    normed_ref,
+    attn_ref,
     proj_ref,
 ):
     peers = in_ref.shape[0]
     groups = peers // GROUP
     width = in_ref.shape[2]
     seqs = peers * ROWS
-    tokens = seqs * COLS
     span = GROUP * ROWS
     order = selection(BLOCK, lambda o: ((o >> 2) & 15) * 16 + (o & 3) * 4 + (o >> 6))
     for g in range(groups):
@@ -99,9 +101,6 @@
     def joined(rows):
         return jnp.where(low, rows[:seqs], rows[seqs:])
 
-    def halves(rows, function):
-        return jnp.concatenate([function(rows[:, :seqs]), function(rows[:, seqs:])], axis=1)
-
     def column(j, carry):
         here = pl.ds(pl.multiple_of(j * seqs, seqs), seqs)
         for pair in range(width // LANES):
@@ -110,7 +109,7 @@
             keys, vals = apart(key), apart(value)
             scores = dot(query, keys, ((1,), (1,))) * scaling
             dprobs = dot(delta, vals, ((1,), (1,)))
-            probs, soft, dscores = [], [], []
+            soft, dscores = [], []
             for h in range(2):
                 part = scores[:, h * seqs : (h + 1) * seqs]
                 exponent = jnp.exp(part - jnp.max(part, axis=-1, keepdims=True))
@@ -130,6 +129,27 @@
 
     lax.fori_loop(0, COLS, column, 0)
 
+    replica = replica_ref[0]
+    for n in range(4):
+        if n < 3:
+            term = dot(normed_ref[...], grads_ref[n], ((0,), (0,)))
+        else:
+            term = dot(delta_ref[...], attn_ref[...], ((0,), (0,)))
+
+        @pl.when(replica == n // 2)
+        def _():
+            keep_ref[n % 2] = term
+
+        @pl.when(replica != n // 2)
+        def _():
+            give_ref[n % 2] = term.astype(BF16)
+
+
+def input_kernel(grads_ref, delta_ref, standard_ref, inverse_ref, weight_ref, back_ref):
+    groups = back_ref.shape[0] // GROUP
+    tokens, width = delta_ref.shape
+    seqs = tokens // COLS
+    span = GROUP * ROWS
     grad_in = dot(grads_ref[0], weight_ref[0], ((1,), (1,)))
     grad_in += dot(grads_ref[1], weight_ref[1], ((1,), (1,)))
     grad_in += dot(grads_ref[2], weight_ref[2], ((1,), (1,)))
@@ -147,41 +167,41 @@
         back_ref[g * GROUP : (g + 1) * GROUP] = reorder(order, rows).reshape(GROUP, CELL, width)
 
 
-def weight_kernel(replica_ref, normed_ref, grads_ref, attn_ref, delta_ref, keep_ref, give_ref):
-    replica = replica_ref[0]
-    for n in range(4):
-        if n < 3:
-            term = dot(normed_ref[...], grads_ref[n], ((0,), (0,)))
-        else:
-            term = dot(delta_ref[...], attn_ref[...], ((0,), (0,)))
-
-        @pl.when(replica == n // 2)
-        def _():
-            keep_ref[n % 2] = term
-
-        @pl.when(replica != n // 2)
-        def _():
-            give_ref[n % 2] = term.astype(BF16)
-
-
-def combine_kernel(keep_ref, got_ref, back_ref, out_ref):
-    peers, cells, width = back_ref.shape
+def spread_kernel(keep_ref, got_ref, out_ref):
+    quarters, held, width = out_ref.shape
+    peers = held // (2 * (width // 128))
     part = width // peers
-    out_ref[:, :cells] = back_ref[...]
-    size = 8 * part
+    piece = part // quarters
+    block = 8 * part
+    cell = 2 * piece
 
     def source_of(o):
-        device = o // (2 * part)
-        inside = o - device * (2 * part)
-        matrix = inside // part
-        return matrix * size + device * part + inside - matrix * part
-
-    order = selection(2 * size, source_of)
+        quarter = o // (8 * cell)
+        rest = o - quarter * (8 * cell)
+        device = rest // cell
+        inside = rest - device * cell
+        return (inside & 1) * block + device * part + quarter * piece + (inside >> 1)
+
+    order = selection(2 * block, source_of)
     for g in range(peers // 8):
-        here = slice(g * size, (g + 1) * size)
+        here = slice(g * block, (g + 1) * block)
         rows = [(keep_ref[m, here] + got_ref[m, here].astype(F32)).astype(BF16) for m in range(2)]
-        moved = reorder(order, jnp.concatenate(rows)).reshape(8, 2 * part, width)
-        out_ref[g * 8 : (g + 1) * 8, cells:] = moved
+        moved = reorder(order, jnp.concatenate(rows))
+        for q in range(quarters):
+            to = slice(g * 8 * cell, (g + 1) * 8 * cell)
+            out_ref[q, to] = moved[q * 8 * cell : (q + 1) * 8 * cell]
+
+
+def leave_kernel(parts_ref, back_ref, out_ref):
+    peers, _, width = back_ref.shape
+    out_ref[:, :CELL] = back_ref[...]
+    total = jnp.sum(parts_ref[...].astype(F32), axis=0).astype(BF16)
+    cell = total.shape[0] // peers
+    out = lax.broadcasted_iota(jnp.int32, (peers * PAD, peers * cell), 0)
+    source = lax.broadcasted_iota(jnp.int32, (peers * PAD, peers * cell), 1)
+    fits = jnp.logical_and((out >> 3) * cell + (out & 7) == source, (out & 7) < cell)
+    order = jnp.where(fits, 1.0, 0.0).astype(BF16)
+    out_ref[:, CELL:] = reorder(order, total).reshape(peers, PAD, width)
 
 
 def final_kernel(in_ref, received_ref, grads_ref):
@@ -196,26 +216,37 @@
         for i in range(ROWS):
             to = slice(i * residues + g * span, i * residues + (g + 1) * span)
             received_ref[to] = moved[i * span : (i + 1) * span]
-    grads_ref[...] = jnp.sum(in_ref[:, CELL:].astype(F32), axis=0)
+    parts = in_ref[:, CELL:].astype(F32)
+    quarters = NX
+    parts = jnp.sum(parts.reshape(quarters, peers // quarters, PAD, width), axis=1)
+    piece = grads_ref.shape[0] // quarters
+    for q in range(quarters):
+        for u in range(piece):
+            grads_ref[q * piece + u] = parts[q, 2 * u : 2 * u + 2]
 
 
 def shape(dims, dtype=BF16):
     return jax.ShapeDtypeStruct(dims, dtype)
 
 
-def call(kernel, in_specs, out_shape, scratch=()):
+def call(kernel, in_specs, out_shape, scratch=(), cost=(1e8, 1e6)):
     return pl.pallas_call(
         kernel,
         in_specs=in_specs,
         out_specs=jax.tree.map(lambda _: VMEM, out_shape),
         out_shape=out_shape,
         scratch_shapes=scratch,
-        compiler_params=pltpu.CompilerParams(vmem_limit_bytes=56 * 1024 * 1024),
-    )
-
-
-def exchange(array):
-    return lax.all_to_all(array, "mp", split_axis=0, concat_axis=0, tiled=True)
+        compiler_params=pltpu.CompilerParams(vmem_limit_bytes=14 * 1024 * 1024),
+        cost_estimate=pl.CostEstimate(
+            flops=int(cost[0]), bytes_accessed=int(cost[1]), transcendentals=0
+        ),
+    )
+
+
+def exchange(array, groups=None):
+    return lax.all_to_all(
+        array, "mp", split_axis=0, concat_axis=0, axis_index_groups=groups, tiled=True
+    )
 
 
 def per_device(activations, out_grads, layer_weights):
@@ -227,39 +258,45 @@
         activations.reshape(tokens, width), out_grads.reshape(tokens, width)
     )
     arrived = exchange(packed)
-    back, normed, grads, attn, delta = call(
-        main_kernel,
-        [VMEM] * 2,
+    weights = layer_weights[0]
+    replica = lax.axis_index("dp").astype(jnp.int32).reshape(1)
+    grads, delta, standard, inverse, keep, give = call(
+        attend_kernel,
+        [SMEM] + [VMEM] * 2,
         (
-            shape((peers, CELL, width)),
-            shape((tokens, width)),
             shape((3, tokens, width)),
             shape((tokens, width)),
-            shape((tokens, width)),
+            shape((tokens, width), F32),
+            shape((tokens, LANES), F32),
+            shape((2, width, width), F32),
+            shape((2, width, width)),
         ),
         [
-            pltpu.VMEM((tokens, width), F32),
-            pltpu.VMEM((tokens, LANES), F32),
+            pltpu.VMEM((tokens, width), BF16),
+            pltpu.VMEM((tokens, width), BF16),
             pltpu.VMEM((4, tokens, width), BF16),
         ],
-    )(arrived, layer_weights[0])
+        cost=(3e9, 9e6),
+    )(replica, arrived, weights)
+    got = lax.ppermute(give, "dp", [(0, 1), (1, 0)])
+    back = call(input_kernel, [VMEM] * 5, shape((peers, CELL, width)), cost=(1e9, 3e6))(
+        grads, delta, standard, inverse, weights
+    )
+    keep, back = lax.optimization_barrier((keep, back))
     sections = lax.axis_size("section")
     back = lax.ppermute(back, "section", [(i + 1, i) for i in range(sections - 1)])
-    replica = lax.axis_index("dp").astype(jnp.int32).reshape(1)
-    keep, give = call(
-        weight_kernel,
-        [SMEM] + [VMEM] * 4,
-        (shape((2, width, width), F32), shape((2, width, width))),
-    )(replica, normed, grads, attn, delta)
-    got = lax.ppermute(give, "dp", [(0, 1), (1, 0)])
-    leaving = call(combine_kernel, [VMEM] * 3, shape((peers, CELL + 2 * part, width)))(
-        keep, got, back
-    )
+    spread = call(
+        spread_kernel, [VMEM] * 2, shape((NX, 2 * width // NX, width)), cost=(1e9, 3e6)
+    )(keep, got)
+    ny = peers // NX
+    groups = [[x * ny + y for x in range(NX)] for y in range(ny)]
+    parts = exchange(spread, groups)
+    leaving = call(leave_kernel, [VMEM] * 2, shape((peers, CELL + PAD, width)))(parts, back)
     landed = exchange(leaving)
     received, weight_grads = call(
-        final_kernel, [VMEM], (shape((tokens, width)), shape((2 * part, width), F32))
+        final_kernel, [VMEM], (shape((tokens, width)), shape((part, 2, width), F32))
     )(landed)
-    return (received.reshape(activations.shape), weight_grads.reshape(1, 2, part, width))
+    return (received.reshape(activations.shape), weight_grads.transpose(1, 0, 2)[None])
 
 
 def solution(mesh):
@@ -269,6 +306,7 @@
         P("section", None, None, None),
     )
     out_specs = (P("dp", "section", "mp", None, None), P("section", "dp", "mp", None))
+
     return jax.shard_map(
         per_device, mesh=mesh, in_specs=in_specs, out_specs=out_specs, check_vma=False
     )

time: 111 us -> 97.5 us (0.88)
  Pallas kernels: 24.2 us -> 15.4 us
  blocking collectives: 32.3 us -> 24.9 us
  starting transfers between devices: 14 us -> 17.6 us
  local copies, waits for them, and re-layouts: 3.25 us -> 1.99 us
    pallas_call x4 -> x5, Pallas kernels: 21.8 us -> 14.1 us  [the longest x1 9.82 us: per_device(): call(attend_kernel, [SMEM] + [VMEM] * 2, (shape((3, tokens, width)), shap...]
    all_to_all x1, blocking collectives: 32.3 us -> 24.9 us  [exchange(): lax.all_to_all(array, 'mp', split_axis=0, concat_axis=0, axis_index_group...]
    all_to_all x1 -> x2, starting transfers between devices: 10.2 us -> 13.8 us  [exchange(): lax.all_to_all(array, 'mp', split_axis=0, concat_axis=0, axis_index_group...]
    pallas_call x1, Pallas kernels: 2.42 us -> 1.31 us  [per_device(): call(pack_kernel, [VMEM] * 2, shape((peers, 2 * CELL, width)))]
    unnamed x9 -> x6, local copies, waits for them, and re-layouts: 2.47 us -> 1.99 us
    all_to_all x1 -> x2, waiting for transfers between devices: 23.2 us -> 23.2 us  [exchange(): lax.all_to_all(array, 'mp', split_axis=0, concat_axis=0, axis_index_group...]
  transfers between devices with their start and end apart: 3 -> 4, of which waited for: 2 -> 3; matrix products, arithmetic and copies ran while one was open for 0% -> 0% of each run, Pallas kernels for 0% -> 2%
where the time goes in v2:
time: 97.5 us; the launch traced here: 97.1 us
  waiting for transfers between devices  36.5 us (37%)
  blocking collectives  24.9 us (26%)
  starting transfers between devices  17.6 us (18%)
  Pallas kernels  15.4 us (16%)
  local copies, waits for them, and re-layouts  1.99 us (2%)
    all_to_all x1, blocking collectives, exchange(): lax.all_to_all(array, 'mp', split_axis=0, concat_axis=0, axis_index_group...  24.9 us
    all_to_all x2, waiting for transfers between devices, exchange(): lax.all_to_all(array, 'mp', split_axis=0, concat_axis=0, axis_index_group...  23.2 us
    all_to_all x2, starting transfers between devices, exchange(): lax.all_to_all(array, 'mp', split_axis=0, concat_axis=0, axis_index_group...  13.8 us
    ppermute x1, waiting for transfers between devices, per_device(): lax.ppermute(back, 'section', [(i + 1, i) for i in range(sections - 1)])  13 us
    pallas_call x1, Pallas kernels, per_device(): call(attend_kernel, [SMEM] + [VMEM] * 2, (shape((3, tokens, width)), shap...  9.82 us
    unnamed x6, local copies, waits for them, and re-layouts  1.99 us
  transfers between devices with their start and end apart: 4, of which 3 were waited for; matrix products, arithmetic and copies ran while one was open for 0% of the time, Pallas kernels for 2%

profile of v2, /device:TPU:200, one launch (start us, length us, event | category | flops | bytes accessed | tf_op | source)
XLA Modules:
  0.0 97.1 jit_solution(1198456764728269887)
XLA Ops:
  0.6 0.0 copy-start.1
  0.6 1.0 %copy-done.1 = bf16[1,1,4,128,384]{4,3,2,1,0:T(8,128)(2,1)S(1)} copy-done((bf16[1,1,4,128,384]{4,3,2,1,0:T(8,128)(2,1)S(1)}, bf16[1,1,4,128,384]{4,3,2,1,0:T(8,128)(2,1)}, u32[]{:S(2)}) %copy-start.1) | copy-done | bytes 393240
  1.6 0.0 copy-start.2
  1.6 1.0 %copy-done.2 = bf16[1,1,4,128,384]{4,3,2,1,0:T(8,128)(2,1)S(1)} copy-done((bf16[1,1,4,128,384]{4,3,2,1,0:T(8,128)(2,1)S(1)}, bf16[1,1,4,128,384]{4,3,2,1,0:T(8,128)(2,1)}, u32[]{:S(2)}) %copy-start.2) | copy-done | bytes 393240
  2.6 1.3 %shard_map.50 = bf16[32,32,384]{2,1,0:T(8,128)(2,1)} custom-call(bf16[512,384]{1,0:T(8,128)(2,1)S(1)} %bitcast.10, bf16[512,384]{1,0:T(8,128)(2,1)S(1)} %bitcast.11), custom_call_target="tpu_custom_call" | custom-call | flops 100000000 | bytes 1000000 | tf_op jit(solution)/shard_map/pallas_call | solution.py:257
  3.9 0.0 copy-start
  3.9 10.3 %all-to-all-start = ((bf16[32,32,384]{2,1,0:T(8,128)(2,1)}), bf16[32,32,384]{2,1,0:T(8,128)(2,1)S(1)}, u32[]{:S(2)}, u32[]{:S(2)}) async-start(bf16[32,32,384]{2,1,0:T(8,128)(2,1)} %shard_map.50), calls=%async_computation | async-start | bytes 1572864 | tf_op jit(solution)/shard_map/all_to_all | solution.py:247
  14.2 23.2 %all-to-all-done.in_ref = bf16[32,32,384]{2,1,0:T(8,128)(2,1)S(1)} async-done(((bf16[32,32,384]{2,1,0:T(8,128)(2,1)}), bf16[32,32,384]{2,1,0:T(8,128)(2,1)S(1)}, u32[]{:S(2)}, u32[]{:S(2)}) %all-to-all-start) | async-done | bytes 786464 | tf_op jit(solution)/shard_map/all_to_all | solution.py:247
  37.4 0.0 copy-done
  37.4 9.8 %shard_map.51 = (bf16[3,512,384]{2,1,0:T(8,128)(2,1)S(1)}, bf16[512,384]{1,0:T(8,128)(2,1)S(1)}, f32[512,384]{1,0:T(8,128)S(1)}, f32[512,128]{1,0:T(8,128)S(1)},...) custom-call(s32[1]{0:T(128)} %bitcast.replica_ref, bf16[32,32,384]{2,1,0:T(8,128)(2,1)S(1)} %all-to-all-done.in_ref, ...), custom_call_target="tpu_custom_call" | custom-call | flops 3000000000 | bytes 9000000 | tf_op jit(solution)/shard_map/pallas_call | solution.py:263
  47.2 1.9 %collective-permute-start = (bf16[2,384,384]{2,1,0:T(8,128)(2,1)S(1)}, bf16[2,384,384]{2,1,0:T(8,128)(2,1)S(1)}, u32[]{:S(2)}, u32[]{:S(2)}) collective-permute-start(bf16[2,384,384]{2,1,0:T(8,128)(2,1)S(1)} %get-tuple-element.18), channel_id=1, source_target_pairs={{0,256},{256,0},{1,257},{257,1},{2,258},{258,2},{3,259},{259,3},{4... | collective-permute-start | bytes 1769480 | tf_op jit(solution)/shard_map/ppermute | solution.py:281
  49.2 1.6 %shard_map.52 = bf16[32,16,384]{2,1,0:T(8,128)(2,1)S(1)} custom-call(bf16[3,512,384]{2,1,0:T(8,128)(2,1)S(1)} %get-tuple-element.13.grads_ref, bf16[512,384]{1,0:T(8,128)(2,1)S(1)} %get-tuple-element.14.delta_ref, f32[512,384]{1,0:T(8,128)S(1)} %get-tuple-element.15.standard_ref, f32[512,128]{1,0:T(8,128)S(1)} %get-tuple-element.16.inverse_ref, ...), custom_call_target="tpu_custom_call" | custom-call | flops 1000000000 | bytes 3000000 | tf_op jit(solution)/shard_map/pallas_call | solution.py:282
  50.8 0.3 collective-permute-done.got_ref
  51.1 1.3 %shard_map.53 = bf16[4,192,384]{2,1,0:T(8,128)(2,1)} custom-call(f32[2,384,384]{2,1,0:T(8,128)S(1)} %get-tuple-element.17.keep_ref, bf16[2,384,384]{2,1,0:T(8,128)(2,1)S(1)} %collective-permute-done.got_ref), custom_call_target="tpu_custom_call" | custom-call | flops 1000000000 | bytes 3000000 | tf_op jit(solution)/shard_map/pallas_call | solution.py:288
  52.4 3.5 %all-to-all-start.1 = ((bf16[4,192,384]{2,1,0:T(8,128)(2,1)}), bf16[4,192,384]{2,1,0:T(8,128)(2,1)S(1)}, u32[]{:S(2)}, u32[]{:S(2)}) async-start(bf16[4,192,384]{2,1,0:T(8,128)(2,1)} %shard_map.53), calls=%async_computation.1 | async-start | bytes 1179648 | tf_op jit(solution)/shard_map/all_to_all | solution.py:247
  55.9 1.9 %collective-permute-start.1 = (bf16[32,16,384]{2,1,0:T(8,128)(2,1)S(1)}, bf16[32,16,384]{2,1,0:T(8,128)(2,1)S(1)}, u32[]{:S(2)}, u32[]{:S(2)}) collective-permute-start(bf16[32,16,384]{2,1,0:T(8,128)(2,1)S(1)} %shard_map.52), channel_id=1, source_target_pairs={{32,0},{64,32},{96,64},{128,96},{160,128},{192,160},{224,192},{33,... | collective-permute-start | bytes 1179656 | tf_op jit(solution)/shard_map/ppermute | solution.py:287
  57.8 13.0 %collective-permute-done.1.back_ref = bf16[32,16,384]{2,1,0:T(8,128)(2,1)S(1)} collective-permute-done((bf16[32,16,384]{2,1,0:T(8,128)(2,1)S(1)}, bf16[32,16,384]{2,1,0:T(8,128)(2,1)S(1)}, u32[]{:S(2)}, u32[]{:S(2)}) %collective-permute-start.1) | collective-permute-done | bytes 393248 | tf_op jit(solution)/shard_map/ppermute | solution.py:287
  70.8 0.0 all-to-all-done.1.parts_ref
  70.8 0.3 shard_map.54
  71.2 24.9 %all_to_all.15.in_ref = bf16[32,24,384]{2,1,0:T(8,128)(2,1)S(1)} all-to-all(bf16[32,24,384]{2,1,0:T(8,128)(2,1)S(1)} %shard_map.54), channel_id=1, replica_groups=mesh['dp'=2,'section'=8,'mp'=32] {'mp'}, dimensions={0} | all-to-all | bytes 1179648 | tf_op jit(solution)/shard_map/all_to_all | solution.py:247
  96.0 1.0 %shard_map.55 = (bf16[512,384]{1,0:T(8,128)(2,1)}, f32[12,2,384]{2,1,0:T(2,128)}) custom-call(bf16[32,24,384]{2,1,0:T(8,128)(2,1)S(1)} %all_to_all.15.in_ref), custom_call_target="tpu_custom_call" | custom-call | flops 100000000 | bytes 1000000 | tf_op jit(solution)/shard_map/pallas_call | solution.py:296
Async XLA Ops:
  0.6 1.0 %copy-start.1 = (bf16[1,1,4,128,384]{4,3,2,1,0:T(8,128)(2,1)S(1)}, bf16[1,1,4,128,384]{4,3,2,1,0:T(8,128)(2,1)}, u32[]{:S(2)}) copy-start(bf16[1,1,4,128,384]{4,3,2,1,0:T(8,128)(2,1)} %param.3) | copy-start | bytes 1179652
  1.6 1.0 %copy-start.2 = (bf16[1,1,4,128,384]{4,3,2,1,0:T(8,128)(2,1)S(1)}, bf16[1,1,4,128,384]{4,3,2,1,0:T(8,128)(2,1)}, u32[]{:S(2)}) copy-start(bf16[1,1,4,128,384]{4,3,2,1,0:T(8,128)(2,1)} %param.4) | copy-start | bytes 1179652
  3.9 33.5 %copy-start = (bf16[1,4,384,384]{3,2,1,0:T(8,128)(2,1)S(1)}, bf16[1,4,384,384]{3,2,1,0:T(8,128)(2,1)}, u32[]{:S(2)}) copy-start(bf16[1,4,384,384]{3,2,1,0:T(8,128)(2,1)} %param.5) | copy-start | bytes 3538948
  3.9 33.5 %all-to-all-start = ((bf16[32,32,384]{2,1,0:T(8,128)(2,1)}), bf16[32,32,384]{2,1,0:T(8,128)(2,1)S(1)}, u32[]{:S(2)}, u32[]{:S(2)}) async-start(bf16[32,32,384]{2,1,0:T(8,128)(2,1)} %shard_map.50), calls=%async_computation | async-start | bytes 1572864 | tf_op jit(solution)/shard_map/all_to_all | solution.py:247
  47.2 3.9 %collective-permute-start = (bf16[2,384,384]{2,1,0:T(8,128)(2,1)S(1)}, bf16[2,384,384]{2,1,0:T(8,128)(2,1)S(1)}, u32[]{:S(2)}, u32[]{:S(2)}) collective-permute-start(bf16[2,384,384]{2,1,0:T(8,128)(2,1)S(1)} %get-tuple-element.18), channel_id=1, source_target_pairs={{0,256},{256,0},{1,257},{257,1},{2,258},{258,2},{3,259},{259,3},{4... | collective-permute-start | bytes 1769480 | tf_op jit(solution)/shard_map/ppermute | solution.py:281
  52.4 18.4 %all-to-all-start.1 = ((bf16[4,192,384]{2,1,0:T(8,128)(2,1)}), bf16[4,192,384]{2,1,0:T(8,128)(2,1)S(1)}, u32[]{:S(2)}, u32[]{:S(2)}) async-start(bf16[4,192,384]{2,1,0:T(8,128)(2,1)} %shard_map.53), calls=%async_computation.1 | async-start | bytes 1179648 | tf_op jit(solution)/shard_map/all_to_all | solution.py:247
  55.9 14.9 %collective-permute-start.1 = (bf16[32,16,384]{2,1,0:T(8,128)(2,1)S(1)}, bf16[32,16,384]{2,1,0:T(8,128)(2,1)S(1)}, u32[]{:S(2)}, u32[]{:S(2)}) collective-permute-start(bf16[32,16,384]{2,1,0:T(8,128)(2,1)S(1)} %shard_map.52), channel_id=1, source_target_pairs={{32,0},{64,32},{96,64},{128,96},{160,128},{192,160},{224,192},{33,... | collective-permute-start | bytes 1179656 | tf_op jit(solution)/shard_map/ppermute | solution.py:287

commit v3 on v2

--- a/solution.py
+++ b/solution.py
@@ -19,6 +19,7 @@
 NX = 4
 PAD = 8
 VMEM = pl.BlockSpec(memory_space=pltpu.VMEM)
+HBM = pl.BlockSpec(memory_space=pltpu.HBM)
 SMEM = pl.BlockSpec(memory_space=pltpu.SMEM)
 
 
@@ -36,16 +37,22 @@
     return dot(matrix, rows).astype(BF16)
 
 
-def pack_kernel(act_ref, grad_ref, out_ref):
+def pack_kernel(act_ref, grad_ref, out_ref, held_ref, sems):
+    copies = [
+        pltpu.make_async_copy(ref, held_ref.at[slot], sems.at[slot])
+        for slot, ref in enumerate((act_ref, grad_ref))
+    ]
+    for copy in copies:
+        copy.start()
     order = selection(BLOCK, lambda o: ((o >> 2) & 3) * 64 + (o >> 4) * 4 + (o & 3))
     groups = out_ref.shape[0] // GROUP
     residues = act_ref.shape[0] // ROWS
     span = GROUP * COLS
-    for slot, ref in enumerate((act_ref, grad_ref)):
+    for slot, copy in enumerate(copies):
+        copy.wait()
         for g in range(groups):
-            rows = jnp.concatenate(
-                [ref[i * residues + g * span : i * residues + (g + 1) * span] for i in range(ROWS)]
-            )
+            starts = [i * residues + g * span for i in range(ROWS)]
+            rows = jnp.concatenate([held_ref[slot, at : at + span] for at in starts])
             moved = reorder(order, rows).reshape(GROUP, CELL, -1)
             out_ref[g * GROUP : (g + 1) * GROUP, slot * CELL : (slot + 1) * CELL] = moved
 
@@ -87,9 +94,9 @@
     inverse_ref[...] = jnp.broadcast_to(inverse, inverse_ref.shape)
     normed = standard.astype(BF16)
     normed_ref[...] = normed
-    for n in range(3):
-        proj_ref[n] = dot(normed, weight_ref[n]).astype(BF16)
-    proj_ref[3] = dot(delta_ref[...], weight_ref[3]).astype(BF16)
+    joint = jnp.concatenate([weight_ref[n] for n in range(3)], axis=1)
+    proj_ref[:, : 3 * width] = dot(normed, joint).astype(BF16)
+    proj_ref[:, 3 * width :] = dot(delta_ref[...], weight_ref[3]).astype(BF16)
 
     scaling = HEAD_DIM ** (-0.5)
     low = lax.broadcasted_iota(jnp.int32, (seqs, LANES), 1) < HEAD_DIM
@@ -103,46 +110,45 @@
 
     def column(j, carry):
         here = pl.ds(pl.multiple_of(j * seqs, seqs), seqs)
-        for pair in range(width // LANES):
-            lanes = slice(pair * LANES, (pair + 1) * LANES)
-            query, key, value, delta = (proj_ref[n, here, lanes] for n in range(4))
-            keys, vals = apart(key), apart(value)
-            scores = dot(query, keys, ((1,), (1,))) * scaling
-            dprobs = dot(delta, vals, ((1,), (1,)))
+        pairs = range(width // LANES)
+        loaded = [
+            [proj_ref[here, n * width + p * LANES : n * width + (p + 1) * LANES] for n in range(4)]
+            for p in pairs
+        ]
+        split = [(apart(key), apart(value)) for _, key, value, _ in loaded]
+        scores = [dot(split[p][0], loaded[p][0], ((1,), (1,))) * scaling for p in pairs]
+        dprobs = [dot(split[p][1], loaded[p][3], ((1,), (1,))) for p in pairs]
+        for p in pairs:
+            query, _, _, delta = loaded[p]
+            keys, vals = split[p]
             soft, dscores = [], []
             for h in range(2):
-                part = scores[:, h * seqs : (h + 1) * seqs]
-                exponent = jnp.exp(part - jnp.max(part, axis=-1, keepdims=True))
-                prob = exponent / jnp.sum(exponent, axis=-1, keepdims=True)
-                dprob = dprobs[:, h * seqs : (h + 1) * seqs]
-                row_delta = jnp.sum(prob * dprob, axis=-1, keepdims=True)
+                part = scores[p][h * seqs : (h + 1) * seqs]
+                exponent = jnp.exp(part - jnp.max(part, axis=0, keepdims=True))
+                prob = exponent * (1.0 / jnp.sum(exponent, axis=0, keepdims=True))
+                dprob = dprobs[p][h * seqs : (h + 1) * seqs]
+                column_delta = jnp.sum(prob * dprob, axis=0, keepdims=True)
                 soft.append(prob.astype(BF16))
-                dscores.append((prob * (dprob - row_delta)).astype(BF16))
-            soft = jnp.concatenate(soft, axis=1)
-            dscores = jnp.concatenate(dscores, axis=1)
-            attn_ref[here, lanes] = dot(soft, vals).astype(BF16)
-            grads_ref[0, here, lanes] = (dot(dscores, keys) * scaling).astype(BF16)
-            key_grad = joined(dot(dscores, query, ((0,), (0,))))
-            grads_ref[1, here, lanes] = (key_grad * scaling).astype(BF16)
-            grads_ref[2, here, lanes] = joined(dot(soft, delta, ((0,), (0,)))).astype(BF16)
+                dscores.append((prob * (dprob - column_delta)).astype(BF16))
+            soft = jnp.concatenate(soft)
+            dscores = jnp.concatenate(dscores)
+            lanes = [slice(n * width + p * LANES, n * width + (p + 1) * LANES) for n in range(3)]
+            attn_ref[here, lanes[0]] = dot(soft, vals, ((0,), (0,))).astype(BF16)
+            query_grad = dot(dscores, keys, ((0,), (0,)))
+            grads_ref[here, lanes[0]] = (query_grad * scaling).astype(BF16)
+            grads_ref[here, lanes[1]] = (joined(dot(dscores, query)) * scaling).astype(BF16)
+            grads_ref[here, lanes[2]] = joined(dot(soft, delta)).astype(BF16)
         return carry
 
     lax.fori_loop(0, COLS, column, 0)
 
-    replica = replica_ref[0]
-    for n in range(4):
-        if n < 3:
-            term = dot(normed_ref[...], grads_ref[n], ((0,), (0,)))
-        else:
-            term = dot(delta_ref[...], attn_ref[...], ((0,), (0,)))
-
-        @pl.when(replica == n // 2)
-        def _():
-            keep_ref[n % 2] = term
-
-        @pl.when(replica != n // 2)
-        def _():
-            give_ref[n % 2] = term.astype(BF16)
+    first = replica_ref[0] == 0
+    term = dot(normed_ref[...], grads_ref[...], ((0,), (0,)))
+    terms = [term[:, n * width : (n + 1) * width] for n in range(3)]
+    terms.append(dot(delta_ref[...], attn_ref[...], ((0,), (0,))))
+    for m in range(2):
+        keep_ref[m] = jnp.where(first, terms[m], terms[m + 2])
+        give_ref[m] = jnp.where(first, terms[m + 2], terms[m]).astype(BF16)
 
 
 def input_kernel(grads_ref, delta_ref, standard_ref, inverse_ref, weight_ref, back_ref):
@@ -150,9 +156,8 @@
     tokens, width = delta_ref.shape
     seqs = tokens // COLS
     span = GROUP * ROWS
-    grad_in = dot(grads_ref[0], weight_ref[0], ((1,), (1,)))
-    grad_in += dot(grads_ref[1], weight_ref[1], ((1,), (1,)))
-    grad_in += dot(grads_ref[2], weight_ref[2], ((1,), (1,)))
+    joint = jnp.concatenate([weight_ref[n] for n in range(3)], axis=1)
+    grad_in = dot(grads_ref[...], joint, ((1,), (1,)))
     standard = standard_ref[...]
     grad_mean = jnp.mean(grad_in, axis=-1, keepdims=True)
     grad_proj = jnp.mean(grad_in * standard, axis=-1, keepdims=True)
@@ -229,14 +234,14 @@
     return jax.ShapeDtypeStruct(dims, dtype)
 
 
-def call(kernel, in_specs, out_shape, scratch=(), cost=(1e8, 1e6)):
+def call(kernel, in_specs, out_shape, scratch=(), cost=(1e8, 1e6), mib=14):
     return pl.pallas_call(
         kernel,
         in_specs=in_specs,
         out_specs=jax.tree.map(lambda _: VMEM, out_shape),
         out_shape=out_shape,
         scratch_shapes=scratch,
-        compiler_params=pltpu.CompilerParams(vmem_limit_bytes=14 * 1024 * 1024),
+        compiler_params=pltpu.CompilerParams(vmem_limit_bytes=mib * 1024 * 1024),
         cost_estimate=pl.CostEstimate(
             flops=int(cost[0]), bytes_accessed=int(cost[1]), transcendentals=0
         ),
@@ -254,7 +259,13 @@
     peers = lax.axis_size("mp")
     tokens = rows * residues
     part = width // peers
-    packed = call(pack_kernel, [VMEM] * 2, shape((peers, 2 * CELL, width)))(
+    packed = call(
+        pack_kernel,
+        [HBM] * 2,
+        shape((peers, 2 * CELL, width)),
+        [pltpu.VMEM((2, tokens, width), BF16), pltpu.SemaphoreType.DMA((2,))],
+        mib=56,
+    )(
         activations.reshape(tokens, width), out_grads.reshape(tokens, width)
     )
     arrived = exchange(packed)
@@ -264,7 +275,7 @@
         attend_kernel,
         [SMEM] + [VMEM] * 2,
         (
-            shape((3, tokens, width)),
+            shape((tokens, 3 * width)),
             shape((tokens, width)),
             shape((tokens, width), F32),
             shape((tokens, LANES), F32),
@@ -274,7 +285,7 @@
         [
             pltpu.VMEM((tokens, width), BF16),
             pltpu.VMEM((tokens, width), BF16),
-            pltpu.VMEM((4, tokens, width), BF16),
+            pltpu.VMEM((tokens, 4 * width), BF16),
         ],
         cost=(3e9, 9e6),
     )(replica, arrived, weights)

time: 97.5 us -> 92.2 us (0.946)
  Pallas kernels: 15.4 us -> 11.8 us
  local copies, waits for them, and re-layouts: 1.99 us -> 0.01 us
    pallas_call x2, Pallas kernels: 11.1 us -> 7.83 us  [the longest x1 5.33 us: per_device(): call(attend_kernel, [SMEM] + [VMEM] * 2, (shape((tokens, 3 * width)), sha...]
    unnamed x6 -> x2, local copies, waits for them, and re-layouts: 1.99 us -> 0.01 us
  transfers between devices with their start and end apart: 4 -> 4, of which waited for: 3 -> 3; matrix products, arithmetic and copies ran while one was open for 0% -> 0% of each run, Pallas kernels for 2% -> 1%
where the time goes in v3:
time: 92.2 us; the launch traced here: 91.8 us
  waiting for transfers between devices  36.8 us (40%)
  blocking collectives  24.9 us (27%)
  starting transfers between devices  17.6 us (19%)
  Pallas kernels  11.8 us (13%)
    all_to_all x1, blocking collectives, exchange(): lax.all_to_all(array, 'mp', split_axis=0, concat_axis=0, axis_index_group...  24.9 us
    all_to_all x2, waiting for transfers between devices, exchange(): lax.all_to_all(array, 'mp', split_axis=0, concat_axis=0, axis_index_group...  23.2 us
    all_to_all x2, starting transfers between devices, exchange(): lax.all_to_all(array, 'mp', split_axis=0, concat_axis=0, axis_index_group...  13.8 us
    ppermute x1, waiting for transfers between devices, per_device(): lax.ppermute(back, 'section', [(i + 1, i) for i in range(sections - 1)])  13 us
    pallas_call x1, Pallas kernels, per_device(): call(attend_kernel, [SMEM] + [VMEM] * 2, (shape((tokens, 3 * width)), sha...  5.33 us
    pallas_call x1, Pallas kernels, per_device(): call(pack_kernel, [HBM] * 2, shape((peers, 2 * CELL, width)), [pltpu.VMEM...  2.5 us
    ppermute x1, starting transfers between devices, per_device(): got = lax.ppermute(give, 'dp', [(0, 1), (1, 0)])  1.92 us
    ppermute x1, starting transfers between devices, per_device(): lax.ppermute(back, 'section', [(i + 1, i) for i in range(sections - 1)])  1.92 us
  transfers between devices with their start and end apart: 4, of which 3 were waited for; matrix products, arithmetic and copies ran while one was open for 0% of the time, Pallas kernels for 1%

profile of v3, /device:TPU:200, one launch (start us, length us, event | category | flops | bytes accessed | tf_op | source)
XLA Modules:
  0.0 91.8 jit_solution(10280848618816064862)
XLA Ops:
  0.6 2.5 %shard_map.50 = bf16[32,32,384]{2,1,0:T(8,128)(2,1)} custom-call(bf16[512,384]{1,0:T(8,128)(2,1)} %bitcast.10, bf16[512,384]{1,0:T(8,128)(2,1)} %bitcast.11), custom_call_target="tpu_custom_call" | custom-call | flops 100000000 | bytes 1000000 | tf_op jit(solution)/shard_map/pallas_call | solution.py:262
  3.1 0.0 copy-start
  3.1 10.3 %all-to-all-start = ((bf16[32,32,384]{2,1,0:T(8,128)(2,1)}), bf16[32,32,384]{2,1,0:T(8,128)(2,1)S(1)}, u32[]{:S(2)}, u32[]{:S(2)}) async-start(bf16[32,32,384]{2,1,0:T(8,128)(2,1)} %shard_map.50), calls=%async_computation | async-start | bytes 1572864 | tf_op jit(solution)/shard_map/all_to_all | solution.py:252
  13.5 23.2 %all-to-all-done.in_ref = bf16[32,32,384]{2,1,0:T(8,128)(2,1)S(1)} async-done(((bf16[32,32,384]{2,1,0:T(8,128)(2,1)}), bf16[32,32,384]{2,1,0:T(8,128)(2,1)S(1)}, u32[]{:S(2)}, u32[]{:S(2)}) %all-to-all-start) | async-done | bytes 786464 | tf_op jit(solution)/shard_map/all_to_all | solution.py:252
  36.6 0.0 copy-done
  36.6 5.3 %shard_map.51 = (bf16[512,1152]{1,0:T(8,128)(2,1)S(1)}, bf16[512,384]{1,0:T(8,128)(2,1)S(1)}, f32[512,384]{1,0:T(8,128)S(1)}, f32[512,128]{1,0:T(8,128)S(1)}, f3...) custom-call(s32[1]{0:T(128)} %bitcast.replica_ref, bf16[32,32,384]{2,1,0:T(8,128)(2,1)S(1)} %all-to-all-done.in_ref, ...), custom_call_target="tpu_custom_call" | custom-call | flops 3000000000 | bytes 9000000 | tf_op jit(solution)/shard_map/pallas_call | solution.py:274
  42.0 1.9 %collective-permute-start = (bf16[2,384,384]{2,1,0:T(8,128)(2,1)S(1)}, bf16[2,384,384]{2,1,0:T(8,128)(2,1)S(1)}, u32[]{:S(2)}, u32[]{:S(2)}) collective-permute-start(bf16[2,384,384]{2,1,0:T(8,128)(2,1)S(1)} %get-tuple-element.18), channel_id=1, source_target_pairs={{0,256},{256,0},{1,257},{257,1},{2,258},{258,2},{3,259},{259,3},{4... | collective-permute-start | bytes 1769480 | tf_op jit(solution)/shard_map/ppermute | solution.py:292
  43.9 1.3 %shard_map.52 = bf16[32,16,384]{2,1,0:T(8,128)(2,1)S(1)} custom-call(bf16[512,1152]{1,0:T(8,128)(2,1)S(1)} %get-tuple-element.13.grads_ref, bf16[512,384]{1,0:T(8,128)(2,1)S(1)} %get-tuple-element.14.delta_ref, f32[512,384]{1,0:T(8,128)S(1)} %get-tuple-element.15.standard_ref, f32[512,128]{1,0:T(8,128)S(1)} %get-tuple-element.16.inverse_ref, ...), custom_call_target="tpu_custom_call" | custom-call | flops 1000000000 | bytes 3000000 | tf_op jit(solution)/shard_map/pallas_call | solution.py:293
  45.2 0.6 collective-permute-done.got_ref
  45.9 1.3 %shard_map.53 = bf16[4,192,384]{2,1,0:T(8,128)(2,1)} custom-call(f32[2,384,384]{2,1,0:T(8,128)S(1)} %get-tuple-element.17.keep_ref, bf16[2,384,384]{2,1,0:T(8,128)(2,1)S(1)} %collective-permute-done.got_ref), custom_call_target="tpu_custom_call" | custom-call | flops 1000000000 | bytes 3000000 | tf_op jit(solution)/shard_map/pallas_call | solution.py:299
  47.2 3.5 %all-to-all-start.1 = ((bf16[4,192,384]{2,1,0:T(8,128)(2,1)}), bf16[4,192,384]{2,1,0:T(8,128)(2,1)S(1)}, u32[]{:S(2)}, u32[]{:S(2)}) async-start(bf16[4,192,384]{2,1,0:T(8,128)(2,1)} %shard_map.53), calls=%async_computation.1 | async-start | bytes 1179648 | tf_op jit(solution)/shard_map/all_to_all | solution.py:252
  50.7 1.9 %collective-permute-start.1 = (bf16[32,16,384]{2,1,0:T(8,128)(2,1)S(1)}, bf16[32,16,384]{2,1,0:T(8,128)(2,1)S(1)}, u32[]{:S(2)}, u32[]{:S(2)}) collective-permute-start(bf16[32,16,384]{2,1,0:T(8,128)(2,1)S(1)} %shard_map.52), channel_id=1, source_target_pairs={{32,0},{64,32},{96,64},{128,96},{160,128},{192,160},{224,192},{33,... | collective-permute-start | bytes 1179656 | tf_op jit(solution)/shard_map/ppermute | solution.py:298
  52.6 13.0 %collective-permute-done.1.back_ref = bf16[32,16,384]{2,1,0:T(8,128)(2,1)S(1)} collective-permute-done((bf16[32,16,384]{2,1,0:T(8,128)(2,1)S(1)}, bf16[32,16,384]{2,1,0:T(8,128)(2,1)S(1)}, u32[]{:S(2)}, u32[]{:S(2)}) %collective-permute-start.1) | collective-permute-done | bytes 393248 | tf_op jit(solution)/shard_map/ppermute | solution.py:298
  65.6 0.0 all-to-all-done.1.parts_ref
  65.6 0.3 shard_map.54
  65.9 24.9 %all_to_all.15.in_ref = bf16[32,24,384]{2,1,0:T(8,128)(2,1)S(1)} all-to-all(bf16[32,24,384]{2,1,0:T(8,128)(2,1)S(1)} %shard_map.54), channel_id=1, replica_groups=mesh['dp'=2,'section'=8,'mp'=32] {'mp'}, dimensions={0} | all-to-all | bytes 1179648 | tf_op jit(solution)/shard_map/all_to_all | solution.py:252
  90.8 1.0 %shard_map.55 = (bf16[512,384]{1,0:T(8,128)(2,1)}, f32[12,2,384]{2,1,0:T(2,128)}) custom-call(bf16[32,24,384]{2,1,0:T(8,128)(2,1)S(1)} %all_to_all.15.in_ref), custom_call_target="tpu_custom_call" | custom-call | flops 100000000 | bytes 1000000 | tf_op jit(solution)/shard_map/pallas_call | solution.py:307
Async XLA Ops:
  3.1 33.5 %copy-start = (bf16[1,4,384,384]{3,2,1,0:T(8,128)(2,1)S(1)}, bf16[1,4,384,384]{3,2,1,0:T(8,128)(2,1)}, u32[]{:S(2)}) copy-start(bf16[1,4,384,384]{3,2,1,0:T(8,128)(2,1)} %param.5) | copy-start | bytes 3538948
  3.1 33.5 %all-to-all-start = ((bf16[32,32,384]{2,1,0:T(8,128)(2,1)}), bf16[32,32,384]{2,1,0:T(8,128)(2,1)S(1)}, u32[]{:S(2)}, u32[]{:S(2)}) async-start(bf16[32,32,384]{2,1,0:T(8,128)(2,1)} %shard_map.50), calls=%async_computation | async-start | bytes 1572864 | tf_op jit(solution)/shard_map/all_to_all | solution.py:252
  42.0 3.9 %collective-permute-start = (bf16[2,384,384]{2,1,0:T(8,128)(2,1)S(1)}, bf16[2,384,384]{2,1,0:T(8,128)(2,1)S(1)}, u32[]{:S(2)}, u32[]{:S(2)}) collective-permute-start(bf16[2,384,384]{2,1,0:T(8,128)(2,1)S(1)} %get-tuple-element.18), channel_id=1, source_target_pairs={{0,256},{256,0},{1,257},{257,1},{2,258},{258,2},{3,259},{259,3},{4... | collective-permute-start | bytes 1769480 | tf_op jit(solution)/shard_map/ppermute | solution.py:292
  47.2 18.4 %all-to-all-start.1 = ((bf16[4,192,384]{2,1,0:T(8,128)(2,1)}), bf16[4,192,384]{2,1,0:T(8,128)(2,1)S(1)}, u32[]{:S(2)}, u32[]{:S(2)}) async-start(bf16[4,192,384]{2,1,0:T(8,128)(2,1)} %shard_map.53), calls=%async_computation.1 | async-start | bytes 1179648 | tf_op jit(solution)/shard_map/all_to_all | solution.py:252
  50.7 14.9 %collective-permute-start.1 = (bf16[32,16,384]{2,1,0:T(8,128)(2,1)S(1)}, bf16[32,16,384]{2,1,0:T(8,128)(2,1)S(1)}, u32[]{:S(2)}, u32[]{:S(2)}) collective-permute-start(bf16[32,16,384]{2,1,0:T(8,128)(2,1)S(1)} %shard_map.52), channel_id=1, source_target_pairs={{32,0},{64,32},{96,64},{128,96},{160,128},{192,160},{224,192},{33,... | collective-permute-start | bytes 1179656 | tf_op jit(solution)/shard_map/ppermute | solution.py:298

commit v4 on v3

--- a/solution.py
+++ b/solution.py
@@ -17,7 +17,7 @@
 GROUP = 16
 BLOCK = GROUP * CELL
 NX = 4
-PAD = 8
+NY = 8
 VMEM = pl.BlockSpec(memory_space=pltpu.VMEM)
 HBM = pl.BlockSpec(memory_space=pltpu.HBM)
 SMEM = pl.BlockSpec(memory_space=pltpu.SMEM)
@@ -172,62 +172,54 @@
         back_ref[g * GROUP : (g + 1) * GROUP] = reorder(order, rows).reshape(GROUP, CELL, width)
 
 
-def spread_kernel(keep_ref, got_ref, out_ref):
-    quarters, held, width = out_ref.shape
-    peers = held // (2 * (width // 128))
-    part = width // peers
-    piece = part // quarters
-    block = 8 * part
-    cell = 2 * piece
+def spread_kernel(place_ref, keep_ref, got_ref, hold_ref, send_ref):
+    part = hold_ref.shape[2]
+    x = lax.div(place_ref[0], NY)
+    near = x + 1 - 2 * lax.rem(x, 2)
+    for ref, blocks in ((hold_ref, (x, NX - 1 - x)), (send_ref, (near, NX - 1 - near))):
+        for slot, block in enumerate(blocks):
+            rows = pl.ds(pl.multiple_of(block * part, part), part)
+            for m in range(2):
+                total = keep_ref[m, rows] + got_ref[m, rows].astype(F32)
+                ref[slot, m] = total.astype(ref.dtype)
+
+
+def halve_kernel(hold_ref, got_ref, own_ref, send_ref):
+    own_ref[...] = hold_ref[0] + got_ref[0].astype(F32)
+    send_ref[...] = (hold_ref[1] + got_ref[1].astype(F32)).astype(BF16)
+
+
+def order_kernel(own_ref, got_ref, out_ref):
+    peers, held, width = out_ref.shape
+    part = held // 2
+    size = peers * held
 
     def source_of(o):
-        quarter = o // (8 * cell)
-        rest = o - quarter * (8 * cell)
-        device = rest // cell
-        inside = rest - device * cell
-        return (inside & 1) * block + device * part + quarter * piece + (inside >> 1)
-
-    order = selection(2 * block, source_of)
-    for g in range(peers // 8):
-        here = slice(g * block, (g + 1) * block)
-        rows = [(keep_ref[m, here] + got_ref[m, here].astype(F32)).astype(BF16) for m in range(2)]
-        moved = reorder(order, jnp.concatenate(rows))
-        for q in range(quarters):
-            to = slice(g * 8 * cell, (g + 1) * 8 * cell)
-            out_ref[q, to] = moved[q * 8 * cell : (q + 1) * 8 * cell]
-
-
-def leave_kernel(parts_ref, back_ref, out_ref):
-    peers, _, width = back_ref.shape
-    out_ref[:, :CELL] = back_ref[...]
-    total = jnp.sum(parts_ref[...].astype(F32), axis=0).astype(BF16)
-    cell = total.shape[0] // peers
-    out = lax.broadcasted_iota(jnp.int32, (peers * PAD, peers * cell), 0)
-    source = lax.broadcasted_iota(jnp.int32, (peers * PAD, peers * cell), 1)
-    fits = jnp.logical_and((out >> 3) * cell + (out & 7) == source, (out & 7) < cell)
-    order = jnp.where(fits, 1.0, 0.0).astype(BF16)
-    out_ref[:, CELL:] = reorder(order, total).reshape(peers, PAD, width)
-
-
-def final_kernel(in_ref, received_ref, grads_ref):
+        peer = o // held
+        inside = o - peer * held
+        return (inside & 1) * (size // 2) + peer * part + (inside >> 1)
+
+    rows = (own_ref[...] + got_ref[...].astype(F32)).astype(BF16).reshape(size, width)
+    out_ref[...] = reorder(selection(size, source_of), rows).reshape(peers, held, width)
+
+
+def total_kernel(in_ref, out_ref):
+    total = jnp.sum(in_ref[...].astype(F32), axis=0)
+    for row in range(out_ref.shape[0]):
+        out_ref[row] = total[2 * row : 2 * row + 2]
+
+
+def unpack_kernel(in_ref, out_ref):
     peers, _, width = in_ref.shape
-    groups = peers // GROUP
     residues = peers * COLS
     span = GROUP * COLS
     order = selection(BLOCK, lambda o: ((o >> 2) & 15) * 16 + (o >> 6) * 4 + (o & 3))
-    for g in range(groups):
-        rows = in_ref[g * GROUP : (g + 1) * GROUP, :CELL].reshape(BLOCK, width)
+    for g in range(peers // GROUP):
+        rows = in_ref[g * GROUP : (g + 1) * GROUP].reshape(BLOCK, width)
         moved = reorder(order, rows)
         for i in range(ROWS):
             to = slice(i * residues + g * span, i * residues + (g + 1) * span)
-            received_ref[to] = moved[i * span : (i + 1) * span]
-    parts = in_ref[:, CELL:].astype(F32)
-    quarters = NX
-    parts = jnp.sum(parts.reshape(quarters, peers // quarters, PAD, width), axis=1)
-    piece = grads_ref.shape[0] // quarters
-    for q in range(quarters):
-        for u in range(piece):
-            grads_ref[q * piece + u] = parts[q, 2 * u : 2 * u + 2]
+            out_ref[to] = moved[i * span : (i + 1) * span]
 
 
 def shape(dims, dtype=BF16):
@@ -293,20 +285,34 @@
     back = call(input_kernel, [VMEM] * 5, shape((peers, CELL, width)), cost=(1e9, 3e6))(
         grads, delta, standard, inverse, weights
     )
-    keep, back = lax.optimization_barrier((keep, back))
+    landed = exchange(back)
+
+    ny = NY
+    block = width // NX
+    place = lax.axis_index("mp").astype(jnp.int32).reshape(1)
+
+    def over_x(array, partner_of):
+        pairs = [(q * ny + y, partner_of(q) * ny + y) for q in range(NX) for y in range(ny)]
+        return lax.ppermute(array, "mp", pairs)
+
+    hold, send = call(
+        spread_kernel,
+        [SMEM] + [VMEM] * 2,
+        (shape((2, 2, block, width), F32), shape((2, 2, block, width))),
+    )(place, keep, got)
+    got = over_x(send, lambda q: q ^ 1)
+    own, send = call(
+        halve_kernel, [VMEM] * 2, (shape((2, block, width), F32), shape((2, block, width)))
+    )(hold, got)
+    got = over_x(send, lambda q: NX - 1 - q)
+
     sections = lax.axis_size("section")
-    back = lax.ppermute(back, "section", [(i + 1, i) for i in range(sections - 1)])
-    spread = call(
-        spread_kernel, [VMEM] * 2, shape((NX, 2 * width // NX, width)), cost=(1e9, 3e6)
-    )(keep, got)
-    ny = peers // NX
-    groups = [[x * ny + y for x in range(NX)] for y in range(ny)]
-    parts = exchange(spread, groups)
-    leaving = call(leave_kernel, [VMEM] * 2, shape((peers, CELL + PAD, width)))(parts, back)
-    landed = exchange(leaving)
-    received, weight_grads = call(
-        final_kernel, [VMEM], (shape((tokens, width)), shape((part, 2, width), F32))
-    )(landed)
+    received = call(unpack_kernel, [VMEM], shape((tokens, width)))(landed)
+    received = lax.ppermute(received, "section", [(i + 1, i) for i in range(sections - 1)])
+
+    parts = call(order_kernel, [VMEM] * 2, shape((ny, 2 * part, width)))(own, got)
+    parts = exchange(parts, [[q * ny + y for y in range(ny)] for q in range(NX)])
+    weight_grads = call(total_kernel, [VMEM], shape((part, 2, width), F32))(parts)
     return (received.reshape(activations.shape), weight_grads.transpose(1, 0, 2)[None])
 
 

time: 92.2 us -> 92.6 us (level)
  the two profiles are of different devices: /device:TPU:200 before, /device:TPU:192 now
where the time goes in v4:
time: 92.6 us; the launch traced here: 92.1 us
  waiting for transfers between devices  46 us (50%)
  starting transfers between devices  31.9 us (34%)
  Pallas kernels  12.7 us (14%)
    all_to_all x3, waiting for transfers between devices, exchange(): lax.all_to_all(array, 'mp', split_axis=0, concat_axis=0, axis_index_group...  29.5 us
    all_to_all x3, starting transfers between devices, exchange(): lax.all_to_all(array, 'mp', split_axis=0, concat_axis=0, axis_index_group...  20.2 us
    ppermute x2, waiting for transfers between devices, over_x(): return lax.ppermute(array, 'mp', pairs)  13.4 us
    ppermute x2, starting transfers between devices, over_x(): return lax.ppermute(array, 'mp', pairs)  7.84 us
    pallas_call x1, Pallas kernels, per_device(): call(attend_kernel, [SMEM] + [VMEM] * 2, (shape((tokens, 3 * width)), sha...  6.15 us
    ppermute x1, waiting for transfers between devices, per_device(): lax.ppermute(received, 'section', [(i + 1, i) for i in range(sections - 1)])  3.15 us
    pallas_call x1, Pallas kernels, per_device(): call(pack_kernel, [HBM] * 2, shape((peers, 2 * CELL, width)), [pltpu.VMEM...  2.51 us
    pallas_call x1, Pallas kernels, per_device(): call(input_kernel, [VMEM] * 5, shape((peers, CELL, width)), cost=(1000000...  2.08 us
  transfers between devices with their start and end apart: 7, of which 5 were waited for; matrix products, arithmetic and copies ran while one was open for 0% of the time, Pallas kernels for 4%

profile of v4, /device:TPU:192, one launch (start us, length us, event | category | flops | bytes accessed | tf_op | source)
XLA Modules:
  0.0 92.1 jit_solution(1513137364302510176)
XLA Ops:
  0.6 2.5 %shard_map.50 = bf16[32,32,384]{2,1,0:T(8,128)(2,1)} custom-call(bf16[512,384]{1,0:T(8,128)(2,1)} %bitcast.12, bf16[512,384]{1,0:T(8,128)(2,1)} %bitcast.13), custom_call_target="tpu_custom_call" | custom-call | flops 100000000 | bytes 1000000 | tf_op jit(solution)/shard_map/pallas_call | solution.py:254
  3.1 0.0 copy-start
  3.2 10.1 %all-to-all-start = ((bf16[32,32,384]{2,1,0:T(8,128)(2,1)}), bf16[32,32,384]{2,1,0:T(8,128)(2,1)S(1)}, u32[]{:S(2)}, u32[]{:S(2)}) async-start(bf16[32,32,384]{2,1,0:T(8,128)(2,1)} %shard_map.50), calls=%async_computation | async-start | bytes 1572864 | tf_op jit(solution)/shard_map/all_to_all | solution.py:244
  13.3 23.3 %all-to-all-done.in_ref = bf16[32,32,384]{2,1,0:T(8,128)(2,1)S(1)} async-done(((bf16[32,32,384]{2,1,0:T(8,128)(2,1)}), bf16[32,32,384]{2,1,0:T(8,128)(2,1)S(1)}, u32[]{:S(2)}, u32[]{:S(2)}) %all-to-all-start) | async-done | bytes 786464 | tf_op jit(solution)/shard_map/all_to_all | solution.py:244
  36.6 0.0 copy-done
  36.6 6.2 %shard_map.51 = (bf16[512,1152]{1,0:T(8,128)(2,1)S(1)}, bf16[512,384]{1,0:T(8,128)(2,1)S(1)}, f32[512,384]{1,0:T(8,128)S(1)}, f32[512,128]{1,0:T(8,128)S(1)}, f3...) custom-call(s32[1]{0:T(128)} %bitcast.replica_ref, bf16[32,32,384]{2,1,0:T(8,128)(2,1)S(1)} %all-to-all-done.in_ref, ...), custom_call_target="tpu_custom_call" | custom-call | flops 3000000000 | bytes 9000000 | tf_op jit(solution)/shard_map/pallas_call | solution.py:266
  42.8 1.9 %collective-permute-start.1 = (bf16[2,384,384]{2,1,0:T(8,128)(2,1)}, bf16[2,384,384]{2,1,0:T(8,128)(2,1)S(1)}, u32[]{:S(2)}, u32[]{:S(2)}) collective-permute-start(bf16[2,384,384]{2,1,0:T(8,128)(2,1)} %get-tuple-element.17), channel_id=1, source_target_pairs={{0,256},{256,0},{1,257},{257,1},{2,258},{258,2},{3,259},{259,3},{4... | collective-permute-start | bytes 1769480 | tf_op jit(solution)/shard_map/ppermute | solution.py:284
  44.7 2.1 %shard_map.52 = bf16[32,16,384]{2,1,0:T(8,128)(2,1)} custom-call(bf16[512,1152]{1,0:T(8,128)(2,1)S(1)} %get-tuple-element.12.grads_ref, bf16[512,384]{1,0:T(8,128)(2,1)S(1)} %get-tuple-element.13.delta_ref, f32[512,384]{1,0:T(8,128)S(1)} %get-tuple-element.14.standard_ref, f32[512,128]{1,0:T(8,128)S(1)} %get-tuple-element.15.inverse_ref, ...), custom_call_target="tpu_custom_call" | custom-call | flops 1000000000 | bytes 3000000 | tf_op jit(solution)/shard_map/pallas_call | solution.py:285
  46.8 4.8 %all-to-all-start.1 = ((bf16[32,16,384]{2,1,0:T(8,128)(2,1)}), bf16[32,16,384]{2,1,0:T(8,128)(2,1)S(1)}, u32[]{:S(2)}, u32[]{:S(2)}) async-start(bf16[32,16,384]{2,1,0:T(8,128)(2,1)} %shard_map.52), calls=%async_computation.1 | async-start | bytes 786432 | tf_op jit(solution)/shard_map/all_to_all | solution.py:244
  51.5 0.0 collective-permute-done.1.got_ref
  51.5 0.1 shard_map.54
  51.7 3.7 %collective-permute-start.2 = (bf16[2,2,96,384]{3,2,1,0:T(8,128)(2,1)S(1)}, bf16[2,2,96,384]{3,2,1,0:T(8,128)(2,1)S(1)}, u32[]{:S(2)}, u32[]{:S(2)}) collective-permute-start(bf16[2,2,96,384]{3,2,1,0:T(8,128)(2,1)S(1)} %get-tuple-element.19), channel_id=1, source_target_pairs={{0,8},{1,9},{2,10},{3,11},{4,12},{5,13},{6,14},{7,15},{8,0},{9,1},... | collective-permute-start | bytes 884744 | tf_op jit(solution)/shard_map/ppermute | solution.py:296
  55.4 11.0 %collective-permute-done.2.got_ref = bf16[2,2,96,384]{3,2,1,0:T(8,128)(2,1)S(1)} collective-permute-done((bf16[2,2,96,384]{3,2,1,0:T(8,128)(2,1)S(1)}, bf16[2,2,96,384]{3,2,1,0:T(8,128)(2,1)S(1)}, u32[]{:S(2)}, u32[]{:S(2)}) %collective-permute-start.2) | collective-permute-done | bytes 294944 | tf_op jit(solution)/shard_map/ppermute | solution.py:296
  66.4 0.1 shard_map.55
  66.5 4.1 %collective-permute-start.3 = (bf16[2,96,384]{2,1,0:T(8,128)(2,1)S(1)}, bf16[2,96,384]{2,1,0:T(8,128)(2,1)S(1)}, u32[]{:S(2)}, u32[]{:S(2)}) collective-permute-start(bf16[2,96,384]{2,1,0:T(8,128)(2,1)S(1)} %get-tuple-element.21), channel_id=1, source_target_pairs={{0,24},{1,25},{2,26},{3,27},{4,28},{5,29},{6,30},{7,31},{8,16},{9,... | collective-permute-start | bytes 442376 | tf_op jit(solution)/shard_map/ppermute | solution.py:296
  70.6 0.0 all-to-all-done.1.in_ref
  70.6 0.3 shard_map.53
  70.9 1.9 %collective-permute-start = (bf16[512,384]{1,0:T(8,128)(2,1)S(1)}, bf16[512,384]{1,0:T(8,128)(2,1)S(1)}, u32[]{:S(2)}, u32[]{:S(2)}) collective-permute-start(bf16[512,384]{1,0:T(8,128)(2,1)S(1)} %shard_map.53), channel_id=1, source_target_pairs={{32,0},{64,32},{96,64},{128,96},{160,128},{192,160},{224,192},{33,... | collective-permute-start | bytes 1179656 | tf_op jit(solution)/shard_map/ppermute | solution.py:311
  72.8 2.3 %collective-permute-done.3.got_ref = bf16[2,96,384]{2,1,0:T(8,128)(2,1)S(1)} collective-permute-done((bf16[2,96,384]{2,1,0:T(8,128)(2,1)S(1)}, bf16[2,96,384]{2,1,0:T(8,128)(2,1)S(1)}, u32[]{:S(2)}, u32[]{:S(2)}) %collective-permute-start.3) | collective-permute-done | bytes 147488 | tf_op jit(solution)/shard_map/ppermute | solution.py:296
  75.2 0.9 shard_map.56
  76.1 5.4 %all-to-all-start.2 = ((bf16[8,24,384]{2,1,0:T(8,128)(2,1)}), bf16[8,24,384]{2,1,0:T(8,128)(2,1)S(1)}, u32[]{:S(2)}, u32[]{:S(2)}) async-start(bf16[8,24,384]{2,1,0:T(8,128)(2,1)} %shard_map.56), calls=%async_computation.2 | async-start | bytes 294912 | tf_op jit(solution)/shard_map/all_to_all | solution.py:244
  81.5 3.1 %collective-permute-done = bf16[512,384]{1,0:T(8,128)(2,1)S(1)} collective-permute-done((bf16[512,384]{1,0:T(8,128)(2,1)S(1)}, bf16[512,384]{1,0:T(8,128)(2,1)S(1)}, u32[]{:S(2)}, u32[]{:S(2)}) %collective-permute-start) | collective-permute-done | bytes 393248 | tf_op jit(solution)/shard_map/ppermute | solution.py:311
  84.6 6.1 %all-to-all-done.2.in_ref = bf16[8,24,384]{2,1,0:T(8,128)(2,1)S(1)} async-done(((bf16[8,24,384]{2,1,0:T(8,128)(2,1)}), bf16[8,24,384]{2,1,0:T(8,128)(2,1)S(1)}, u32[]{:S(2)}, u32[]{:S(2)}) %all-to-all-start.2) | async-done | bytes 147488 | tf_op jit(solution)/shard_map/all_to_all | solution.py:244
  90.7 0.6 shard_map.57
  91.4 0.7 copy.6
Async XLA Ops:
  3.1 33.5 %copy-start = (bf16[1,4,384,384]{3,2,1,0:T(8,128)(2,1)S(1)}, bf16[1,4,384,384]{3,2,1,0:T(8,128)(2,1)}, u32[]{:S(2)}) copy-start(bf16[1,4,384,384]{3,2,1,0:T(8,128)(2,1)} %param.5) | copy-start | bytes 3538948
  3.2 33.5 %all-to-all-start = ((bf16[32,32,384]{2,1,0:T(8,128)(2,1)}), bf16[32,32,384]{2,1,0:T(8,128)(2,1)S(1)}, u32[]{:S(2)}, u32[]{:S(2)}) async-start(bf16[32,32,384]{2,1,0:T(8,128)(2,1)} %shard_map.50), calls=%async_computation | async-start | bytes 1572864 | tf_op jit(solution)/shard_map/all_to_all | solution.py:244
  42.8 8.8 %collective-permute-start.1 = (bf16[2,384,384]{2,1,0:T(8,128)(2,1)}, bf16[2,384,384]{2,1,0:T(8,128)(2,1)S(1)}, u32[]{:S(2)}, u32[]{:S(2)}) collective-permute-start(bf16[2,384,384]{2,1,0:T(8,128)(2,1)} %get-tuple-element.17), channel_id=1, source_target_pairs={{0,256},{256,0},{1,257},{257,1},{2,258},{258,2},{3,259},{259,3},{4... | collective-permute-start | bytes 1769480 | tf_op jit(solution)/shard_map/ppermute | solution.py:284
  46.8 23.8 %all-to-all-start.1 = ((bf16[32,16,384]{2,1,0:T(8,128)(2,1)}), bf16[32,16,384]{2,1,0:T(8,128)(2,1)S(1)}, u32[]{:S(2)}, u32[]{:S(2)}) async-start(bf16[32,16,384]{2,1,0:T(8,128)(2,1)} %shard_map.52), calls=%async_computation.1 | async-start | bytes 786432 | tf_op jit(solution)/shard_map/all_to_all | solution.py:244
  51.7 14.7 %collective-permute-start.2 = (bf16[2,2,96,384]{3,2,1,0:T(8,128)(2,1)S(1)}, bf16[2,2,96,384]{3,2,1,0:T(8,128)(2,1)S(1)}, u32[]{:S(2)}, u32[]{:S(2)}) collective-permute-start(bf16[2,2,96,384]{3,2,1,0:T(8,128)(2,1)S(1)} %get-tuple-element.19), channel_id=1, source_target_pairs={{0,8},{1,9},{2,10},{3,11},{4,12},{5,13},{6,14},{7,15},{8,0},{9,1},... | collective-permute-start | bytes 884744 | tf_op jit(solution)/shard_map/ppermute | solution.py:296
  66.5 8.7 %collective-permute-start.3 = (bf16[2,96,384]{2,1,0:T(8,128)(2,1)S(1)}, bf16[2,96,384]{2,1,0:T(8,128)(2,1)S(1)}, u32[]{:S(2)}, u32[]{:S(2)}) collective-permute-start(bf16[2,96,384]{2,1,0:T(8,128)(2,1)S(1)} %get-tuple-element.21), channel_id=1, source_target_pairs={{0,24},{1,25},{2,26},{3,27},{4,28},{5,29},{6,30},{7,31},{8,16},{9,... | collective-permute-start | bytes 442376 | tf_op jit(solution)/shard_map/ppermute | solution.py:296
  70.9 13.7 %collective-permute-start = (bf16[512,384]{1,0:T(8,128)(2,1)S(1)}, bf16[512,384]{1,0:T(8,128)(2,1)S(1)}, u32[]{:S(2)}, u32[]{:S(2)}) collective-permute-start(bf16[512,384]{1,0:T(8,128)(2,1)S(1)} %shard_map.53), channel_id=1, source_target_pairs={{32,0},{64,32},{96,64},{128,96},{160,128},{192,160},{224,192},{33,... | collective-permute-start | bytes 1179656 | tf_op jit(solution)/shard_map/ppermute | solution.py:311
  76.1 14.6 %all-to-all-start.2 = ((bf16[8,24,384]{2,1,0:T(8,128)(2,1)}), bf16[8,24,384]{2,1,0:T(8,128)(2,1)S(1)}, u32[]{:S(2)}, u32[]{:S(2)}) async-start(bf16[8,24,384]{2,1,0:T(8,128)(2,1)} %shard_map.56), calls=%async_computation.2 | async-start | bytes 294912 | tf_op jit(solution)/shard_map/all_to_all | solution.py:244

commit v5 on v3

--- a/solution.py
+++ b/solution.py
@@ -13,10 +13,12 @@
 LANES = 128
 ROWS = 4
 COLS = 4
+HALF = COLS // 2
 CELL = ROWS * COLS
 GROUP = 16
 BLOCK = GROUP * CELL
 NX = 4
+NY = 8
 PAD = 8
 VMEM = pl.BlockSpec(memory_space=pltpu.VMEM)
 HBM = pl.BlockSpec(memory_space=pltpu.HBM)
@@ -28,8 +30,8 @@
 
 
 def selection(size, source_of):
-    out = lax.broadcasted_iota(jnp.int32, (size, size), 0)
-    source = lax.broadcasted_iota(jnp.int32, (size, size), 1)
+    out = lax.broadcasted_iota(jnp.int32, size, 0)
+    source = lax.broadcasted_iota(jnp.int32, size, 1)
     return jnp.where(source_of(out) == source, 1.0, 0.0).astype(BF16)
 
 
@@ -44,7 +46,7 @@
     ]
     for copy in copies:
         copy.start()
-    order = selection(BLOCK, lambda o: ((o >> 2) & 3) * 64 + (o >> 4) * 4 + (o & 3))
+    order = selection((BLOCK, BLOCK), lambda o: ((o >> 2) & 3) * 64 + (o >> 4) * 4 + (o & 3))
     groups = out_ref.shape[0] // GROUP
     residues = act_ref.shape[0] // ROWS
     span = GROUP * COLS
@@ -57,31 +59,23 @@
             out_ref[g * GROUP : (g + 1) * GROUP, slot * CELL : (slot + 1) * CELL] = moved
 
 
-def attend_kernel(
-    replica_ref,
-    in_ref,
-    weight_ref,
-    grads_ref,
-    delta_ref,
-    standard_ref,
-    inverse_ref,
-    keep_ref,
-    give_ref,
-    normed_ref,
-    attn_ref,
-    proj_ref,
-):
-    peers = in_ref.shape[0]
+def attend(first, in_ref, weight_ref, joint, refs, scratch):
+    back_ref, normed_ref, delta_ref, grads_ref, attn_ref = refs
+    standard_ref, proj_ref = scratch
+    peers, _, width = in_ref.shape
     groups = peers // GROUP
-    width = in_ref.shape[2]
     seqs = peers * ROWS
     span = GROUP * ROWS
-    order = selection(BLOCK, lambda o: ((o >> 2) & 15) * 16 + (o & 3) * 4 + (o >> 6))
+
+    def source_of(o):
+        return ((o >> 2) & 15) * CELL + (o & 3) * COLS + (o >> 6) + first
+
+    order = selection((HALF * span, BLOCK), source_of)
     for g in range(groups):
         peers_of = slice(g * GROUP, (g + 1) * GROUP)
         acts = dot(order, in_ref[peers_of, :CELL].reshape(BLOCK, width))
         outs = reorder(order, in_ref[peers_of, CELL : 2 * CELL].reshape(BLOCK, width))
-        for j in range(COLS):
+        for j in range(HALF):
             to = slice(j * seqs + g * span, j * seqs + (g + 1) * span)
             standard_ref[to] = acts[j * span : (j + 1) * span]
             delta_ref[to] = outs[j * span : (j + 1) * span]
@@ -91,10 +85,8 @@
     inverse = lax.rsqrt(jnp.mean(centred * centred, axis=-1, keepdims=True) + EPS)
     standard = centred * inverse
     standard_ref[...] = standard
-    inverse_ref[...] = jnp.broadcast_to(inverse, inverse_ref.shape)
     normed = standard.astype(BF16)
     normed_ref[...] = normed
-    joint = jnp.concatenate([weight_ref[n] for n in range(3)], axis=1)
     proj_ref[:, : 3 * width] = dot(normed, joint).astype(BF16)
     proj_ref[:, 3 * width :] = dot(delta_ref[...], weight_ref[3]).astype(BF16)
 
@@ -140,72 +132,125 @@
             grads_ref[here, lanes[2]] = joined(dot(soft, delta)).astype(BF16)
         return carry
 
-    lax.fori_loop(0, COLS, column, 0)
-
-    first = replica_ref[0] == 0
-    term = dot(normed_ref[...], grads_ref[...], ((0,), (0,)))
-    terms = [term[:, n * width : (n + 1) * width] for n in range(3)]
-    terms.append(dot(delta_ref[...], attn_ref[...], ((0,), (0,))))
-    for m in range(2):
-        keep_ref[m] = jnp.where(first, terms[m], terms[m + 2])
-        give_ref[m] = jnp.where(first, terms[m + 2], terms[m]).astype(BF16)
-
-
-def input_kernel(grads_ref, delta_ref, standard_ref, inverse_ref, weight_ref, back_ref):
-    groups = back_ref.shape[0] // GROUP
-    tokens, width = delta_ref.shape
-    seqs = tokens // COLS
-    span = GROUP * ROWS
-    joint = jnp.concatenate([weight_ref[n] for n in range(3)], axis=1)
+    lax.fori_loop(0, HALF, column, 0)
+
     grad_in = dot(grads_ref[...], joint, ((1,), (1,)))
     standard = standard_ref[...]
     grad_mean = jnp.mean(grad_in, axis=-1, keepdims=True)
     grad_proj = jnp.mean(grad_in * standard, axis=-1, keepdims=True)
-    branch = inverse_ref[:, :1] * (grad_in - grad_mean - standard * grad_proj)
+    branch = inverse * (grad_in - grad_mean - standard * grad_proj)
     branch = branch.astype(BF16).astype(F32)
     input_grad = (delta_ref[...].astype(F32) + branch).astype(BF16)
-    order = selection(BLOCK, lambda o: (o & 3) * 64 + (o >> 4) * 4 + ((o >> 2) & 3))
+
+    def back_from(o):
+        return (o & 1) * span + (o >> 3) * ROWS + ((o >> 1) & 3)
+
+    order = selection((HALF * span, HALF * span), back_from)
     for g in range(groups):
         rows = jnp.concatenate(
-            [input_grad[j * seqs + g * span : j * seqs + (g + 1) * span] for j in range(COLS)]
+            [input_grad[j * seqs + g * span : j * seqs + (g + 1) * span] for j in range(HALF)]
         )
-        back_ref[g * GROUP : (g + 1) * GROUP] = reorder(order, rows).reshape(GROUP, CELL, width)
-
-
-def spread_kernel(keep_ref, got_ref, out_ref):
-    quarters, held, width = out_ref.shape
-    peers = held // (2 * (width // 128))
+        moved = reorder(order, rows).reshape(GROUP, CELL // 2, width)
+        back_ref[g * GROUP : (g + 1) * GROUP] = moved
+
+
+def early_kernel(in_ref, weight_ref, *refs):
+    joint = jnp.concatenate([weight_ref[n] for n in range(3)], axis=1)
+    attend(0, in_ref, weight_ref, joint, refs[:5], refs[5:])
+
+
+def late_kernel(
+    replica_ref,
+    in_ref,
+    weight_ref,
+    early_normed_ref,
+    early_delta_ref,
+    early_grads_ref,
+    early_attn_ref,
+    back_ref,
+    keep_ref,
+    give_ref,
+    normed_ref,
+    delta_ref,
+    grads_ref,
+    attn_ref,
+    standard_ref,
+    proj_ref,
+    terms_ref,
+):
+    joint = jnp.concatenate([weight_ref[n] for n in range(3)], axis=1)
+    refs = (back_ref, normed_ref, delta_ref, grads_ref, attn_ref)
+    attend(HALF, in_ref, weight_ref, joint, refs, (standard_ref, proj_ref))
+    width = in_ref.shape[2]
+    down = ((0,), (0,))
+    first = replica_ref[0] == 0
+    term = dot(early_normed_ref[...], early_grads_ref[...], down)
+    term += dot(normed_ref[...], grads_ref[...], down)
+    terms = [term[:, n * width : (n + 1) * width] for n in range(3)]
+    term = dot(early_delta_ref[...], early_attn_ref[...], down)
+    terms.append(term + dot(delta_ref[...], attn_ref[...], down))
+    tiles = [slice(n * LANES, (n + 1) * LANES) for n in range(width // LANES)]
+    for m in range(2):
+        kept = jnp.where(first, terms[m], terms[m + 2])
+        given = jnp.where(first, terms[m + 2], terms[m])
+        for n, lanes in enumerate(tiles):
+            terms_ref[m, n] = kept[:, lanes]
+            terms_ref[2 + m, n] = given[:, lanes]
+    peers = in_ref.shape[0]
     part = width // peers
-    piece = part // quarters
-    block = 8 * part
-    cell = 2 * piece
+    piece = part // NX
+    for q in range(NX):
+        for u in range(piece):
+            for m in range(2):
+                to = slice((2 * u + m) * peers, (2 * u + m + 1) * peers)
+                rows = pl.ds(q * piece + u, peers, stride=part)
+                for n, lanes in enumerate(tiles):
+                    keep_ref[q, to, lanes] = terms_ref[m, n, rows]
+                    give_ref[q, to, lanes] = terms_ref[2 + m, n, rows].astype(BF16)
+
+
+def beside(x):
+    return x + 1 - 2 * lax.rem(x, 2)
+
+
+def across(x):
+    return NX - 1 - x
+
+
+def spread_kernel(place_ref, keep_ref, got_ref, hold_ref, beside_ref, across_ref):
+    x = lax.div(place_ref[0], NY)
+    size = beside_ref.shape[1]
+    for stream, (send_ref, near, far) in enumerate(
+        ((beside_ref, beside, across), (across_ref, across, beside))
+    ):
+        rows = slice(stream * size, (stream + 1) * size)
+        target = near(x)
+        for slot, (stays, leaves) in enumerate(((x, target), (far(x), far(target)))):
+            hold_ref[stream, slot] = keep_ref[stays, rows] + got_ref[stays, rows].astype(F32)
+            total = keep_ref[leaves, rows] + got_ref[leaves, rows].astype(F32)
+            send_ref[slot] = total.astype(BF16)
+
+
+def halve_kernel(hold_ref, beside_ref, across_ref, own_ref, send_across_ref, send_beside_ref):
+    for stream, (got_ref, send_ref) in enumerate(
+        ((beside_ref, send_across_ref), (across_ref, send_beside_ref))
+    ):
+        own_ref[stream] = hold_ref[stream, 0] + got_ref[0].astype(F32)
+        send_ref[...] = (hold_ref[stream, 1] + got_ref[1].astype(F32)).astype(BF16)
+
+
+def leave_kernel(own_ref, across_ref, beside_ref, early_ref, late_ref, out_ref):
+    peers, half, width = early_ref.shape
+    out_ref[:, :half] = early_ref[...]
+    out_ref[:, half:CELL] = late_ref[...]
+    got = (across_ref[...].astype(F32), beside_ref[...].astype(F32))
+    total = jnp.concatenate([(own_ref[n] + got[n]).astype(BF16) for n in range(2)])
+    cell = total.shape[0] // peers
 
     def source_of(o):
-        quarter = o // (8 * cell)
-        rest = o - quarter * (8 * cell)
-        device = rest // cell
-        inside = rest - device * cell
-        return (inside & 1) * block + device * part + quarter * piece + (inside >> 1)
-
-    order = selection(2 * block, source_of)
-    for g in range(peers // 8):
-        here = slice(g * block, (g + 1) * block)
-        rows = [(keep_ref[m, here] + got_ref[m, here].astype(F32)).astype(BF16) for m in range(2)]
-        moved = reorder(order, jnp.concatenate(rows))
-        for q in range(quarters):
-            to = slice(g * 8 * cell, (g + 1) * 8 * cell)
-            out_ref[q, to] = moved[q * 8 * cell : (q + 1) * 8 * cell]
-
-
-def leave_kernel(parts_ref, back_ref, out_ref):
-    peers, _, width = back_ref.shape
-    out_ref[:, :CELL] = back_ref[...]
-    total = jnp.sum(parts_ref[...].astype(F32), axis=0).astype(BF16)
-    cell = total.shape[0] // peers
-    out = lax.broadcasted_iota(jnp.int32, (peers * PAD, peers * cell), 0)
-    source = lax.broadcasted_iota(jnp.int32, (peers * PAD, peers * cell), 1)
-    fits = jnp.logical_and((out >> 3) * cell + (out & 7) == source, (out & 7) < cell)
-    order = jnp.where(fits, 1.0, 0.0).astype(BF16)
+        return jnp.where((o & 7) < cell, (o & 7) * peers + (o >> 3), -1)
+
+    order = selection((peers * PAD, peers * cell), source_of)
     out_ref[:, CELL:] = reorder(order, total).reshape(peers, PAD, width)
 
 
@@ -214,7 +259,11 @@
     groups = peers // GROUP
     residues = peers * COLS
     span = GROUP * COLS
-    order = selection(BLOCK, lambda o: ((o >> 2) & 15) * 16 + (o >> 6) * 4 + (o & 3))
+
+    def source_of(o):
+        return ((o >> 2) & 15) * CELL + ((o >> 1) & 1) * 8 + (o >> 6) * HALF + (o & 1)
+
+    order = selection((BLOCK, BLOCK), source_of)
     for g in range(groups):
         rows = in_ref[g * GROUP : (g + 1) * GROUP, :CELL].reshape(BLOCK, width)
         moved = reorder(order, rows)
@@ -271,38 +320,69 @@
     arrived = exchange(packed)
     weights = layer_weights[0]
     replica = lax.axis_index("dp").astype(jnp.int32).reshape(1)
-    grads, delta, standard, inverse, keep, give = call(
-        attend_kernel,
+    rows_held = tokens // 2
+    back_shape = shape((peers, CELL // 2, width))
+    held = [
+        shape((rows_held, width)),
+        shape((rows_held, width)),
+        shape((rows_held, 3 * width)),
+        shape((rows_held, width)),
+    ]
+    scratch = [pltpu.VMEM((rows_held, width), F32), pltpu.VMEM((rows_held, 4 * width), BF16)]
+    cost = (2e9, 6e6)
+    early, *kept = call(early_kernel, [VMEM] * 2, (back_shape, *held), scratch, cost)(
+        arrived, weights
+    )
+    sections = lax.axis_size("section")
+
+    def along(array):
+        return lax.ppermute(array, "section", [(i + 1, i) for i in range(sections - 1)])
+
+    early = along(early)
+    terms_shape = (NX, 2 * width // NX, width)
+    late, keep, give = call(
+        late_kernel,
+        [SMEM] + [VMEM] * 6,
+        (back_shape, shape(terms_shape, F32), shape(terms_shape)),
+        [
+            *(pltpu.VMEM(one.shape, BF16) for one in held),
+            *scratch,
+            pltpu.VMEM((4, width // LANES, width, LANES), F32),
+        ],
+        cost,
+    )(replica, arrived, weights, *kept)
+    got = lax.ppermute(give, "dp", [(0, 1), (1, 0)])
+    late = along(late)
+    place = lax.axis_index("mp").astype(jnp.int32).reshape(1)
+    size = width // NX
+
+    def over_x(array, partner_of):
+        pairs = [(q * NY + y, partner_of(q) * NY + y) for q in range(NX) for y in range(NY)]
+        return lax.ppermute(array, "mp", pairs)
+
+    def beside_of(q):
+        return q ^ 1
+
+    def across_of(q):
+        return NX - 1 - q
+
+    hold, near, far = call(
+        spread_kernel,
         [SMEM] + [VMEM] * 2,
-        (
-            shape((tokens, 3 * width)),
-            shape((tokens, width)),
-            shape((tokens, width), F32),
-            shape((tokens, LANES), F32),
-            shape((2, width, width), F32),
-            shape((2, width, width)),
-        ),
-        [
-            pltpu.VMEM((tokens, width), BF16),
-            pltpu.VMEM((tokens, width), BF16),
-            pltpu.VMEM((tokens, 4 * width), BF16),
-        ],
-        cost=(3e9, 9e6),
-    )(replica, arrived, weights)
-    got = lax.ppermute(give, "dp", [(0, 1), (1, 0)])
-    back = call(input_kernel, [VMEM] * 5, shape((peers, CELL, width)), cost=(1e9, 3e6))(
-        grads, delta, standard, inverse, weights
-    )
-    keep, back = lax.optimization_barrier((keep, back))
-    sections = lax.axis_size("section")
-    back = lax.ppermute(back, "section", [(i + 1, i) for i in range(sections - 1)])
-    spread = call(
-        spread_kernel, [VMEM] * 2, shape((NX, 2 * width // NX, width)), cost=(1e9, 3e6)
-    )(keep, got)
-    ny = peers // NX
-    groups = [[x * ny + y for x in range(NX)] for y in range(ny)]
-    parts = exchange(spread, groups)
-    leaving = call(leave_kernel, [VMEM] * 2, shape((peers, CELL + PAD, width)))(parts, back)
+        (shape((2, 2, size, width), F32), *[shape((2, size, width))] * 2),
+    )(place, keep, got)
+    near = over_x(near, beside_of)
+    far = over_x(far, across_of)
+    own, far, near = call(
+        halve_kernel,
+        [VMEM] * 3,
+        (shape((2, size, width), F32), *[shape((size, width))] * 2),
+    )(hold, near, far)
+    far = over_x(far, across_of)
+    near = over_x(near, beside_of)
+    leaving = call(leave_kernel, [VMEM] * 5, shape((peers, CELL + PAD, width)))(
+        own, far, near, early, late
+    )
     landed = exchange(leaving)
     received, weight_grads = call(
         final_kernel, [VMEM], (shape((tokens, width)), shape((part, 2, width), F32))

time: 92.2 us -> 94.5 us (1.025)
  starting transfers between devices: 17.6 us -> 27.2 us
  waiting for transfers between devices: 36.8 us -> 31.2 us
  blocking collectives: 24.9 us -> 22.8 us
    ppermute x1 -> x6, starting transfers between devices: 1.92 us -> 14.9 us  [the longest x4 11.1 us: over_x(): return lax.ppermute(array, 'mp', pairs)]
    ppermute x1 -> x6, waiting for transfers between devices: 13 us -> 5.82 us  [the longest x2 3.65 us: along(): lax.ppermute(array, 'section', [(i + 1, i) for i in range(sections - 1)])]
    all_to_all x2 -> x1, starting transfers between devices: 13.8 us -> 10.3 us  [exchange(): lax.all_to_all(array, 'mp', split_axis=0, concat_axis=0, axis_index_group...]
    all_to_all x1, blocking collectives: 24.9 us -> 22.8 us  [exchange(): lax.all_to_all(array, 'mp', split_axis=0, concat_axis=0, axis_index_group...]
    ppermute x1, waiting for transfers between devices: 0.63 us -> 2.18 us  [per_device(): got = lax.ppermute(give, 'dp', [(0, 1), (1, 0)])]
    pallas_call x4 -> x5, Pallas kernels: 8.3 us -> 8.65 us  [the longest x1 4.97 us: per_device(): call(late_kernel, [SMEM] + [VMEM] * 6, (back_shape, shape(terms_shape, F3...]
    all_to_all x2 -> x1, waiting for transfers between devices: 23.2 us -> 23.2 us  [exchange(): lax.all_to_all(array, 'mp', split_axis=0, concat_axis=0, axis_index_group...]
  transfers between devices with their start and end apart: 4 -> 8, of which waited for: 3 -> 6; matrix products, arithmetic and copies ran while one was open for 0% -> 0% of each run, Pallas kernels for 1% -> 0%
where the time goes in v5:
time: 94.5 us; the launch traced here: 94.1 us
  waiting for transfers between devices  31.2 us (33%)
  starting transfers between devices  27.2 us (29%)
  blocking collectives  22.8 us (24%)
  Pallas kernels  12.2 us (13%)
    all_to_all x1, waiting for transfers between devices, exchange(): lax.all_to_all(array, 'mp', split_axis=0, concat_axis=0, axis_index_group...  23.2 us
    all_to_all x1, blocking collectives, exchange(): lax.all_to_all(array, 'mp', split_axis=0, concat_axis=0, axis_index_group...  22.8 us
    ppermute x4, starting transfers between devices, over_x(): return lax.ppermute(array, 'mp', pairs)  11.1 us
    all_to_all x1, starting transfers between devices, exchange(): lax.all_to_all(array, 'mp', split_axis=0, concat_axis=0, axis_index_group...  10.3 us
    pallas_call x1, Pallas kernels, per_device(): call(late_kernel, [SMEM] + [VMEM] * 6, (back_shape, shape(terms_shape, F3...  4.97 us
    ppermute x2, starting transfers between devices, along(): lax.ppermute(array, 'section', [(i + 1, i) for i in range(sections - 1)])  3.84 us
    ppermute x2, waiting for transfers between devices, along(): lax.ppermute(array, 'section', [(i + 1, i) for i in range(sections - 1)])  3.65 us
    pallas_call x1, Pallas kernels, per_device(): call(early_kernel, [VMEM] * 2, (back_shape, *held), scratch, cost)  3.25 us
  transfers between devices with their start and end apart: 8, of which 6 were waited for; matrix products, arithmetic and copies ran while one was open for 0% of the time, Pallas kernels for 0%

profile of v5, /device:TPU:200, one launch (start us, length us, event | category | flops | bytes accessed | tf_op | source)
XLA Modules:
  0.0 94.1 jit_solution(8130588248634322671)
XLA Ops:
  0.6 2.5 %shard_map.50 = bf16[32,32,384]{2,1,0:T(8,128)(2,1)} custom-call(bf16[512,384]{1,0:T(8,128)(2,1)} %bitcast.11, bf16[512,384]{1,0:T(8,128)(2,1)} %bitcast.12), custom_call_target="tpu_custom_call" | custom-call | flops 100000000 | bytes 1000000 | tf_op jit(solution)/shard_map/pallas_call | solution.py:311
  3.2 0.0 copy-start
  3.2 10.3 %all-to-all-start = ((bf16[32,32,384]{2,1,0:T(8,128)(2,1)}), bf16[32,32,384]{2,1,0:T(8,128)(2,1)S(1)}, u32[]{:S(2)}, u32[]{:S(2)}) async-start(bf16[32,32,384]{2,1,0:T(8,128)(2,1)} %shard_map.50), calls=%async_computation | async-start | bytes 1572864 | tf_op jit(solution)/shard_map/all_to_all | solution.py:301
  13.5 23.2 %all-to-all-done.in_ref = bf16[32,32,384]{2,1,0:T(8,128)(2,1)S(1)} async-done(((bf16[32,32,384]{2,1,0:T(8,128)(2,1)}), bf16[32,32,384]{2,1,0:T(8,128)(2,1)S(1)}, u32[]{:S(2)}, u32[]{:S(2)}) %all-to-all-start) | async-done | bytes 786464 | tf_op jit(solution)/shard_map/all_to_all | solution.py:301
  36.7 0.0 copy-done
  36.7 3.3 %shard_map.51 = (bf16[32,8,384]{2,1,0:T(8,128)(2,1)S(1)}, bf16[256,384]{1,0:T(8,128)(2,1)S(1)}, bf16[256,384]{1,0:T(8,128)(2,1)S(1)}, bf16[256,1152]{1,0:T(8,128)(2,1)S(1)}, bf16[256,384]{1,0:T(8,128)(2,1)S(1)}) custom-call(bf16[32,32,384]{2,1,0:T(8,128)(2,1)S(1)} %all-to-all-done.in_ref, bf16[4,384,384]{2,1,0:T(8,128)(2,1)S(1)} %bitcast.9), custom_call_target="tpu_custom_call" | custom-call | flops 2000000000 | bytes 6000000 | tf_op jit(solution)/shard_map/pallas_call | solution.py:333
  39.9 5.0 %shard_map.52 = (bf16[32,8,384]{2,1,0:T(8,128)(2,1)S(1)}, f32[4,192,384]{2,1,0:T(8,128)S(1)}, bf16[4,192,384]{2,1,0:T(8,128)(2,1)}) custom-call(s32[1]{0:T(128)} %bitcast.1.replica_ref, bf16[32,32,384]{2,1,0:T(8,128)(2,1)S(1)} %all-to-all-done.in_ref, bf16[4,384,384]{2,1,0:T(8,128)(2,1)S(1)} %bitcast.10, ...), custom_call_target="tpu_custom_call" | custom-call | flops 2000000000 | bytes 6000000 | tf_op jit(solution)/shard_map/pallas_call | solution.py:343
  44.9 1.9 %collective-permute-start = (bf16[4,192,384]{2,1,0:T(8,128)(2,1)}, bf16[4,192,384]{2,1,0:T(8,128)(2,1)S(1)}, u32[]{:S(2)}, u32[]{:S(2)}) collective-permute-start(bf16[4,192,384]{2,1,0:T(8,128)(2,1)} %get-tuple-element.23), channel_id=1, source_target_pairs={{0,256},{256,0},{1,257},{257,1},{2,258},{258,2},{3,259},{259,3},{4... | collective-permute-start | bytes 1769480 | tf_op jit(solution)/shard_map/ppermute | solution.py:354
  46.8 2.2 %collective-permute-done.got_ref = bf16[4,192,384]{2,1,0:T(8,128)(2,1)S(1)} collective-permute-done((bf16[4,192,384]{2,1,0:T(8,128)(2,1)}, bf16[4,192,384]{2,1,0:T(8,128)(2,1)S(1)}, u32[]{:S(2)}, u32[]{:S(2)}) %collective-permute-start) | collective-permute-done | bytes 589856 | tf_op jit(solution)/shard_map/ppermute | solution.py:354
  49.0 0.1 shard_map.53
  49.1 2.5 %collective-permute-start.1 = (bf16[2,96,384]{2,1,0:T(8,128)(2,1)S(1)}, bf16[2,96,384]{2,1,0:T(8,128)(2,1)S(1)}, u32[]{:S(2)}, u32[]{:S(2)}) collective-permute-start(bf16[2,96,384]{2,1,0:T(8,128)(2,1)S(1)} %get-tuple-element.25), channel_id=1, source_target_pairs={{0,8},{1,9},{2,10},{3,11},{4,12},{5,13},{6,14},{7,15},{8,0},{9,1},... | collective-permute-start | bytes 442376 | tf_op jit(solution)/shard_map/ppermute | solution.py:361
  51.6 3.3 %collective-permute-start.2 = (bf16[2,96,384]{2,1,0:T(8,128)(2,1)S(1)}, bf16[2,96,384]{2,1,0:T(8,128)(2,1)S(1)}, u32[]{:S(2)}, u32[]{:S(2)}) collective-permute-start(bf16[2,96,384]{2,1,0:T(8,128)(2,1)S(1)} %get-tuple-element.26), channel_id=1, source_target_pairs={{0,24},{1,25},{2,26},{3,27},{4,28},{5,29},{6,30},{7,31},{8,16},{9,... | collective-permute-start | bytes 442376 | tf_op jit(solution)/shard_map/ppermute | solution.py:361
  54.9 1.9 %collective-permute-start.6 = (bf16[32,8,384]{2,1,0:T(8,128)(2,1)S(1)}, bf16[32,8,384]{2,1,0:T(8,128)(2,1)S(1)}, u32[]{:S(2)}, u32[]{:S(2)}) collective-permute-start(bf16[32,8,384]{2,1,0:T(8,128)(2,1)S(1)} %get-tuple-element.31), channel_id=1, source_target_pairs={{32,0},{64,32},{96,64},{128,96},{160,128},{192,160},{224,192},{33,... | collective-permute-start | bytes 589832 | tf_op jit(solution)/shard_map/ppermute | solution.py:339
  56.9 1.9 %collective-permute-start.5 = (bf16[32,8,384]{2,1,0:T(8,128)(2,1)S(1)}, bf16[32,8,384]{2,1,0:T(8,128)(2,1)S(1)}, u32[]{:S(2)}, u32[]{:S(2)}) collective-permute-start(bf16[32,8,384]{2,1,0:T(8,128)(2,1)S(1)} %get-tuple-element.30), channel_id=1, source_target_pairs={{32,0},{64,32},{96,64},{128,96},{160,128},{192,160},{224,192},{33,... | collective-permute-start | bytes 589832 | tf_op jit(solution)/shard_map/ppermute | solution.py:339
  58.8 0.0 collective-permute-done.1.beside_ref
  58.8 1.5 %collective-permute-done.2.across_ref = bf16[2,96,384]{2,1,0:T(8,128)(2,1)S(1)} collective-permute-done((bf16[2,96,384]{2,1,0:T(8,128)(2,1)S(1)}, bf16[2,96,384]{2,1,0:T(8,128)(2,1)S(1)}, u32[]{:S(2)}, u32[]{:S(2)}) %collective-permute-start.2) | collective-permute-done | bytes 147488 | tf_op jit(solution)/shard_map/ppermute | solution.py:361
  60.3 0.1 shard_map.54
  60.4 3.3 %collective-permute-start.3 = (bf16[96,384]{1,0:T(8,128)(2,1)S(1)}, bf16[96,384]{1,0:T(8,128)(2,1)S(1)}, u32[]{:S(2)}, u32[]{:S(2)}) collective-permute-start(bf16[96,384]{1,0:T(8,128)(2,1)S(1)} %get-tuple-element.28), channel_id=1, source_target_pairs={{0,24},{1,25},{2,26},{3,27},{4,28},{5,29},{6,30},{7,31},{8,16},{9,... | collective-permute-start | bytes 221192 | tf_op jit(solution)/shard_map/ppermute | solution.py:361
  63.7 1.9 %collective-permute-start.4 = (bf16[96,384]{1,0:T(8,128)(2,1)S(1)}, bf16[96,384]{1,0:T(8,128)(2,1)S(1)}, u32[]{:S(2)}, u32[]{:S(2)}) collective-permute-start(bf16[96,384]{1,0:T(8,128)(2,1)S(1)} %get-tuple-element.29), channel_id=1, source_target_pairs={{0,8},{1,9},{2,10},{3,11},{4,12},{5,13},{6,14},{7,15},{8,0},{9,1},... | collective-permute-start | bytes 221192 | tf_op jit(solution)/shard_map/ppermute | solution.py:361
  65.6 0.5 collective-permute-done.6.late_ref
  66.2 3.1 %collective-permute-done.5.early_ref = bf16[32,8,384]{2,1,0:T(8,128)(2,1)S(1)} collective-permute-done((bf16[32,8,384]{2,1,0:T(8,128)(2,1)S(1)}, bf16[32,8,384]{2,1,0:T(8,128)(2,1)S(1)}, u32[]{:S(2)}, u32[]{:S(2)}) %collective-permute-start.5) | collective-permute-done | bytes 196640 | tf_op jit(solution)/shard_map/ppermute | solution.py:339
  69.3 0.0 collective-permute-done.3.across_ref
  69.3 0.7 collective-permute-done.4.beside_ref
  70.0 0.3 shard_map.55
  70.2 22.8 %all_to_all.10.in_ref = bf16[32,24,384]{2,1,0:T(8,128)(2,1)S(1)} all-to-all(bf16[32,24,384]{2,1,0:T(8,128)(2,1)S(1)} %shard_map.55), channel_id=1, replica_groups=mesh['dp'=2,'section'=8,'mp'=32] {'mp'}, dimensions={0} | all-to-all | bytes 1179648 | tf_op jit(solution)/shard_map/all_to_all | solution.py:301
  93.0 1.0 %shard_map.56 = (bf16[512,384]{1,0:T(8,128)(2,1)}, f32[12,2,384]{2,1,0:T(2,128)}) custom-call(bf16[32,24,384]{2,1,0:T(8,128)(2,1)S(1)} %all_to_all.10.in_ref), custom_call_target="tpu_custom_call" | custom-call | flops 100000000 | bytes 1000000 | tf_op jit(solution)/shard_map/pallas_call | solution.py:387
Async XLA Ops:
  3.2 33.5 %copy-start = (bf16[1,4,384,384]{3,2,1,0:T(8,128)(2,1)S(1)}, bf16[1,4,384,384]{3,2,1,0:T(8,128)(2,1)}, u32[]{:S(2)}) copy-start(bf16[1,4,384,384]{3,2,1,0:T(8,128)(2,1)} %param.5) | copy-start | bytes 3538948
  3.2 33.5 %all-to-all-start = ((bf16[32,32,384]{2,1,0:T(8,128)(2,1)}), bf16[32,32,384]{2,1,0:T(8,128)(2,1)S(1)}, u32[]{:S(2)}, u32[]{:S(2)}) async-start(bf16[32,32,384]{2,1,0:T(8,128)(2,1)} %shard_map.50), calls=%async_computation | async-start | bytes 1572864 | tf_op jit(solution)/shard_map/all_to_all | solution.py:301
  44.9 4.1 %collective-permute-start = (bf16[4,192,384]{2,1,0:T(8,128)(2,1)}, bf16[4,192,384]{2,1,0:T(8,128)(2,1)S(1)}, u32[]{:S(2)}, u32[]{:S(2)}) collective-permute-start(bf16[4,192,384]{2,1,0:T(8,128)(2,1)} %get-tuple-element.23), channel_id=1, source_target_pairs={{0,256},{256,0},{1,257},{257,1},{2,258},{258,2},{3,259},{259,3},{4... | collective-permute-start | bytes 1769480 | tf_op jit(solution)/shard_map/ppermute | solution.py:354
  49.1 9.7 %collective-permute-start.1 = (bf16[2,96,384]{2,1,0:T(8,128)(2,1)S(1)}, bf16[2,96,384]{2,1,0:T(8,128)(2,1)S(1)}, u32[]{:S(2)}, u32[]{:S(2)}) collective-permute-start(bf16[2,96,384]{2,1,0:T(8,128)(2,1)S(1)} %get-tuple-element.25), channel_id=1, source_target_pairs={{0,8},{1,9},{2,10},{3,11},{4,12},{5,13},{6,14},{7,15},{8,0},{9,1},... | collective-permute-start | bytes 442376 | tf_op jit(solution)/shard_map/ppermute | solution.py:361
  51.6 8.7 %collective-permute-start.2 = (bf16[2,96,384]{2,1,0:T(8,128)(2,1)S(1)}, bf16[2,96,384]{2,1,0:T(8,128)(2,1)S(1)}, u32[]{:S(2)}, u32[]{:S(2)}) collective-permute-start(bf16[2,96,384]{2,1,0:T(8,128)(2,1)S(1)} %get-tuple-element.26), channel_id=1, source_target_pairs={{0,24},{1,25},{2,26},{3,27},{4,28},{5,29},{6,30},{7,31},{8,16},{9,... | collective-permute-start | bytes 442376 | tf_op jit(solution)/shard_map/ppermute | solution.py:361
  54.9 11.2 %collective-permute-start.6 = (bf16[32,8,384]{2,1,0:T(8,128)(2,1)S(1)}, bf16[32,8,384]{2,1,0:T(8,128)(2,1)S(1)}, u32[]{:S(2)}, u32[]{:S(2)}) collective-permute-start(bf16[32,8,384]{2,1,0:T(8,128)(2,1)S(1)} %get-tuple-element.31), channel_id=1, source_target_pairs={{32,0},{64,32},{96,64},{128,96},{160,128},{192,160},{224,192},{33,... | collective-permute-start | bytes 589832 | tf_op jit(solution)/shard_map/ppermute | solution.py:339
  56.9 12.4 %collective-permute-start.5 = (bf16[32,8,384]{2,1,0:T(8,128)(2,1)S(1)}, bf16[32,8,384]{2,1,0:T(8,128)(2,1)S(1)}, u32[]{:S(2)}, u32[]{:S(2)}) collective-permute-start(bf16[32,8,384]{2,1,0:T(8,128)(2,1)S(1)} %get-tuple-element.30), channel_id=1, source_target_pairs={{32,0},{64,32},{96,64},{128,96},{160,128},{192,160},{224,192},{33,... | collective-permute-start | bytes 589832 | tf_op jit(solution)/shard_map/ppermute | solution.py:339
  60.4 8.9 %collective-permute-start.3 = (bf16[96,384]{1,0:T(8,128)(2,1)S(1)}, bf16[96,384]{1,0:T(8,128)(2,1)S(1)}, u32[]{:S(2)}, u32[]{:S(2)}) collective-permute-start(bf16[96,384]{1,0:T(8,128)(2,1)S(1)} %get-tuple-element.28), channel_id=1, source_target_pairs={{0,24},{1,25},{2,26},{3,27},{4,28},{5,29},{6,30},{7,31},{8,16},{9,... | collective-permute-start | bytes 221192 | tf_op jit(solution)/shard_map/ppermute | solution.py:361
  63.7 6.2 %collective-permute-start.4 = (bf16[96,384]{1,0:T(8,128)(2,1)S(1)}, bf16[96,384]{1,0:T(8,128)(2,1)S(1)}, u32[]{:S(2)}, u32[]{:S(2)}) collective-permute-start(bf16[96,384]{1,0:T(8,128)(2,1)S(1)} %get-tuple-element.29), channel_id=1, source_target_pairs={{0,8},{1,9},{2,10},{3,11},{4,12},{5,13},{6,14},{7,15},{8,0},{9,1},... | collective-permute-start | bytes 221192 | tf_op jit(solution)/shard_map/ppermute | solution.py:361

commit v6 on v3

v6 whole, which is shorter than its diff:
```python
import jax
import jax.numpy as jnp
import numpy as np
from jax import lax
from jax.experimental import pallas as pl
from jax.experimental.pallas import tpu as pltpu
from jax.sharding import PartitionSpec as P


HEAD_DIM = 64
EPS = 1e-05
F32 = jnp.float32
BF16 = jnp.bfloat16
LANES = 128
ROWS = 4
COLS = 4
CELL = ROWS * COLS
GROUP = 16
BLOCK = GROUP * CELL
NX = 4
PAD = 8
VMEM = pl.BlockSpec(memory_space=pltpu.VMEM)
SMEM = pl.BlockSpec(memory_space=pltpu.SMEM)


def dot(a, b, dims=((1,), (0,))):
    return lax.dot_general(a, b, (dims, ((), ())), preferred_element_type=F32)


def selection(size, source_of):
    out = lax.broadcasted_iota(jnp.int32, (size, size), 0)
    source = lax.broadcasted_iota(jnp.int32, (size, size), 1)
    return jnp.where(source_of(out) == source, 1.0, 0.0).astype(BF16)


def table(rows, columns, source_of):
    matrix = np.zeros((rows, columns), np.float32)
    for o in range(rows):
        if source_of(o) >= 0:
            matrix[o, source_of(o)] = 1.0
    return jnp.asarray(matrix, BF16)


def reorder(matrix, rows):
    return dot(matrix, rows).astype(BF16)


def pack_kernel(act_ref, grad_ref, out_ref, order_ref):
    @pl.when(pl.program_id(0) == 0)
    def _():
        order_ref[...] = selection(
            BLOCK, lambda o: ((o >> 2) & 3) * 64 + (o >> 4) * 4 + (o & 3)
        )

    for slot, ref in enumerate((act_ref, grad_ref)):
        moved = reorder(order_ref[...], ref[...].reshape(BLOCK, -1)).reshape(GROUP, CELL, -1)
        out_ref[:, slot * CELL : (slot + 1) * CELL] = moved


def attend_kernel(
    replica_ref,
    order_ref,
    in_ref,
    weight_ref,
    grads_ref,
    delta_ref,
    standard_ref,
    inverse_ref,
    keep_ref,
    give_ref,
    normed_ref,
    attn_ref,
    proj_ref,
):
    peers = in_ref.shape[0]
    groups = peers // GROUP
    width = in_ref.shape[2]
    seqs = peers * ROWS
    span = GROUP * ROWS
    order = order_ref[...]
    for g in range(groups):
        peers_of = slice(g * GROUP, (g + 1) * GROUP)
        acts = dot(order, in_ref[peers_of, :CELL].reshape(BLOCK, width))
        outs = reorder(order, in_ref[peers_of, CELL : 2 * CELL].reshape(BLOCK, width))
        for j in range(COLS):
            to = slice(j * seqs + g * span, j * seqs + (g + 1) * span)
            standard_ref[to] = acts[j * span : (j + 1) * span]
            delta_ref[to] = outs[j * span : (j + 1) * span]
    values = standard_ref[...]
    mean_value = jnp.mean(values, axis=-1, keepdims=True)
    centred = values - mean_value
    inverse = lax.rsqrt(jnp.mean(centred * centred, axis=-1, keepdims=True) + EPS)
    standard = centred * inverse
    standard_ref[...] = standard
    inverse_ref[...] = jnp.broadcast_to(inverse, inverse_ref.shape)
    normed = standard.astype(BF16)
    normed_ref[...] = normed
    joint = jnp.concatenate([weight_ref[n] for n in range(3)], axis=1)
    proj_ref[:, : 3 * width] = dot(normed, joint).astype(BF16)
    proj_ref[:, 3 * width :] = dot(delta_ref[...], weight_ref[3]).astype(BF16)

    scaling = HEAD_DIM ** (-0.5)
    low = lax.broadcasted_iota(jnp.int32, (seqs, LANES), 1) < HEAD_DIM

    def apart(pair):
        zero = jnp.zeros_like(pair)
        return jnp.concatenate([jnp.where(low, pair, zero), jnp.where(low, zero, pair)])

    def joined(columns):
        top, bottom = columns[:HEAD_DIM, :seqs], columns[HEAD_DIM:, seqs:]
        return jnp.concatenate([top, bottom]).astype(BF16).T

    def column(j, carry):
        here = pl.ds(pl.multiple_of(j * seqs, seqs), seqs)
        pairs = range(width // LANES)
        loaded = [
            [proj_ref[here, n * width + p * LANES : n * width + (p + 1) * LANES] for n in range(4)]
            for p in pairs
        ]
        split = [(apart(query), apart(delta)) for query, _, _, delta in loaded]
        scores = [dot(loaded[p][1], split[p][0], ((1,), (1,))) * scaling for p in pairs]
        dprobs = [dot(loaded[p][2], split[p][1], ((1,), (1,))) for p in pairs]
        for p in pairs:
            _, key, value, _ = loaded[p]
            queries, deltas = split[p]
            exponent = jnp.exp(scores[p] - jnp.max(scores[p], axis=0, keepdims=True))
            probs = exponent * (1.0 / jnp.sum(exponent, axis=0, keepdims=True))
            column_delta = jnp.sum(probs * dprobs[p], axis=0, keepdims=True)
            soft = probs.astype(BF16)
            dscores = (probs * (dprobs[p] - column_delta)).astype(BF16)
            lanes = [slice(n * width + p * LANES, n * width + (p + 1) * LANES) for n in range(3)]
            attn_ref[here, lanes[0]] = joined(dot(value, soft, ((0,), (0,))))
            grads_ref[here, lanes[0]] = joined(dot(key, dscores, ((0,), (0,))) * scaling)
            grads_ref[here, lanes[1]] = (dot(dscores, queries) * scaling).astype(BF16)
            grads_ref[here, lanes[2]] = dot(soft, deltas).astype(BF16)
        return carry

    lax.fori_loop(0, COLS, column, 0, unroll=4)

    first = replica_ref[0] == 0
    term = dot(normed_ref[...], grads_ref[...], ((0,), (0,)))
    terms = [term[:, n * width : (n + 1) * width] for n in range(3)]
    terms.append(dot(delta_ref[...], attn_ref[...], ((0,), (0,))))
    for m in range(2):
        keep_ref[m] = jnp.where(first, terms[m], terms[m + 2])
        give_ref[m] = jnp.where(first, terms[m + 2], terms[m]).astype(BF16)


def input_kernel(order_ref, grads_ref, delta_ref, standard_ref, inverse_ref, weight_ref, back_ref):
    groups = back_ref.shape[0] // GROUP
    tokens, width = delta_ref.shape
    seqs = tokens // COLS
    span = GROUP * ROWS
    joint = jnp.concatenate([weight_ref[n] for n in range(3)], axis=1)
    grad_in = dot(grads_ref[...], joint, ((1,), (1,)))
    standard = standard_ref[...]
    grad_mean = jnp.mean(grad_in, axis=-1, keepdims=True)
    grad_proj = jnp.mean(grad_in * standard, axis=-1, keepdims=True)
    branch = inverse_ref[:, :1] * (grad_in - grad_mean - standard * grad_proj)
    branch = branch.astype(BF16).astype(F32)
    input_grad = (delta_ref[...].astype(F32) + branch).astype(BF16)
    order = order_ref[...]
    for g in range(groups):
        rows = jnp.concatenate(
            [input_grad[j * seqs + g * span : j * seqs + (g + 1) * span] for j in range(COLS)]
        )
        back_ref[g * GROUP : (g + 1) * GROUP] = reorder(order, rows).reshape(GROUP, CELL, width)


def spread_kernel(order_ref, keep_ref, got_ref, out_ref):
    quarters = out_ref.shape[0]
    block = order_ref.shape[0] // 2
    size = 2 * block // quarters
    for g in range(keep_ref.shape[1] // block):
        here = slice(g * block, (g + 1) * block)
        rows = [(keep_ref[m, here] + got_ref[m, here].astype(F32)).astype(BF16) for m in range(2)]
        moved = reorder(order_ref[...], jnp.concatenate(rows))
        for q in range(quarters):
            out_ref[q, g * size : (g + 1) * size] = moved[q * size : (q + 1) * size]


def leave_kernel(order_ref, parts_ref, back_ref, out_ref):
    peers, _, width = back_ref.shape
    out_ref[:, :CELL] = back_ref[...]
    total = jnp.sum(parts_ref[...].astype(F32), axis=0).astype(BF16)
    out_ref[:, CELL:] = reorder(order_ref[...], total).reshape(peers, PAD, width)


def final_kernel(order_ref, in_ref, received_ref, grads_ref):
    peers, _, width = in_ref.shape
    groups = peers // GROUP
    residues = peers * COLS
    span = GROUP * COLS
    order = order_ref[...]
    for g in range(groups):
        rows = in_ref[g * GROUP : (g + 1) * GROUP, :CELL].reshape(BLOCK, width)
        moved = reorder(order, rows)
        for i in range(ROWS):
            to = slice(i * residues + g * span, i * residues + (g + 1) * span)
            received_ref[to] = moved[i * span : (i + 1) * span]
    parts = in_ref[:, CELL:].astype(F32)
    quarters = NX
    parts = jnp.sum(parts.reshape(quarters, peers // quarters, PAD, width), axis=1)
    piece = grads_ref.shape[0] // quarters
    for q in range(quarters):
        for u in range(piece):
            grads_ref[q * piece + u] = parts[q, 2 * u : 2 * u + 2]


def shape(dims, dtype=BF16):
    return jax.ShapeDtypeStruct(dims, dtype)


def call(kernel, in_specs, out_shape, scratch=(), cost=(1e8, 1e6)):
    return pl.pallas_call(
        kernel,
        in_specs=in_specs,
        out_specs=jax.tree.map(lambda _: VMEM, out_shape),
        out_shape=out_shape,
        scratch_shapes=scratch,
        compiler_params=pltpu.CompilerParams(vmem_limit_bytes=14 * 1024 * 1024),
        cost_estimate=pl.CostEstimate(
            flops=int(cost[0]), bytes_accessed=int(cost[1]), transcendentals=0
        ),
    )


def exchange(array, groups=None):
    return lax.all_to_all(
        array, "mp", split_axis=0, concat_axis=0, axis_index_groups=groups, tiled=True
    )


def per_device(activations, out_grads, layer_weights):
    rows, residues, width = activations.shape[2:]
    peers = lax.axis_size("mp")
    tokens = rows * residues
    part = width // peers
    groups = peers // GROUP
    span = GROUP * COLS
    taken = pl.BlockSpec((rows, 1, span, width), lambda g: (0, g, 0, 0))
    packed = pl.pallas_call(
        pack_kernel,
        grid=(groups,),
        in_specs=[taken] * 2,
        out_specs=pl.BlockSpec((GROUP, 2 * CELL, width), lambda g: (g, 0, 0)),
        out_shape=shape((peers, 2 * CELL, width)),
        scratch_shapes=[pltpu.VMEM((BLOCK, BLOCK), BF16)],
        compiler_params=pltpu.CompilerParams(vmem_limit_bytes=56 * 1024 * 1024),
    )(
        activations.reshape(rows, groups, span, width),
        out_grads.reshape(rows, groups, span, width),
    )
    arrived = exchange(packed)
    weights = layer_weights[0]
    replica = lax.axis_index("dp").astype(jnp.int32).reshape(1)
    grads, delta, standard, inverse, keep, give = call(
        attend_kernel,
        [SMEM] + [VMEM] * 3,
        (
            shape((tokens, 3 * width)),
            shape((tokens, width)),
            shape((tokens, width), F32),
            shape((tokens, LANES), F32),
            shape((2, width, width), F32),
            shape((2, width, width)),
        ),
        [
            pltpu.VMEM((tokens, width), BF16),
            pltpu.VMEM((tokens, width), BF16),
            pltpu.VMEM((tokens, 4 * width), BF16),
        ],
        cost=(3e9, 9e6),
    )(
        replica,
        table(BLOCK, BLOCK, lambda o: ((o >> 2) & 15) * 16 + (o & 3) * 4 + (o >> 6)),
        arrived,
        weights,
    )
    got = lax.ppermute(give, "dp", [(0, 1), (1, 0)])
    order = table(BLOCK, BLOCK, lambda o: (o & 3) * 64 + (o >> 4) * 4 + ((o >> 2) & 3))
    back = call(input_kernel, [VMEM] * 6, shape((peers, CELL, width)), cost=(1e9, 3e6))(
        order, grads, delta, standard, inverse, weights
    )
    keep, back = lax.optimization_barrier((keep, back))
    sections = lax.axis_size("section")
    back = lax.ppermute(back, "section", [(i + 1, i) for i in range(sections - 1)])
    piece = part // NX

    def spread_from(o):
        quarter, rest = divmod(o, 16 * piece)
        device, inside = divmod(rest, 2 * piece)
        return (inside & 1) * 8 * part + device * part + quarter * piece + (inside >> 1)

    spread = call(
        spread_kernel, [VMEM] * 3, shape((NX, 2 * width // NX, width)), cost=(1e9, 3e6)
    )(table(16 * part, 16 * part, spread_from), keep, got)
    ny = peers // NX
    groups = [[x * ny + y for x in range(NX)] for y in range(ny)]
    parts = exchange(spread, groups)
    cell = 2 * piece
    order = table(
        peers * PAD, peers * cell, lambda o: (o >> 3) * cell + (o & 7) if (o & 7) < cell else -1
    )
    leaving = call(leave_kernel, [VMEM] * 3, shape((peers, CELL + PAD, width)))(order, parts, back)
    landed = exchange(leaving)
    received, weight_grads = call(
        final_kernel, [VMEM] * 2, (shape((tokens, width)), shape((part, 2, width), F32))
    )(
        table(BLOCK, BLOCK, lambda o: ((o >> 2) & 15) * 16 + (o >> 6) * 4 + (o & 3)),
        landed,
    )
    return (received.reshape(activations.shape), weight_grads.transpose(1, 0, 2)[None])


def solution(mesh):
    in_specs = (
        P("dp", "section", "mp", None, None),
        P("dp", "section", "mp", None, None),
        P("section", None, None, None),
    )
    out_specs = (P("dp", "section", "mp", None, None), P("section", "dp", "mp", None))

    return jax.shard_map(
        per_device, mesh=mesh, in_specs=in_specs, out_specs=out_specs, check_vma=False
    )
```

time: 92.2 us -> 91.3 us (level)
  Pallas kernels: 11.8 us -> 10.7 us
    pallas_call x6, Pallas kernels: 11.8 us -> 10.7 us  [the longest x1 4.47 us: per_device(): call(attend_kernel, [SMEM] + [VMEM] * 3, (shape((tokens, 3 * width)), sha...]
where the time goes in v6:
time: 91.3 us; the launch traced here: 91 us
  waiting for transfers between devices  36.8 us (40%)
  blocking collectives  24.8 us (27%)
  starting transfers between devices  17.9 us (20%)
  Pallas kernels  10.7 us (12%)
    all_to_all x1, blocking collectives, exchange(): lax.all_to_all(array, 'mp', split_axis=0, concat_axis=0, axis_index_group...  24.8 us
    all_to_all x2, waiting for transfers between devices, exchange(): lax.all_to_all(array, 'mp', split_axis=0, concat_axis=0, axis_index_group...  23.2 us
    all_to_all x2, starting transfers between devices, exchange(): lax.all_to_all(array, 'mp', split_axis=0, concat_axis=0, axis_index_group...  13.9 us
    ppermute x1, waiting for transfers between devices, per_device(): lax.ppermute(back, 'section', [(i + 1, i) for i in range(sections - 1)])  13 us
    pallas_call x1, Pallas kernels, per_device(): call(attend_kernel, [SMEM] + [VMEM] * 3, (shape((tokens, 3 * width)), sha...  4.47 us
    pallas_call x1, Pallas kernels, per_device(): pl.pallas_call(pack_kernel, grid=(groups,), in_specs=[taken] * 2, out_spe...  2.44 us
    ppermute x1, starting transfers between devices, per_device(): lax.ppermute(back, 'section', [(i + 1, i) for i in range(sections - 1)])  2.05 us
    ppermute x1, starting transfers between devices, per_device(): got = lax.ppermute(give, 'dp', [(0, 1), (1, 0)])  1.92 us
  transfers between devices with their start and end apart: 4, of which 3 were waited for; matrix products, arithmetic and copies ran while one was open for 0% of the time, Pallas kernels for 1%

profile of v6, /device:TPU:200, one launch (start us, length us, event | category | flops | bytes accessed | tf_op | source)
XLA Modules:
  0.0 91.0 jit_solution(11183150136025213091)
XLA Ops:
  0.6 2.4 %shard_map.95 = bf16[32,32,384]{2,1,0:T(8,128)(2,1)} custom-call(bf16[4,2,64,384]{3,2,1,0:T(8,128)(2,1)} %bitcast.10, bf16[4,2,64,384]{3,2,1,0:T(8,128)(2,1)} %bitcast.11), custom_call_target="tpu_custom_call" | custom-call | tf_op jit(solution)/shard_map/pallas_call | solution.py:242
  3.1 0.0 copy-start
  3.1 0.0 copy-start.4
  3.1 10.3 %all-to-all-start = ((bf16[32,32,384]{2,1,0:T(8,128)(2,1)}), bf16[32,32,384]{2,1,0:T(8,128)(2,1)S(1)}, u32[]{:S(2)}, u32[]{:S(2)}) async-start(bf16[32,32,384]{2,1,0:T(8,128)(2,1)} %shard_map.95), calls=%async_computation | async-start | bytes 1572864 | tf_op jit(solution)/shard_map/all_to_all | solution.py:229
  13.4 23.2 %all-to-all-done.in_ref = bf16[32,32,384]{2,1,0:T(8,128)(2,1)S(1)} async-done(((bf16[32,32,384]{2,1,0:T(8,128)(2,1)}), bf16[32,32,384]{2,1,0:T(8,128)(2,1)S(1)}, u32[]{:S(2)}, u32[]{:S(2)}) %all-to-all-start) | async-done | bytes 786464 | tf_op jit(solution)/shard_map/all_to_all | solution.py:229
  36.5 0.0 copy-done
  36.5 0.0 copy-done.4
  36.5 0.0 copy-start.1
  36.5 4.5 %shard_map.96 = (bf16[512,1152]{1,0:T(8,128)(2,1)S(1)}, bf16[512,384]{1,0:T(8,128)(2,1)S(1)}, f32[512,384]{1,0:T(8,128)S(1)}, f32[512,128]{1,0:T(8,128)S(1)}, f3...) custom-call(s32[1]{0:T(128)} %bitcast.replica_ref, bf16[256,256]{1,0:T(8,128)(2,1)S(1)} %copy-done.4, ...), custom_call_target="tpu_custom_call" | custom-call | flops 3000000000 | bytes 9000000 | tf_op jit(solution)/shard_map/pallas_call | solution.py:257
  41.0 1.9 %collective-permute-start = (bf16[2,384,384]{2,1,0:T(8,128)(2,1)S(1)}, bf16[2,384,384]{2,1,0:T(8,128)(2,1)S(1)}, u32[]{:S(2)}, u32[]{:S(2)}) collective-permute-start(bf16[2,384,384]{2,1,0:T(8,128)(2,1)S(1)} %get-tuple-element.18), channel_id=1, source_target_pairs={{0,256},{256,0},{1,257},{257,1},{2,258},{258,2},{3,259},{259,3},{4... | collective-permute-start | bytes 1769480 | tf_op jit(solution)/shard_map/ppermute | solution.py:280
  43.0 0.0 copy-done.1
  43.0 0.0 copy-start.5
  43.0 1.3 %shard_map.97 = bf16[32,16,384]{2,1,0:T(8,128)(2,1)S(1)} custom-call(bf16[256,256]{1,0:T(8,128)(2,1)S(1)} %copy-done.1, bf16[512,1152]{1,0:T(8,128)(2,1)S(1)} %get-tuple-element.13.grads_ref, bf16[512,384]{1,0:T(8,128)(2,1)S(1)} %get-tuple-element.14.delta_ref, f32[512,384]{1,0:T(8,128)S(1)} %get-tuple-element.15.standard_ref, ...), custom_call_target="tpu_custom_call" | custom-call | flops 1000000000 | bytes 3000000 | tf_op jit(solution)/shard_map/pallas_call | solution.py:282
  44.3 0.7 collective-permute-done.got_ref
  44.9 0.0 copy-done.5
  44.9 1.2 %shard_map.98 = bf16[4,192,384]{2,1,0:T(8,128)(2,1)} custom-call(bf16[192,192]{1,0:T(8,128)(2,1)S(1)} %copy-done.5, f32[2,384,384]{2,1,0:T(8,128)S(1)} %get-tuple-element.17.keep_ref, bf16[2,384,384]{2,1,0:T(8,128)(2,1)S(1)} %collective-permute-done.got_ref), custom_call_target="tpu_custom_call" | custom-call | flops 1000000000 | bytes 3000000 | tf_op jit(solution)/shard_map/pallas_call | solution.py:295
  46.1 0.0 copy-start.3
  46.1 3.6 %all-to-all-start.1 = ((bf16[4,192,384]{2,1,0:T(8,128)(2,1)}), bf16[4,192,384]{2,1,0:T(8,128)(2,1)S(1)}, u32[]{:S(2)}, u32[]{:S(2)}) async-start(bf16[4,192,384]{2,1,0:T(8,128)(2,1)} %shard_map.98), calls=%async_computation.1 | async-start | bytes 1179648 | tf_op jit(solution)/shard_map/all_to_all | solution.py:229
  49.7 0.0 copy-start.2
  49.7 2.1 %collective-permute-start.1 = (bf16[32,16,384]{2,1,0:T(8,128)(2,1)S(1)}, bf16[32,16,384]{2,1,0:T(8,128)(2,1)S(1)}, u32[]{:S(2)}, u32[]{:S(2)}) collective-permute-start(bf16[32,16,384]{2,1,0:T(8,128)(2,1)S(1)} %shard_map.97), channel_id=1, source_target_pairs={{32,0},{64,32},{96,64},{128,96},{160,128},{192,160},{224,192},{33,... | collective-permute-start | bytes 1179656 | tf_op jit(solution)/shard_map/ppermute | solution.py:287
  51.8 13.0 %collective-permute-done.1.back_ref = bf16[32,16,384]{2,1,0:T(8,128)(2,1)S(1)} collective-permute-done((bf16[32,16,384]{2,1,0:T(8,128)(2,1)S(1)}, bf16[32,16,384]{2,1,0:T(8,128)(2,1)S(1)}, u32[]{:S(2)}, u32[]{:S(2)}) %collective-permute-start.1) | collective-permute-done | bytes 393248 | tf_op jit(solution)/shard_map/ppermute | solution.py:287
  64.8 0.0 all-to-all-done.1.parts_ref
  64.8 0.0 copy-done.3
  64.8 0.3 shard_map.99
  65.1 24.8 %all_to_all.15.in_ref = bf16[32,24,384]{2,1,0:T(8,128)(2,1)S(1)} all-to-all(bf16[32,24,384]{2,1,0:T(8,128)(2,1)S(1)} %shard_map.99), channel_id=1, replica_groups=mesh['dp'=2,'section'=8,'mp'=32] {'mp'}, dimensions={0} | all-to-all | bytes 1179648 | tf_op jit(solution)/shard_map/all_to_all | solution.py:229
  89.9 0.0 copy-done.2
  89.9 1.0 %shard_map.100 = (bf16[512,384]{1,0:T(8,128)(2,1)}, f32[12,2,384]{2,1,0:T(2,128)}) custom-call(bf16[256,256]{1,0:T(8,128)(2,1)S(1)} %copy-done.2, bf16[32,24,384]{2,1,0:T(8,128)(2,1)S(1)} %all_to_all.15.in_ref), custom_call_target="tpu_custom_call" | custom-call | flops 100000000 | bytes 1000000 | tf_op jit(solution)/shard_map/pallas_call | solution.py:307
Async XLA Ops:
  3.1 33.5 %copy-start = (bf16[1,4,384,384]{3,2,1,0:T(8,128)(2,1)S(1)}, bf16[1,4,384,384]{3,2,1,0:T(8,128)(2,1)}, u32[]{:S(2)}) copy-start(bf16[1,4,384,384]{3,2,1,0:T(8,128)(2,1)} %param.10) | copy-start | bytes 3538948
  3.1 33.5 %copy-start.4 = (bf16[256,256]{1,0:T(8,128)(2,1)S(1)}, bf16[256,256]{1,0:T(8,128)(2,1)}, u32[]{:S(2)}) copy-start(bf16[256,256]{1,0:T(8,128)(2,1)} %constant.16.clone.order_ref) | copy-start | bytes 393220
  3.1 33.5 %all-to-all-start = ((bf16[32,32,384]{2,1,0:T(8,128)(2,1)}), bf16[32,32,384]{2,1,0:T(8,128)(2,1)S(1)}, u32[]{:S(2)}, u32[]{:S(2)}) async-start(bf16[32,32,384]{2,1,0:T(8,128)(2,1)} %shard_map.95), calls=%async_computation | async-start | bytes 1572864 | tf_op jit(solution)/shard_map/all_to_all | solution.py:229
  36.5 6.4 %copy-start.1 = (bf16[256,256]{1,0:T(8,128)(2,1)S(1)}, bf16[256,256]{1,0:T(8,128)(2,1)}, u32[]{:S(2)}) copy-start(bf16[256,256]{1,0:T(8,128)(2,1)} %constant.17.clone.order_ref) | copy-start | bytes 393220
  41.0 3.9 %collective-permute-start = (bf16[2,384,384]{2,1,0:T(8,128)(2,1)S(1)}, bf16[2,384,384]{2,1,0:T(8,128)(2,1)S(1)}, u32[]{:S(2)}, u32[]{:S(2)}) collective-permute-start(bf16[2,384,384]{2,1,0:T(8,128)(2,1)S(1)} %get-tuple-element.18), channel_id=1, source_target_pairs={{0,256},{256,0},{1,257},{257,1},{2,258},{258,2},{3,259},{259,3},{4... | collective-permute-start | bytes 1769480 | tf_op jit(solution)/shard_map/ppermute | solution.py:280
  43.0 2.0 %copy-start.5 = (bf16[192,192]{1,0:T(8,128)(2,1)S(1)}, bf16[192,192]{1,0:T(8,128)(2,1)}, u32[]{:S(2)}) copy-start(bf16[192,192]{1,0:T(8,128)(2,1)} %constant.18.clone.order_ref) | copy-start | bytes 221188
  46.1 18.7 %copy-start.3 = (bf16[256,192]{1,0:T(8,128)(2,1)S(1)}, bf16[256,192]{1,0:T(8,128)(2,1)}, u32[]{:S(2)}) copy-start(bf16[256,192]{1,0:T(8,128)(2,1)} %constant.19.clone.order_ref) | copy-start | bytes 294916
  46.1 18.7 %all-to-all-start.1 = ((bf16[4,192,384]{2,1,0:T(8,128)(2,1)}), bf16[4,192,384]{2,1,0:T(8,128)(2,1)S(1)}, u32[]{:S(2)}, u32[]{:S(2)}) async-start(bf16[4,192,384]{2,1,0:T(8,128)(2,1)} %shard_map.98), calls=%async_computation.1 | async-start | bytes 1179648 | tf_op jit(solution)/shard_map/all_to_all | solution.py:229
  49.7 40.2 %copy-start.2 = (bf16[256,256]{1,0:T(8,128)(2,1)S(1)}, bf16[256,256]{1,0:T(8,128)(2,1)}, u32[]{:S(2)}) copy-start(bf16[256,256]{1,0:T(8,128)(2,1)} %constant.20.clone.order_ref) | copy-start | bytes 393220
  49.7 15.0 %collective-permute-start.1 = (bf16[32,16,384]{2,1,0:T(8,128)(2,1)S(1)}, bf16[32,16,384]{2,1,0:T(8,128)(2,1)S(1)}, u32[]{:S(2)}, u32[]{:S(2)}) collective-permute-start(bf16[32,16,384]{2,1,0:T(8,128)(2,1)S(1)} %shard_map.97), channel_id=1, source_target_pairs={{32,0},{64,32},{96,64},{128,96},{160,128},{192,160},{224,192},{33,... | collective-permute-start | bytes 1179656 | tf_op jit(solution)/shard_map/ppermute | solution.py:287

commit v7 on v6

--- a/solution.py
+++ b/solution.py
@@ -45,7 +45,7 @@
     return dot(matrix, rows).astype(BF16)
 
 
-def pack_kernel(act_ref, grad_ref, out_ref, order_ref):
+def pack_kernel(_, act_ref, grad_ref, out_ref, order_ref):
     @pl.when(pl.program_id(0) == 0)
     def _():
         order_ref[...] = selection(
@@ -179,11 +179,14 @@
             out_ref[q, g * size : (g + 1) * size] = moved[q * size : (q + 1) * size]
 
 
-def leave_kernel(order_ref, parts_ref, back_ref, out_ref):
-    peers, _, width = back_ref.shape
+def collect_kernel(order_ref, parts_ref, out_ref):
+    total = jnp.sum(parts_ref[...].astype(F32), axis=0).astype(BF16)
+    out_ref[...] = reorder(order_ref[...], total).reshape(out_ref.shape)
+
+
+def leave_kernel(back_ref, cells_ref, out_ref):
     out_ref[:, :CELL] = back_ref[...]
-    total = jnp.sum(parts_ref[...].astype(F32), axis=0).astype(BF16)
-    out_ref[:, CELL:] = reorder(order_ref[...], total).reshape(peers, PAD, width)
+    out_ref[:, CELL:] = cells_ref[...]
 
 
 def final_kernel(order_ref, in_ref, received_ref, grads_ref):
@@ -236,24 +239,25 @@
     peers = lax.axis_size("mp")
     tokens = rows * residues
     part = width // peers
+    replica = lax.axis_index("dp").astype(jnp.int32).reshape(1)
     groups = peers // GROUP
     span = GROUP * COLS
     taken = pl.BlockSpec((rows, 1, span, width), lambda g: (0, g, 0, 0))
     packed = pl.pallas_call(
         pack_kernel,
         grid=(groups,),
-        in_specs=[taken] * 2,
+        in_specs=[SMEM] + [taken] * 2,
         out_specs=pl.BlockSpec((GROUP, 2 * CELL, width), lambda g: (g, 0, 0)),
         out_shape=shape((peers, 2 * CELL, width)),
         scratch_shapes=[pltpu.VMEM((BLOCK, BLOCK), BF16)],
         compiler_params=pltpu.CompilerParams(vmem_limit_bytes=56 * 1024 * 1024),
     )(
+        replica,
         activations.reshape(rows, groups, span, width),
         out_grads.reshape(rows, groups, span, width),
     )
     arrived = exchange(packed)
     weights = layer_weights[0]
-    replica = lax.axis_index("dp").astype(jnp.int32).reshape(1)
     grads, delta, standard, inverse, keep, give = call(
         attend_kernel,
         [SMEM] + [VMEM] * 3,
@@ -302,7 +306,8 @@
     order = table(
         peers * PAD, peers * cell, lambda o: (o >> 3) * cell + (o & 7) if (o & 7) < cell else -1
     )
-    leaving = call(leave_kernel, [VMEM] * 3, shape((peers, CELL + PAD, width)))(order, parts, back)
+    cells = call(collect_kernel, [VMEM] * 2, shape((peers, PAD, width)))(order, parts)
+    leaving = call(leave_kernel, [VMEM] * 2, shape((peers, CELL + PAD, width)))(back, cells)
     landed = exchange(leaving)
     received, weight_grads = call(
         final_kernel, [VMEM] * 2, (shape((tokens, width)), shape((part, 2, width), F32))

time: 91.3 us -> 90.9 us (level)
  blocking collectives: 24.8 us -> 58.3 us
  waiting for transfers between devices: 36.8 us -> 13.3 us
  starting transfers between devices: 17.9 us -> 7.45 us
    all_to_all x1 -> x2, blocking collectives: 24.8 us -> 58.3 us  [exchange(): lax.all_to_all(array, 'mp', split_axis=0, concat_axis=0, axis_index_group...]
    all_to_all x2 -> x1, waiting for transfers between devices: 23.2 us -> 8.79 us  [exchange(): lax.all_to_all(array, 'mp', split_axis=0, concat_axis=0, axis_index_group...]
    all_to_all x2 -> x1, starting transfers between devices: 13.9 us -> 3.61 us  [exchange(): lax.all_to_all(array, 'mp', split_axis=0, concat_axis=0, axis_index_group...]
    ppermute x1, waiting for transfers between devices: 13 us -> 3.88 us  [per_device(): lax.ppermute(back, 'section', [(i + 1, i) for i in range(sections - 1)])]
    pallas_call x2 -> x3, Pallas kernels: 2.74 us -> 2.76 us  [the longest x1 2.44 us: per_device(): pl.pallas_call(pack_kernel, grid=(groups,), in_specs=[SMEM] + [taken] * 2...]
  transfers between devices with their start and end apart: 4 -> 3, of which waited for: 3 -> 3; matrix products, arithmetic and copies ran while one was open for 0% -> 0% of each run, Pallas kernels for 1% -> 2%
where the time goes in v7:
time: 90.9 us; the launch traced here: 90.6 us
  blocking collectives  58.3 us (64%)
  waiting for transfers between devices  13.3 us (15%)
  Pallas kernels  10.7 us (12%)
  starting transfers between devices  7.45 us (8%)
    all_to_all x2, blocking collectives, exchange(): lax.all_to_all(array, 'mp', split_axis=0, concat_axis=0, axis_index_group...  58.3 us
    all_to_all x1, waiting for transfers between devices, exchange(): lax.all_to_all(array, 'mp', split_axis=0, concat_axis=0, axis_index_group...  8.79 us
    pallas_call x1, Pallas kernels, per_device(): call(attend_kernel, [SMEM] + [VMEM] * 3, (shape((tokens, 3 * width)), sha...  4.48 us
    ppermute x1, waiting for transfers between devices, per_device(): lax.ppermute(back, 'section', [(i + 1, i) for i in range(sections - 1)])  3.88 us
    all_to_all x1, starting transfers between devices, exchange(): lax.all_to_all(array, 'mp', split_axis=0, concat_axis=0, axis_index_group...  3.61 us
    pallas_call x1, Pallas kernels, per_device(): pl.pallas_call(pack_kernel, grid=(groups,), in_specs=[SMEM] + [taken] * 2...  2.44 us
    ppermute x1, starting transfers between devices, per_device(): got = lax.ppermute(give, 'dp', [(0, 1), (1, 0)])  1.92 us
    ppermute x1, starting transfers between devices, per_device(): lax.ppermute(back, 'section', [(i + 1, i) for i in range(sections - 1)])  1.92 us
  transfers between devices with their start and end apart: 3, of which 3 were waited for; matrix products, arithmetic and copies ran while one was open for 0% of the time, Pallas kernels for 2%

profile of v7, /device:TPU:200, one launch (start us, length us, event | category | flops | bytes accessed | tf_op | source)
XLA Modules:
  0.0 90.6 jit_solution(3522266834129524027)
XLA Ops:
  0.6 2.4 %shard_map.95 = bf16[32,32,384]{2,1,0:T(8,128)(2,1)} custom-call(s32[1]{0:T(128)} %bitcast._.replica_ref, bf16[4,2,64,384]{3,2,1,0:T(8,128)(2,1)} %bitcast.10, bf16[4,2,64,384]{3,2,1,0:T(8,128)(2,1)} %bitcast.11), custom_call_target="tpu_custom_call" | custom-call | tf_op jit(solution)/shard_map/pallas_call | solution.py:246
  3.1 0.0 copy-start
  3.1 0.0 copy-start.4
  3.1 33.5 %all_to_all.15.in_ref = bf16[32,32,384]{2,1,0:T(8,128)(2,1)S(1)} all-to-all(bf16[32,32,384]{2,1,0:T(8,128)(2,1)} %shard_map.95), channel_id=1, replica_groups=mesh['dp'=2,'section'=8,'mp'=32] {'mp'}, dimensions={0} | all-to-all | bytes 1572864 | tf_op jit(solution)/shard_map/all_to_all | solution.py:232
  36.5 0.0 copy-done
  36.5 0.0 copy-done.4
  36.5 0.0 copy-start.2
  36.5 4.5 %shard_map.96 = (bf16[512,1152]{1,0:T(8,128)(2,1)S(1)}, bf16[512,384]{1,0:T(8,128)(2,1)S(1)}, f32[512,384]{1,0:T(8,128)S(1)}, f32[512,128]{1,0:T(8,128)S(1)}, f3...) custom-call(s32[1]{0:T(128)} %bitcast._.replica_ref, bf16[256,256]{1,0:T(8,128)(2,1)S(1)} %copy-done.4, ...), custom_call_target="tpu_custom_call" | custom-call | flops 3000000000 | bytes 9000000 | tf_op jit(solution)/shard_map/pallas_call | solution.py:261
  41.0 1.9 %collective-permute-start.1 = (bf16[2,384,384]{2,1,0:T(8,128)(2,1)S(1)}, bf16[2,384,384]{2,1,0:T(8,128)(2,1)S(1)}, u32[]{:S(2)}, u32[]{:S(2)}) collective-permute-start(bf16[2,384,384]{2,1,0:T(8,128)(2,1)S(1)} %get-tuple-element.19), channel_id=1, source_target_pairs={{0,256},{256,0},{1,257},{257,1},{2,258},{258,2},{3,259},{259,3},{4... | collective-permute-start | bytes 1769480 | tf_op jit(solution)/shard_map/ppermute | solution.py:284
  43.0 0.0 copy-done.2
  43.0 0.0 copy-start.5
  43.0 1.3 %shard_map.97 = bf16[32,16,384]{2,1,0:T(8,128)(2,1)S(1)} custom-call(bf16[256,256]{1,0:T(8,128)(2,1)S(1)} %copy-done.2, bf16[512,1152]{1,0:T(8,128)(2,1)S(1)} %get-tuple-element.13.grads_ref, bf16[512,384]{1,0:T(8,128)(2,1)S(1)} %get-tuple-element.14.delta_ref, f32[512,384]{1,0:T(8,128)S(1)} %get-tuple-element.15.standard_ref, ...), custom_call_target="tpu_custom_call" | custom-call | flops 1000000000 | bytes 3000000 | tf_op jit(solution)/shard_map/pallas_call | solution.py:286
  44.3 0.7 collective-permute-done.1.got_ref
  44.9 0.0 copy-done.5
  44.9 1.2 %shard_map.98 = bf16[4,192,384]{2,1,0:T(8,128)(2,1)} custom-call(bf16[192,192]{1,0:T(8,128)(2,1)S(1)} %copy-done.5, f32[2,384,384]{2,1,0:T(8,128)S(1)} %get-tuple-element.18.keep_ref, bf16[2,384,384]{2,1,0:T(8,128)(2,1)S(1)} %collective-permute-done.1.got_ref), custom_call_target="tpu_custom_call" | custom-call | flops 1000000000 | bytes 3000000 | tf_op jit(solution)/shard_map/pallas_call | solution.py:299
  46.1 0.0 copy-start.1
  46.1 3.6 %all-to-all-start.1 = ((bf16[4,192,384]{2,1,0:T(8,128)(2,1)}), bf16[4,192,384]{2,1,0:T(8,128)(2,1)S(1)}, u32[]{:S(2)}, u32[]{:S(2)}) async-start(bf16[4,192,384]{2,1,0:T(8,128)(2,1)} %shard_map.98), calls=%async_computation.1 | async-start | bytes 1179648 | tf_op jit(solution)/shard_map/all_to_all | solution.py:232
  49.7 1.9 %collective-permute-start = (bf16[32,16,384]{2,1,0:T(8,128)(2,1)S(1)}, bf16[32,16,384]{2,1,0:T(8,128)(2,1)S(1)}, u32[]{:S(2)}, u32[]{:S(2)}) collective-permute-start(bf16[32,16,384]{2,1,0:T(8,128)(2,1)S(1)} %shard_map.97), channel_id=1, source_target_pairs={{32,0},{64,32},{96,64},{128,96},{160,128},{192,160},{224,192},{33,... | collective-permute-start | bytes 1179656 | tf_op jit(solution)/shard_map/ppermute | solution.py:291
  51.7 8.8 %all-to-all-done.1.parts_ref = bf16[4,192,384]{2,1,0:T(8,128)(2,1)S(1)} async-done(((bf16[4,192,384]{2,1,0:T(8,128)(2,1)}), bf16[4,192,384]{2,1,0:T(8,128)(2,1)S(1)}, u32[]{:S(2)}, u32[]{:S(2)}) %all-to-all-start.1) | async-done | bytes 589856 | tf_op jit(solution)/shard_map/all_to_all | solution.py:232
  60.4 0.0 copy-done.1
  60.4 0.3 shard_map.99.cells_ref
  60.7 0.0 copy-start.3
  60.7 3.9 %collective-permute-done.back_ref = bf16[32,16,384]{2,1,0:T(8,128)(2,1)S(1)} collective-permute-done((bf16[32,16,384]{2,1,0:T(8,128)(2,1)S(1)}, bf16[32,16,384]{2,1,0:T(8,128)(2,1)S(1)}, u32[]{:S(2)}, u32[]{:S(2)}) %collective-permute-start) | collective-permute-done | bytes 393248 | tf_op jit(solution)/shard_map/ppermute | solution.py:291
  64.6 0.1 shard_map.100
  64.7 24.9 %all_to_all.16.in_ref = bf16[32,24,384]{2,1,0:T(8,128)(2,1)S(1)} all-to-all(bf16[32,24,384]{2,1,0:T(8,128)(2,1)S(1)} %shard_map.100), channel_id=1, replica_groups=mesh['dp'=2,'section'=8,'mp'=32] {'mp'}, dimensions={0} | all-to-all | bytes 1179648 | tf_op jit(solution)/shard_map/all_to_all | solution.py:232
  89.5 0.0 copy-done.3
  89.5 1.0 %shard_map.101 = (bf16[512,384]{1,0:T(8,128)(2,1)}, f32[12,2,384]{2,1,0:T(2,128)}) custom-call(bf16[256,256]{1,0:T(8,128)(2,1)S(1)} %copy-done.3, bf16[32,24,384]{2,1,0:T(8,128)(2,1)S(1)} %all_to_all.16.in_ref), custom_call_target="tpu_custom_call" | custom-call | flops 100000000 | bytes 1000000 | tf_op jit(solution)/shard_map/pallas_call | solution.py:312
Async XLA Ops:
  3.1 33.5 %copy-start = (bf16[1,4,384,384]{3,2,1,0:T(8,128)(2,1)S(1)}, bf16[1,4,384,384]{3,2,1,0:T(8,128)(2,1)}, u32[]{:S(2)}) copy-start(bf16[1,4,384,384]{3,2,1,0:T(8,128)(2,1)} %param.10) | copy-start | bytes 3538948
  3.1 33.5 %copy-start.4 = (bf16[256,256]{1,0:T(8,128)(2,1)S(1)}, bf16[256,256]{1,0:T(8,128)(2,1)}, u32[]{:S(2)}) copy-start(bf16[256,256]{1,0:T(8,128)(2,1)} %constant.16.clone.order_ref) | copy-start | bytes 393220
  36.5 6.4 %copy-start.2 = (bf16[256,256]{1,0:T(8,128)(2,1)S(1)}, bf16[256,256]{1,0:T(8,128)(2,1)}, u32[]{:S(2)}) copy-start(bf16[256,256]{1,0:T(8,128)(2,1)} %constant.17.clone.order_ref) | copy-start | bytes 393220
  41.0 3.9 %collective-permute-start.1 = (bf16[2,384,384]{2,1,0:T(8,128)(2,1)S(1)}, bf16[2,384,384]{2,1,0:T(8,128)(2,1)S(1)}, u32[]{:S(2)}, u32[]{:S(2)}) collective-permute-start(bf16[2,384,384]{2,1,0:T(8,128)(2,1)S(1)} %get-tuple-element.19), channel_id=1, source_target_pairs={{0,256},{256,0},{1,257},{257,1},{2,258},{258,2},{3,259},{259,3},{4... | collective-permute-start | bytes 1769480 | tf_op jit(solution)/shard_map/ppermute | solution.py:284
  43.0 2.0 %copy-start.5 = (bf16[192,192]{1,0:T(8,128)(2,1)S(1)}, bf16[192,192]{1,0:T(8,128)(2,1)}, u32[]{:S(2)}) copy-start(bf16[192,192]{1,0:T(8,128)(2,1)} %constant.18.clone.order_ref) | copy-start | bytes 221188
  46.1 14.3 %copy-start.1 = (bf16[256,192]{1,0:T(8,128)(2,1)S(1)}, bf16[256,192]{1,0:T(8,128)(2,1)}, u32[]{:S(2)}) copy-start(bf16[256,192]{1,0:T(8,128)(2,1)} %constant.19.clone.order_ref) | copy-start | bytes 294916
  46.1 14.3 %all-to-all-start.1 = ((bf16[4,192,384]{2,1,0:T(8,128)(2,1)}), bf16[4,192,384]{2,1,0:T(8,128)(2,1)S(1)}, u32[]{:S(2)}, u32[]{:S(2)}) async-start(bf16[4,192,384]{2,1,0:T(8,128)(2,1)} %shard_map.98), calls=%async_computation.1 | async-start | bytes 1179648 | tf_op jit(solution)/shard_map/all_to_all | solution.py:232
  49.7 14.9 %collective-permute-start = (bf16[32,16,384]{2,1,0:T(8,128)(2,1)S(1)}, bf16[32,16,384]{2,1,0:T(8,128)(2,1)S(1)}, u32[]{:S(2)}, u32[]{:S(2)}) collective-permute-start(bf16[32,16,384]{2,1,0:T(8,128)(2,1)S(1)} %shard_map.97), channel_id=1, source_target_pairs={{32,0},{64,32},{96,64},{128,96},{160,128},{192,160},{224,192},{33,... | collective-permute-start | bytes 1179656 | tf_op jit(solution)/shard_map/ppermute | solution.py:291
  60.7 28.8 %copy-start.3 = (bf16[256,256]{1,0:T(8,128)(2,1)S(1)}, bf16[256,256]{1,0:T(8,128)(2,1)}, u32[]{:S(2)}) copy-start(bf16[256,256]{1,0:T(8,128)(2,1)} %constant.20.clone.order_ref) | copy-start | bytes 393220

commit v8 on v7

--- a/solution.py
+++ b/solution.py
@@ -60,14 +60,15 @@
 def attend_kernel(
     replica_ref,
     order_ref,
+    back_order_ref,
     in_ref,
     weight_ref,
+    back_ref,
+    keep_ref,
+    give_ref,
     grads_ref,
     delta_ref,
     standard_ref,
-    inverse_ref,
-    keep_ref,
-    give_ref,
     normed_ref,
     attn_ref,
     proj_ref,
@@ -92,7 +93,6 @@
     inverse = lax.rsqrt(jnp.mean(centred * centred, axis=-1, keepdims=True) + EPS)
     standard = centred * inverse
     standard_ref[...] = standard
-    inverse_ref[...] = jnp.broadcast_to(inverse, inverse_ref.shape)
     normed = standard.astype(BF16)
     normed_ref[...] = normed
     joint = jnp.concatenate([weight_ref[n] for n in range(3)], axis=1)
@@ -137,6 +137,20 @@
 
     lax.fori_loop(0, COLS, column, 0, unroll=4)
 
+    grad_in = dot(grads_ref[...], joint, ((1,), (1,)))
+    standard = standard_ref[...]
+    grad_mean = jnp.mean(grad_in, axis=-1, keepdims=True)
+    grad_proj = jnp.mean(grad_in * standard, axis=-1, keepdims=True)
+    branch = inverse * (grad_in - grad_mean - standard * grad_proj)
+    branch = branch.astype(BF16).astype(F32)
+    input_grad = (delta_ref[...].astype(F32) + branch).astype(BF16)
+    order = back_order_ref[...]
+    for g in range(groups):
+        rows = jnp.concatenate(
+            [input_grad[j * seqs + g * span : j * seqs + (g + 1) * span] for j in range(COLS)]
+        )
+        back_ref[g * GROUP : (g + 1) * GROUP] = reorder(order, rows).reshape(GROUP, CELL, width)
+
     first = replica_ref[0] == 0
     term = dot(normed_ref[...], grads_ref[...], ((0,), (0,)))
     terms = [term[:, n * width : (n + 1) * width] for n in range(3)]
@@ -144,27 +158,6 @@
     for m in range(2):
         keep_ref[m] = jnp.where(first, terms[m], terms[m + 2])
         give_ref[m] = jnp.where(first, terms[m + 2], terms[m]).astype(BF16)
-
-
-def input_kernel(order_ref, grads_ref, delta_ref, standard_ref, inverse_ref, weight_ref, back_ref):
-    groups = back_ref.shape[0] // GROUP
-    tokens, width = delta_ref.shape
-    seqs = tokens // COLS
-    span = GROUP * ROWS
-    joint = jnp.concatenate([weight_ref[n] for n in range(3)], axis=1)
-    grad_in = dot(grads_ref[...], joint, ((1,), (1,)))
-    standard = standard_ref[...]
-    grad_mean = jnp.mean(grad_in, axis=-1, keepdims=True)
-    grad_proj = jnp.mean(grad_in * standard, axis=-1, keepdims=True)
-    branch = inverse_ref[:, :1] * (grad_in - grad_mean - standard * grad_proj)
-    branch = branch.astype(BF16).astype(F32)
-    input_grad = (delta_ref[...].astype(F32) + branch).astype(BF16)
-    order = order_ref[...]
-    for g in range(groups):
-        rows = jnp.concatenate(
-            [input_grad[j * seqs + g * span : j * seqs + (g + 1) * span] for j in range(COLS)]
-        )
-        back_ref[g * GROUP : (g + 1) * GROUP] = reorder(order, rows).reshape(GROUP, CELL, width)
 
 
 def spread_kernel(order_ref, keep_ref, got_ref, out_ref):
@@ -258,35 +251,31 @@
     )
     arrived = exchange(packed)
     weights = layer_weights[0]
-    grads, delta, standard, inverse, keep, give = call(
+    back, keep, give = call(
         attend_kernel,
-        [SMEM] + [VMEM] * 3,
+        [SMEM] + [VMEM] * 4,
         (
-            shape((tokens, 3 * width)),
-            shape((tokens, width)),
-            shape((tokens, width), F32),
-            shape((tokens, LANES), F32),
+            shape((peers, CELL, width)),
             shape((2, width, width), F32),
             shape((2, width, width)),
         ),
         [
+            pltpu.VMEM((tokens, 3 * width), BF16),
+            pltpu.VMEM((tokens, width), BF16),
+            pltpu.VMEM((tokens, width), F32),
             pltpu.VMEM((tokens, width), BF16),
             pltpu.VMEM((tokens, width), BF16),
             pltpu.VMEM((tokens, 4 * width), BF16),
         ],
-        cost=(3e9, 9e6),
+        cost=(4e9, 9e6),
     )(
         replica,
         table(BLOCK, BLOCK, lambda o: ((o >> 2) & 15) * 16 + (o & 3) * 4 + (o >> 6)),
+        table(BLOCK, BLOCK, lambda o: (o & 3) * 64 + (o >> 4) * 4 + ((o >> 2) & 3)),
         arrived,
         weights,
     )
     got = lax.ppermute(give, "dp", [(0, 1), (1, 0)])
-    order = table(BLOCK, BLOCK, lambda o: (o & 3) * 64 + (o >> 4) * 4 + ((o >> 2) & 3))
-    back = call(input_kernel, [VMEM] * 6, shape((peers, CELL, width)), cost=(1e9, 3e6))(
-        order, grads, delta, standard, inverse, weights
-    )
-    keep, back = lax.optimization_barrier((keep, back))
     sections = lax.axis_size("section")
     back = lax.ppermute(back, "section", [(i + 1, i) for i in range(sections - 1)])
     piece = part // NX

time: 90.9 us -> 92 us (1.012)
  waiting for transfers between devices: 13.3 us -> 14.6 us
    ppermute x1, waiting for transfers between devices: 0.67 us -> 1.97 us  [per_device(): got = lax.ppermute(give, 'dp', [(0, 1), (1, 0)])]
    pallas_call x2 -> x1, Pallas kernels: 5.75 us -> 5.51 us  [per_device(): call(attend_kernel, [SMEM] + [VMEM] * 4, (shape((peers, CELL, width)), sh...]
  transfers between devices with their start and end apart: 3 -> 3, of which waited for: 3 -> 3; matrix products, arithmetic and copies ran while one was open for 0% -> 0% of each run, Pallas kernels for 2% -> 0%
where the time goes in v8:
time: 92 us; the launch traced here: 91.6 us
  blocking collectives  58.3 us (63%)
  waiting for transfers between devices  14.6 us (16%)
  Pallas kernels  10.5 us (11%)
  starting transfers between devices  7.45 us (8%)
    all_to_all x2, blocking collectives, exchange(): lax.all_to_all(array, 'mp', split_axis=0, concat_axis=0, axis_index_group...  58.3 us
    all_to_all x1, waiting for transfers between devices, exchange(): lax.all_to_all(array, 'mp', split_axis=0, concat_axis=0, axis_index_group...  8.79 us
    pallas_call x1, Pallas kernels, per_device(): call(attend_kernel, [SMEM] + [VMEM] * 4, (shape((peers, CELL, width)), sh...  5.51 us
    ppermute x1, waiting for transfers between devices, per_device(): lax.ppermute(back, 'section', [(i + 1, i) for i in range(sections - 1)])  3.88 us
    all_to_all x1, starting transfers between devices, exchange(): lax.all_to_all(array, 'mp', split_axis=0, concat_axis=0, axis_index_group...  3.61 us
    pallas_call x1, Pallas kernels, per_device(): pl.pallas_call(pack_kernel, grid=(groups,), in_specs=[SMEM] + [taken] * 2...  2.44 us
    ppermute x1, waiting for transfers between devices, per_device(): got = lax.ppermute(give, 'dp', [(0, 1), (1, 0)])  1.97 us
    ppermute x1, starting transfers between devices, per_device(): got = lax.ppermute(give, 'dp', [(0, 1), (1, 0)])  1.92 us
  transfers between devices with their start and end apart: 3, of which 3 were waited for; matrix products, arithmetic and copies ran while one was open for 0% of the time, Pallas kernels for 0%

profile of v8, /device:TPU:200, one launch (start us, length us, event | category | flops | bytes accessed | tf_op | source)
XLA Modules:
  0.0 91.6 jit_solution(18339201819406660436)
XLA Ops:
  0.6 2.4 %shard_map.95 = bf16[32,32,384]{2,1,0:T(8,128)(2,1)} custom-call(s32[1]{0:T(128)} %bitcast._.replica_ref, bf16[4,2,64,384]{3,2,1,0:T(8,128)(2,1)} %bitcast.9, bf16[4,2,64,384]{3,2,1,0:T(8,128)(2,1)} %bitcast.10), custom_call_target="tpu_custom_call" | custom-call | tf_op jit(solution)/shard_map/pallas_call | solution.py:239
  3.1 0.0 copy-start.2
  3.1 0.0 copy-start.3
  3.1 0.0 copy-start.4
  3.1 33.5 %all_to_all.15.in_ref = bf16[32,32,384]{2,1,0:T(8,128)(2,1)S(1)} all-to-all(bf16[32,32,384]{2,1,0:T(8,128)(2,1)} %shard_map.95), channel_id=1, replica_groups=mesh['dp'=2,'section'=8,'mp'=32] {'mp'}, dimensions={0} | all-to-all | bytes 1572864 | tf_op jit(solution)/shard_map/all_to_all | solution.py:225
  36.6 0.0 copy-done.2
  36.6 0.0 copy-done.3
  36.6 0.0 copy-done.4
  36.6 0.0 copy-start.5
  36.6 5.5 %shard_map.96 = (bf16[32,16,384]{2,1,0:T(8,128)(2,1)S(1)}, f32[2,384,384]{2,1,0:T(8,128)S(1)}, bf16[2,384,384]{2,1,0:T(8,128)(2,1)S(1)}) custom-call(s32[1]{0:T(128)} %bitcast._.replica_ref, bf16[256,256]{1,0:T(8,128)(2,1)S(1)} %copy-done.4, bf16[256,256]{1,0:T(8,128)(2,1)S(1)} %copy-done.3, bf16[32,32,384]{2,1,0:T(8,128)(2,1)S(1)} %all_to_all.15.in_ref, ...), custom_call_target="tpu_custom_call" | custom-call | flops 4000000000 | bytes 9000000 | tf_op jit(solution)/shard_map/pallas_call | solution.py:254
  42.1 1.9 %collective-permute-start.1 = (bf16[2,384,384]{2,1,0:T(8,128)(2,1)S(1)}, bf16[2,384,384]{2,1,0:T(8,128)(2,1)S(1)}, u32[]{:S(2)}, u32[]{:S(2)}) collective-permute-start(bf16[2,384,384]{2,1,0:T(8,128)(2,1)S(1)} %get-tuple-element.9), channel_id=1, source_target_pairs={{0,256},{256,0},{1,257},{257,1},{2,258},{258,2},{3,259},{259,3},{4... | collective-permute-start | bytes 1769480 | tf_op jit(solution)/shard_map/ppermute | solution.py:278
  44.0 2.0 %collective-permute-done.1.got_ref = bf16[2,384,384]{2,1,0:T(8,128)(2,1)S(1)} collective-permute-done((bf16[2,384,384]{2,1,0:T(8,128)(2,1)S(1)}, bf16[2,384,384]{2,1,0:T(8,128)(2,1)S(1)}, u32[]{:S(2)}, u32[]{:S(2)}) %collective-permute-start.1) | collective-permute-done | bytes 589856 | tf_op jit(solution)/shard_map/ppermute | solution.py:278
  46.0 0.0 copy-done.5
  46.0 1.2 %shard_map.97 = bf16[4,192,384]{2,1,0:T(8,128)(2,1)} custom-call(bf16[192,192]{1,0:T(8,128)(2,1)S(1)} %copy-done.5, f32[2,384,384]{2,1,0:T(8,128)S(1)} %get-tuple-element.8.keep_ref, bf16[2,384,384]{2,1,0:T(8,128)(2,1)S(1)} %collective-permute-done.1.got_ref), custom_call_target="tpu_custom_call" | custom-call | flops 1000000000 | bytes 3000000 | tf_op jit(solution)/shard_map/pallas_call | solution.py:288
  47.2 0.0 copy-start
  47.2 3.6 %all-to-all-start.1 = ((bf16[4,192,384]{2,1,0:T(8,128)(2,1)}), bf16[4,192,384]{2,1,0:T(8,128)(2,1)S(1)}, u32[]{:S(2)}, u32[]{:S(2)}) async-start(bf16[4,192,384]{2,1,0:T(8,128)(2,1)} %shard_map.97), calls=%async_computation.1 | async-start | bytes 1179648 | tf_op jit(solution)/shard_map/all_to_all | solution.py:225
  50.8 1.9 %collective-permute-start = (bf16[32,16,384]{2,1,0:T(8,128)(2,1)S(1)}, bf16[32,16,384]{2,1,0:T(8,128)(2,1)S(1)}, u32[]{:S(2)}, u32[]{:S(2)}) collective-permute-start(bf16[32,16,384]{2,1,0:T(8,128)(2,1)S(1)} %get-tuple-element.7), channel_id=1, source_target_pairs={{32,0},{64,32},{96,64},{128,96},{160,128},{192,160},{224,192},{33,... | collective-permute-start | bytes 1179656 | tf_op jit(solution)/shard_map/ppermute | solution.py:280
  52.7 8.8 %all-to-all-done.1.parts_ref = bf16[4,192,384]{2,1,0:T(8,128)(2,1)S(1)} async-done(((bf16[4,192,384]{2,1,0:T(8,128)(2,1)}), bf16[4,192,384]{2,1,0:T(8,128)(2,1)S(1)}, u32[]{:S(2)}, u32[]{:S(2)}) %all-to-all-start.1) | async-done | bytes 589856 | tf_op jit(solution)/shard_map/all_to_all | solution.py:225
  61.5 0.0 copy-done
  61.5 0.3 shard_map.98.cells_ref
  61.8 0.0 copy-start.1
  61.8 3.9 %collective-permute-done.back_ref = bf16[32,16,384]{2,1,0:T(8,128)(2,1)S(1)} collective-permute-done((bf16[32,16,384]{2,1,0:T(8,128)(2,1)S(1)}, bf16[32,16,384]{2,1,0:T(8,128)(2,1)S(1)}, u32[]{:S(2)}, u32[]{:S(2)}) %collective-permute-start) | collective-permute-done | bytes 393248 | tf_op jit(solution)/shard_map/ppermute | solution.py:280
  65.7 0.1 shard_map.99
  65.7 24.9 %all_to_all.16.in_ref = bf16[32,24,384]{2,1,0:T(8,128)(2,1)S(1)} all-to-all(bf16[32,24,384]{2,1,0:T(8,128)(2,1)S(1)} %shard_map.99), channel_id=1, replica_groups=mesh['dp'=2,'section'=8,'mp'=32] {'mp'}, dimensions={0} | all-to-all | bytes 1179648 | tf_op jit(solution)/shard_map/all_to_all | solution.py:225
  90.6 0.0 copy-done.1
  90.6 1.0 %shard_map.100 = (bf16[512,384]{1,0:T(8,128)(2,1)}, f32[12,2,384]{2,1,0:T(2,128)}) custom-call(bf16[256,256]{1,0:T(8,128)(2,1)S(1)} %copy-done.1, bf16[32,24,384]{2,1,0:T(8,128)(2,1)S(1)} %all_to_all.16.in_ref), custom_call_target="tpu_custom_call" | custom-call | flops 100000000 | bytes 1000000 | tf_op jit(solution)/shard_map/pallas_call | solution.py:301
Async XLA Ops:
  3.1 33.5 %copy-start.2 = (bf16[1,4,384,384]{3,2,1,0:T(8,128)(2,1)S(1)}, bf16[1,4,384,384]{3,2,1,0:T(8,128)(2,1)}, u32[]{:S(2)}) copy-start(bf16[1,4,384,384]{3,2,1,0:T(8,128)(2,1)} %param.10) | copy-start | bytes 3538948
  3.1 33.5 %copy-start.3 = (bf16[256,256]{1,0:T(8,128)(2,1)S(1)}, bf16[256,256]{1,0:T(8,128)(2,1)}, u32[]{:S(2)}) copy-start(bf16[256,256]{1,0:T(8,128)(2,1)} %constant.17.clone.back_order_ref) | copy-start | bytes 393220
  3.1 33.5 %copy-start.4 = (bf16[256,256]{1,0:T(8,128)(2,1)S(1)}, bf16[256,256]{1,0:T(8,128)(2,1)}, u32[]{:S(2)}) copy-start(bf16[256,256]{1,0:T(8,128)(2,1)} %constant.16.clone.order_ref) | copy-start | bytes 393220
  36.6 9.4 %copy-start.5 = (bf16[192,192]{1,0:T(8,128)(2,1)S(1)}, bf16[192,192]{1,0:T(8,128)(2,1)}, u32[]{:S(2)}) copy-start(bf16[192,192]{1,0:T(8,128)(2,1)} %constant.18.clone.order_ref) | copy-start | bytes 221188
  42.1 3.9 %collective-permute-start.1 = (bf16[2,384,384]{2,1,0:T(8,128)(2,1)S(1)}, bf16[2,384,384]{2,1,0:T(8,128)(2,1)S(1)}, u32[]{:S(2)}, u32[]{:S(2)}) collective-permute-start(bf16[2,384,384]{2,1,0:T(8,128)(2,1)S(1)} %get-tuple-element.9), channel_id=1, source_target_pairs={{0,256},{256,0},{1,257},{257,1},{2,258},{258,2},{3,259},{259,3},{4... | collective-permute-start | bytes 1769480 | tf_op jit(solution)/shard_map/ppermute | solution.py:278
  47.2 14.3 %copy-start = (bf16[256,192]{1,0:T(8,128)(2,1)S(1)}, bf16[256,192]{1,0:T(8,128)(2,1)}, u32[]{:S(2)}) copy-start(bf16[256,192]{1,0:T(8,128)(2,1)} %constant.19.clone.order_ref) | copy-start | bytes 294916
  47.2 14.3 %all-to-all-start.1 = ((bf16[4,192,384]{2,1,0:T(8,128)(2,1)}), bf16[4,192,384]{2,1,0:T(8,128)(2,1)S(1)}, u32[]{:S(2)}, u32[]{:S(2)}) async-start(bf16[4,192,384]{2,1,0:T(8,128)(2,1)} %shard_map.97), calls=%async_computation.1 | async-start | bytes 1179648 | tf_op jit(solution)/shard_map/all_to_all | solution.py:225
  50.8 14.9 %collective-permute-start = (bf16[32,16,384]{2,1,0:T(8,128)(2,1)S(1)}, bf16[32,16,384]{2,1,0:T(8,128)(2,1)S(1)}, u32[]{:S(2)}, u32[]{:S(2)}) collective-permute-start(bf16[32,16,384]{2,1,0:T(8,128)(2,1)S(1)} %get-tuple-element.7), channel_id=1, source_target_pairs={{32,0},{64,32},{96,64},{128,96},{160,128},{192,160},{224,192},{33,... | collective-permute-start | bytes 1179656 | tf_op jit(solution)/shard_map/ppermute | solution.py:280
  61.8 28.8 %copy-start.1 = (bf16[256,256]{1,0:T(8,128)(2,1)S(1)}, bf16[256,256]{1,0:T(8,128)(2,1)}, u32[]{:S(2)}) copy-start(bf16[256,256]{1,0:T(8,128)(2,1)} %constant.20.clone.order_ref) | copy-start | bytes 393220

commit v9 on v8

--- a/solution.py
+++ b/solution.py
@@ -45,7 +45,7 @@
     return dot(matrix, rows).astype(BF16)
 
 
-def pack_kernel(_, act_ref, grad_ref, out_ref, order_ref):
+def pack_kernel(_, __, act_ref, grad_ref, out_ref, order_ref):
     @pl.when(pl.program_id(0) == 0)
     def _():
         order_ref[...] = selection(
@@ -177,8 +177,9 @@
     out_ref[...] = reorder(order_ref[...], total).reshape(out_ref.shape)
 
 
-def leave_kernel(back_ref, cells_ref, out_ref):
-    out_ref[:, :CELL] = back_ref[...]
+def leave_kernel(last_ref, back_ref, cells_ref, out_ref):
+    back = back_ref[...]
+    out_ref[:, :CELL] = jnp.where(last_ref[0] == 1, jnp.zeros_like(back), back)
     out_ref[:, CELL:] = cells_ref[...]
 
 
@@ -233,19 +234,22 @@
     tokens = rows * residues
     part = width // peers
     replica = lax.axis_index("dp").astype(jnp.int32).reshape(1)
+    last = lax.axis_index("section") == lax.axis_size("section") - 1
+    last = last.astype(jnp.int32).reshape(1)
     groups = peers // GROUP
     span = GROUP * COLS
     taken = pl.BlockSpec((rows, 1, span, width), lambda g: (0, g, 0, 0))
     packed = pl.pallas_call(
         pack_kernel,
         grid=(groups,),
-        in_specs=[SMEM] + [taken] * 2,
+        in_specs=[SMEM] * 2 + [taken] * 2,
         out_specs=pl.BlockSpec((GROUP, 2 * CELL, width), lambda g: (g, 0, 0)),
         out_shape=shape((peers, 2 * CELL, width)),
         scratch_shapes=[pltpu.VMEM((BLOCK, BLOCK), BF16)],
         compiler_params=pltpu.CompilerParams(vmem_limit_bytes=56 * 1024 * 1024),
     )(
         replica,
+        last,
         activations.reshape(rows, groups, span, width),
         out_grads.reshape(rows, groups, span, width),
     )
@@ -277,7 +281,7 @@
     )
     got = lax.ppermute(give, "dp", [(0, 1), (1, 0)])
     sections = lax.axis_size("section")
-    back = lax.ppermute(back, "section", [(i + 1, i) for i in range(sections - 1)])
+    back = lax.ppermute(back, "section", [(i, (i - 1) % sections) for i in range(sections)])
     piece = part // NX
 
     def spread_from(o):
@@ -296,7 +300,9 @@
         peers * PAD, peers * cell, lambda o: (o >> 3) * cell + (o & 7) if (o & 7) < cell else -1
     )
     cells = call(collect_kernel, [VMEM] * 2, shape((peers, PAD, width)))(order, parts)
-    leaving = call(leave_kernel, [VMEM] * 2, shape((peers, CELL + PAD, width)))(back, cells)
+    leaving = call(leave_kernel, [SMEM] + [VMEM] * 2, shape((peers, CELL + PAD, width)))(
+        last, back, cells
+    )
     landed = exchange(leaving)
     received, weight_grads = call(
         final_kernel, [VMEM] * 2, (shape((tokens, width)), shape((part, 2, width), F32))

time: 92 us -> 96.5 us (1.049)
  the two profiles are of different devices: /device:TPU:200 before, /device:TPU:8 now
where the time goes in v9:
time: 96.5 us; the launch traced here: 96.1 us
  blocking collectives  58 us (60%)
  starting transfers between devices  16.5 us (17%)
  Pallas kernels  10.5 us (11%)
  waiting for transfers between devices  10.3 us (11%)
    all_to_all x2, blocking collectives, exchange(): lax.all_to_all(array, 'mp', split_axis=0, concat_axis=0, axis_index_group...  58 us
    ppermute x1, starting transfers between devices, per_device(): lax.ppermute(back, 'section', [(i, (i - 1) % sections) for i in range(sec...  11 us
    ppermute x1, waiting for transfers between devices, per_device(): lax.ppermute(back, 'section', [(i, (i - 1) % sections) for i in range(sec...  8.34 us
    pallas_call x1, Pallas kernels, per_device(): call(attend_kernel, [SMEM] + [VMEM] * 4, (shape((peers, CELL, width)), sh...  5.51 us
    all_to_all x1, starting transfers between devices, exchange(): lax.all_to_all(array, 'mp', split_axis=0, concat_axis=0, axis_index_group...  3.61 us
    pallas_call x1, Pallas kernels, per_device(): pl.pallas_call(pack_kernel, grid=(groups,), in_specs=[SMEM] * 2 + [taken]...  2.44 us
    ppermute x1, waiting for transfers between devices, per_device(): got = lax.ppermute(give, 'dp', [(0, 1), (1, 0)])  1.97 us
  transfers between devices with their start and end apart: 3, of which 2 were waited for; matrix products, arithmetic and copies ran while one was open for 0% of the time, Pallas kernels for 0%

profile of v9, /device:TPU:8, one launch (start us, length us, event | category | flops | bytes accessed | tf_op | source)
XLA Modules:
  0.0 96.1 jit_solution(17427033469085050671)
XLA Ops:
  0.6 2.4 %shard_map.95 = bf16[32,32,384]{2,1,0:T(8,128)(2,1)} custom-call(s32[1]{0:T(128)} %bitcast.1._.replica_ref, s32[1]{0:T(128)} %bitcast.__.last_ref, bf16[4,2,64,384]{3,2,1,0:T(8,128)(2,1)} %bitcast.10, bf16[4,2,64,384]{3,2,1,0:T(8,128)(2,1)} %bitcast.11), custom_call_target="tpu_custom_call" | custom-call | tf_op jit(solution)/shard_map/pallas_call | solution.py:242
  3.1 0.0 copy-start.2
  3.1 0.0 copy-start.3
  3.1 0.0 copy-start.4
  3.1 33.5 %all_to_all.15.in_ref = bf16[32,32,384]{2,1,0:T(8,128)(2,1)S(1)} all-to-all(bf16[32,32,384]{2,1,0:T(8,128)(2,1)} %shard_map.95), channel_id=1, replica_groups=mesh['dp'=2,'section'=8,'mp'=32] {'mp'}, dimensions={0} | all-to-all | bytes 1572864 | tf_op jit(solution)/shard_map/all_to_all | solution.py:226
  36.6 0.0 copy-done.2
  36.6 0.0 copy-done.3
  36.6 0.0 copy-done.4
  36.6 0.0 copy-start.5
  36.6 5.5 %shard_map.96 = (bf16[32,16,384]{2,1,0:T(8,128)(2,1)S(1)}, f32[2,384,384]{2,1,0:T(8,128)S(1)}, bf16[2,384,384]{2,1,0:T(8,128)(2,1)S(1)}) custom-call(s32[1]{0:T(128)} %bitcast.1._.replica_ref, bf16[256,256]{1,0:T(8,128)(2,1)S(1)} %copy-done.4, bf16[256,256]{1,0:T(8,128)(2,1)S(1)} %copy-done.3, bf16[32,32,384]{2,1,0:T(8,128)(2,1)S(1)} %all_to_all.15.in_ref, ...), custom_call_target="tpu_custom_call" | custom-call | flops 4000000000 | bytes 9000000 | tf_op jit(solution)/shard_map/pallas_call | solution.py:258
  42.1 1.9 %collective-permute-start.1 = (bf16[2,384,384]{2,1,0:T(8,128)(2,1)S(1)}, bf16[2,384,384]{2,1,0:T(8,128)(2,1)S(1)}, u32[]{:S(2)}, u32[]{:S(2)}) collective-permute-start(bf16[2,384,384]{2,1,0:T(8,128)(2,1)S(1)} %get-tuple-element.9), channel_id=1, source_target_pairs={{0,256},{256,0},{1,257},{257,1},{2,258},{258,2},{3,259},{259,3},{4... | collective-permute-start | bytes 1769480 | tf_op jit(solution)/shard_map/ppermute | solution.py:282
  44.0 2.0 %collective-permute-done.1.got_ref = bf16[2,384,384]{2,1,0:T(8,128)(2,1)S(1)} collective-permute-done((bf16[2,384,384]{2,1,0:T(8,128)(2,1)S(1)}, bf16[2,384,384]{2,1,0:T(8,128)(2,1)S(1)}, u32[]{:S(2)}, u32[]{:S(2)}) %collective-permute-start.1) | collective-permute-done | bytes 589856 | tf_op jit(solution)/shard_map/ppermute | solution.py:282
  46.0 0.0 copy-done.5
  46.0 1.2 %shard_map.97 = bf16[4,192,384]{2,1,0:T(8,128)(2,1)} custom-call(bf16[192,192]{1,0:T(8,128)(2,1)S(1)} %copy-done.5, f32[2,384,384]{2,1,0:T(8,128)S(1)} %get-tuple-element.8.keep_ref, bf16[2,384,384]{2,1,0:T(8,128)(2,1)S(1)} %collective-permute-done.1.got_ref), custom_call_target="tpu_custom_call" | custom-call | flops 1000000000 | bytes 3000000 | tf_op jit(solution)/shard_map/pallas_call | solution.py:292
  47.2 0.0 copy-start
  47.2 3.6 %all-to-all-start.1 = ((bf16[4,192,384]{2,1,0:T(8,128)(2,1)}), bf16[4,192,384]{2,1,0:T(8,128)(2,1)S(1)}, u32[]{:S(2)}, u32[]{:S(2)}) async-start(bf16[4,192,384]{2,1,0:T(8,128)(2,1)} %shard_map.97), calls=%async_computation.1 | async-start | bytes 1179648 | tf_op jit(solution)/shard_map/all_to_all | solution.py:226
  50.8 11.0 %collective-permute-start = (bf16[32,16,384]{2,1,0:T(8,128)(2,1)S(1)}, bf16[32,16,384]{2,1,0:T(8,128)(2,1)S(1)}, u32[]{:S(2)}, u32[]{:S(2)}) collective-permute-start(bf16[32,16,384]{2,1,0:T(8,128)(2,1)S(1)} %get-tuple-element.7), channel_id=1, source_target_pairs={{0,224},{32,0},{64,32},{96,64},{128,96},{160,128},{192,160},{224,1... | collective-permute-start | bytes 1179656 | tf_op jit(solution)/shard_map/ppermute | solution.py:284
  61.8 0.0 all-to-all-done.1.parts_ref
  61.8 0.0 copy-done
  61.8 0.3 shard_map.98.cells_ref
  62.1 0.0 copy-start.1
  62.1 8.3 %collective-permute-done.back_ref = bf16[32,16,384]{2,1,0:T(8,128)(2,1)S(1)} collective-permute-done((bf16[32,16,384]{2,1,0:T(8,128)(2,1)S(1)}, bf16[32,16,384]{2,1,0:T(8,128)(2,1)S(1)}, u32[]{:S(2)}, u32[]{:S(2)}) %collective-permute-start) | collective-permute-done | bytes 393248 | tf_op jit(solution)/shard_map/ppermute | solution.py:284
  70.4 0.1 shard_map.99
  70.5 24.6 %all_to_all.16.in_ref = bf16[32,24,384]{2,1,0:T(8,128)(2,1)S(1)} all-to-all(bf16[32,24,384]{2,1,0:T(8,128)(2,1)S(1)} %shard_map.99), channel_id=1, replica_groups=mesh['dp'=2,'section'=8,'mp'=32] {'mp'}, dimensions={0} | all-to-all | bytes 1179648 | tf_op jit(solution)/shard_map/all_to_all | solution.py:226
  95.1 0.0 copy-done.1
  95.1 1.0 %shard_map.100 = (bf16[512,384]{1,0:T(8,128)(2,1)}, f32[12,2,384]{2,1,0:T(2,128)}) custom-call(bf16[256,256]{1,0:T(8,128)(2,1)S(1)} %copy-done.1, bf16[32,24,384]{2,1,0:T(8,128)(2,1)S(1)} %all_to_all.16.in_ref), custom_call_target="tpu_custom_call" | custom-call | flops 100000000 | bytes 1000000 | tf_op jit(solution)/shard_map/pallas_call | solution.py:307
Async XLA Ops:
  3.1 33.5 %copy-start.2 = (bf16[1,4,384,384]{3,2,1,0:T(8,128)(2,1)S(1)}, bf16[1,4,384,384]{3,2,1,0:T(8,128)(2,1)}, u32[]{:S(2)}) copy-start(bf16[1,4,384,384]{3,2,1,0:T(8,128)(2,1)} %param.10) | copy-start | bytes 3538948
  3.1 33.5 %copy-start.3 = (bf16[256,256]{1,0:T(8,128)(2,1)S(1)}, bf16[256,256]{1,0:T(8,128)(2,1)}, u32[]{:S(2)}) copy-start(bf16[256,256]{1,0:T(8,128)(2,1)} %constant.25.clone.back_order_ref) | copy-start | bytes 393220
  3.1 33.5 %copy-start.4 = (bf16[256,256]{1,0:T(8,128)(2,1)S(1)}, bf16[256,256]{1,0:T(8,128)(2,1)}, u32[]{:S(2)}) copy-start(bf16[256,256]{1,0:T(8,128)(2,1)} %constant.24.clone.order_ref) | copy-start | bytes 393220
  36.6 9.4 %copy-start.5 = (bf16[192,192]{1,0:T(8,128)(2,1)S(1)}, bf16[192,192]{1,0:T(8,128)(2,1)}, u32[]{:S(2)}) copy-start(bf16[192,192]{1,0:T(8,128)(2,1)} %constant.26.clone.order_ref) | copy-start | bytes 221188
  42.1 3.9 %collective-permute-start.1 = (bf16[2,384,384]{2,1,0:T(8,128)(2,1)S(1)}, bf16[2,384,384]{2,1,0:T(8,128)(2,1)S(1)}, u32[]{:S(2)}, u32[]{:S(2)}) collective-permute-start(bf16[2,384,384]{2,1,0:T(8,128)(2,1)S(1)} %get-tuple-element.9), channel_id=1, source_target_pairs={{0,256},{256,0},{1,257},{257,1},{2,258},{258,2},{3,259},{259,3},{4... | collective-permute-start | bytes 1769480 | tf_op jit(solution)/shard_map/ppermute | solution.py:282
  47.2 14.6 %copy-start = (bf16[256,192]{1,0:T(8,128)(2,1)S(1)}, bf16[256,192]{1,0:T(8,128)(2,1)}, u32[]{:S(2)}) copy-start(bf16[256,192]{1,0:T(8,128)(2,1)} %constant.27.clone.order_ref) | copy-start | bytes 294916
  47.2 14.6 %all-to-all-start.1 = ((bf16[4,192,384]{2,1,0:T(8,128)(2,1)}), bf16[4,192,384]{2,1,0:T(8,128)(2,1)S(1)}, u32[]{:S(2)}, u32[]{:S(2)}) async-start(bf16[4,192,384]{2,1,0:T(8,128)(2,1)} %shard_map.97), calls=%async_computation.1 | async-start | bytes 1179648 | tf_op jit(solution)/shard_map/all_to_all | solution.py:226
  50.8 19.6 %collective-permute-start = (bf16[32,16,384]{2,1,0:T(8,128)(2,1)S(1)}, bf16[32,16,384]{2,1,0:T(8,128)(2,1)S(1)}, u32[]{:S(2)}, u32[]{:S(2)}) collective-permute-start(bf16[32,16,384]{2,1,0:T(8,128)(2,1)S(1)} %get-tuple-element.7), channel_id=1, source_target_pairs={{0,224},{32,0},{64,32},{96,64},{128,96},{160,128},{192,160},{224,1... | collective-permute-start | bytes 1179656 | tf_op jit(solution)/shard_map/ppermute | solution.py:284
  62.1 33.0 %copy-start.1 = (bf16[256,256]{1,0:T(8,128)(2,1)S(1)}, bf16[256,256]{1,0:T(8,128)(2,1)}, u32[]{:S(2)}) copy-start(bf16[256,256]{1,0:T(8,128)(2,1)} %constant.28.clone.order_ref) | copy-start | bytes 393220

commit v10 on v8

--- a/solution.py
+++ b/solution.py
@@ -18,6 +18,7 @@
 GROUP = 16
 BLOCK = GROUP * CELL
 NX = 4
+NY = 8
 PAD = 8
 VMEM = pl.BlockSpec(memory_space=pltpu.VMEM)
 SMEM = pl.BlockSpec(memory_space=pltpu.SMEM)
@@ -184,21 +185,12 @@
 
 def final_kernel(order_ref, in_ref, received_ref, grads_ref):
     peers, _, width = in_ref.shape
-    groups = peers // GROUP
-    residues = peers * COLS
-    span = GROUP * COLS
-    order = order_ref[...]
-    for g in range(groups):
-        rows = in_ref[g * GROUP : (g + 1) * GROUP, :CELL].reshape(BLOCK, width)
-        moved = reorder(order, rows)
-        for i in range(ROWS):
-            to = slice(i * residues + g * span, i * residues + (g + 1) * span)
-            received_ref[to] = moved[i * span : (i + 1) * span]
+    moved = reorder(order_ref[...], in_ref[:, :CELL].reshape(BLOCK, width))
+    received_ref[...] = moved.reshape(received_ref.shape)
     parts = in_ref[:, CELL:].astype(F32)
-    quarters = NX
-    parts = jnp.sum(parts.reshape(quarters, peers // quarters, PAD, width), axis=1)
-    piece = grads_ref.shape[0] // quarters
-    for q in range(quarters):
+    parts = jnp.sum(parts.reshape(peers // NY, NY, PAD, width), axis=1)
+    piece = grads_ref.shape[0] * NY // peers
+    for q in range(peers // NY):
         for u in range(piece):
             grads_ref[q * piece + u] = parts[q, 2 * u : 2 * u + 2]
 
@@ -298,12 +290,18 @@
     cells = call(collect_kernel, [VMEM] * 2, shape((peers, PAD, width)))(order, parts)
     leaving = call(leave_kernel, [VMEM] * 2, shape((peers, CELL + PAD, width)))(back, cells)
     landed = exchange(leaving)
-    received, weight_grads = call(
-        final_kernel, [VMEM] * 2, (shape((tokens, width)), shape((part, 2, width), F32))
-    )(
-        table(BLOCK, BLOCK, lambda o: ((o >> 2) & 15) * 16 + (o >> 6) * 4 + (o & 3)),
-        landed,
-    )
+    order = table(BLOCK, BLOCK, lambda o: ((o >> 2) & 15) * 16 + (o >> 6) * 4 + (o & 3))
+    received, weight_grads = pl.pallas_call(
+        final_kernel,
+        grid=(peers // GROUP,),
+        in_specs=[
+            pl.BlockSpec((BLOCK, BLOCK), lambda g: (0, 0)),
+            pl.BlockSpec((GROUP, CELL + PAD, width), lambda g: (g, 0, 0)),
+        ],
+        out_specs=(taken, pl.BlockSpec((part * GROUP // peers, 2, width), lambda g: (g, 0, 0))),
+        out_shape=(shape((rows, peers // GROUP, span, width)), shape((part, 2, width), F32)),
+        compiler_params=pltpu.CompilerParams(vmem_limit_bytes=14 * 1024 * 1024),
+    )(order, landed)
     return (received.reshape(activations.shape), weight_grads.transpose(1, 0, 2)[None])
 
 

time: 92 us -> 92.1 us (level)
  no operation moved by 1% of the time
where the time goes in v10:
time: 92.1 us; the launch traced here: 91.7 us
  blocking collectives  58.3 us (63%)
  waiting for transfers between devices  14.6 us (16%)
  Pallas kernels  10.6 us (12%)
  starting transfers between devices  7.45 us (8%)
    all_to_all x2, blocking collectives, exchange(): lax.all_to_all(array, 'mp', split_axis=0, concat_axis=0, axis_index_group...  58.3 us
    all_to_all x1, waiting for transfers between devices, exchange(): lax.all_to_all(array, 'mp', split_axis=0, concat_axis=0, axis_index_group...  8.79 us
    pallas_call x1, Pallas kernels, per_device(): call(attend_kernel, [SMEM] + [VMEM] * 4, (shape((peers, CELL, width)), sh...  5.51 us
    ppermute x1, waiting for transfers between devices, per_device(): lax.ppermute(back, 'section', [(i + 1, i) for i in range(sections - 1)])  3.88 us
    all_to_all x1, starting transfers between devices, exchange(): lax.all_to_all(array, 'mp', split_axis=0, concat_axis=0, axis_index_group...  3.61 us
    pallas_call x1, Pallas kernels, per_device(): pl.pallas_call(pack_kernel, grid=(groups,), in_specs=[SMEM] + [taken] * 2...  2.44 us
    ppermute x1, waiting for transfers between devices, per_device(): got = lax.ppermute(give, 'dp', [(0, 1), (1, 0)])  1.97 us
    ppermute x1, starting transfers between devices, per_device(): got = lax.ppermute(give, 'dp', [(0, 1), (1, 0)])  1.92 us
  transfers between devices with their start and end apart: 3, of which 3 were waited for; matrix products, arithmetic and copies ran while one was open for 0% of the time, Pallas kernels for 0%

profile of v10, /device:TPU:200, one launch (start us, length us, event | category | flops | bytes accessed | tf_op | source)
XLA Modules:
  0.0 91.7 jit_solution(3334067806025723490)
XLA Ops:
  0.6 2.4 %shard_map.95 = bf16[32,32,384]{2,1,0:T(8,128)(2,1)} custom-call(s32[1]{0:T(128)} %bitcast._.replica_ref, bf16[4,2,64,384]{3,2,1,0:T(8,128)(2,1)} %bitcast.9, bf16[4,2,64,384]{3,2,1,0:T(8,128)(2,1)} %bitcast.10), custom_call_target="tpu_custom_call" | custom-call | tf_op jit(solution)/shard_map/pallas_call | solution.py:231
  3.1 0.0 copy-start.2
  3.1 0.0 copy-start.3
  3.1 0.0 copy-start.4
  3.1 33.5 %all_to_all.15.in_ref = bf16[32,32,384]{2,1,0:T(8,128)(2,1)S(1)} all-to-all(bf16[32,32,384]{2,1,0:T(8,128)(2,1)} %shard_map.95), channel_id=1, replica_groups=mesh['dp'=2,'section'=8,'mp'=32] {'mp'}, dimensions={0} | all-to-all | bytes 1572864 | tf_op jit(solution)/shard_map/all_to_all | solution.py:217
  36.6 0.0 copy-done.2
  36.6 0.0 copy-done.3
  36.6 0.0 copy-done.4
  36.6 0.0 copy-start.5
  36.6 5.5 %shard_map.96 = (bf16[32,16,384]{2,1,0:T(8,128)(2,1)S(1)}, f32[2,384,384]{2,1,0:T(8,128)S(1)}, bf16[2,384,384]{2,1,0:T(8,128)(2,1)S(1)}) custom-call(s32[1]{0:T(128)} %bitcast._.replica_ref, bf16[256,256]{1,0:T(8,128)(2,1)S(1)} %copy-done.4, bf16[256,256]{1,0:T(8,128)(2,1)S(1)} %copy-done.3, bf16[32,32,384]{2,1,0:T(8,128)(2,1)S(1)} %all_to_all.15.in_ref, ...), custom_call_target="tpu_custom_call" | custom-call | flops 4000000000 | bytes 9000000 | tf_op jit(solution)/shard_map/pallas_call | solution.py:246
  42.1 1.9 %collective-permute-start.1 = (bf16[2,384,384]{2,1,0:T(8,128)(2,1)S(1)}, bf16[2,384,384]{2,1,0:T(8,128)(2,1)S(1)}, u32[]{:S(2)}, u32[]{:S(2)}) collective-permute-start(bf16[2,384,384]{2,1,0:T(8,128)(2,1)S(1)} %get-tuple-element.9), channel_id=1, source_target_pairs={{0,256},{256,0},{1,257},{257,1},{2,258},{258,2},{3,259},{259,3},{4... | collective-permute-start | bytes 1769480 | tf_op jit(solution)/shard_map/ppermute | solution.py:270
  44.0 2.0 %collective-permute-done.1.got_ref = bf16[2,384,384]{2,1,0:T(8,128)(2,1)S(1)} collective-permute-done((bf16[2,384,384]{2,1,0:T(8,128)(2,1)S(1)}, bf16[2,384,384]{2,1,0:T(8,128)(2,1)S(1)}, u32[]{:S(2)}, u32[]{:S(2)}) %collective-permute-start.1) | collective-permute-done | bytes 589856 | tf_op jit(solution)/shard_map/ppermute | solution.py:270
  46.0 0.0 copy-done.5
  46.0 1.2 %shard_map.97 = bf16[4,192,384]{2,1,0:T(8,128)(2,1)} custom-call(bf16[192,192]{1,0:T(8,128)(2,1)S(1)} %copy-done.5, f32[2,384,384]{2,1,0:T(8,128)S(1)} %get-tuple-element.8.keep_ref, bf16[2,384,384]{2,1,0:T(8,128)(2,1)S(1)} %collective-permute-done.1.got_ref), custom_call_target="tpu_custom_call" | custom-call | flops 1000000000 | bytes 3000000 | tf_op jit(solution)/shard_map/pallas_call | solution.py:280
  47.2 0.0 copy-start
  47.2 3.6 %all-to-all-start.1 = ((bf16[4,192,384]{2,1,0:T(8,128)(2,1)}), bf16[4,192,384]{2,1,0:T(8,128)(2,1)S(1)}, u32[]{:S(2)}, u32[]{:S(2)}) async-start(bf16[4,192,384]{2,1,0:T(8,128)(2,1)} %shard_map.97), calls=%async_computation.1 | async-start | bytes 1179648 | tf_op jit(solution)/shard_map/all_to_all | solution.py:217
  50.8 1.9 %collective-permute-start = (bf16[32,16,384]{2,1,0:T(8,128)(2,1)S(1)}, bf16[32,16,384]{2,1,0:T(8,128)(2,1)S(1)}, u32[]{:S(2)}, u32[]{:S(2)}) collective-permute-start(bf16[32,16,384]{2,1,0:T(8,128)(2,1)S(1)} %get-tuple-element.7), channel_id=1, source_target_pairs={{32,0},{64,32},{96,64},{128,96},{160,128},{192,160},{224,192},{33,... | collective-permute-start | bytes 1179656 | tf_op jit(solution)/shard_map/ppermute | solution.py:272
  52.7 8.8 %all-to-all-done.1.parts_ref = bf16[4,192,384]{2,1,0:T(8,128)(2,1)S(1)} async-done(((bf16[4,192,384]{2,1,0:T(8,128)(2,1)}), bf16[4,192,384]{2,1,0:T(8,128)(2,1)S(1)}, u32[]{:S(2)}, u32[]{:S(2)}) %all-to-all-start.1) | async-done | bytes 589856 | tf_op jit(solution)/shard_map/all_to_all | solution.py:217
  61.5 0.0 copy-done
  61.5 0.3 shard_map.98.cells_ref
  61.8 0.0 copy-start.1
  61.8 3.9 %collective-permute-done.back_ref = bf16[32,16,384]{2,1,0:T(8,128)(2,1)S(1)} collective-permute-done((bf16[32,16,384]{2,1,0:T(8,128)(2,1)S(1)}, bf16[32,16,384]{2,1,0:T(8,128)(2,1)S(1)}, u32[]{:S(2)}, u32[]{:S(2)}) %collective-permute-start) | collective-permute-done | bytes 393248 | tf_op jit(solution)/shard_map/ppermute | solution.py:272
  65.7 0.1 shard_map.99
  65.7 24.9 %all_to_all.16.in_ref = bf16[32,24,384]{2,1,0:T(8,128)(2,1)S(1)} all-to-all(bf16[32,24,384]{2,1,0:T(8,128)(2,1)S(1)} %shard_map.99), channel_id=1, replica_groups=mesh['dp'=2,'section'=8,'mp'=32] {'mp'}, dimensions={0} | all-to-all | bytes 1179648 | tf_op jit(solution)/shard_map/all_to_all | solution.py:217
  90.6 0.0 copy-done.1
  90.6 1.1 %shard_map.100 = (bf16[4,2,64,384]{3,2,1,0:T(8,128)(2,1)}, f32[12,2,384]{2,1,0:T(2,128)}) custom-call(bf16[256,256]{1,0:T(8,128)(2,1)S(1)} %copy-done.1, bf16[32,24,384]{2,1,0:T(8,128)(2,1)S(1)} %all_to_all.16.in_ref), custom_call_target="tpu_custom_call" | custom-call | tf_op jit(solution)/shard_map/pallas_call | solution.py:294
Async XLA Ops:
  3.1 33.5 %copy-start.2 = (bf16[1,4,384,384]{3,2,1,0:T(8,128)(2,1)S(1)}, bf16[1,4,384,384]{3,2,1,0:T(8,128)(2,1)}, u32[]{:S(2)}) copy-start(bf16[1,4,384,384]{3,2,1,0:T(8,128)(2,1)} %param.10) | copy-start | bytes 3538948
  3.1 33.5 %copy-start.3 = (bf16[256,256]{1,0:T(8,128)(2,1)S(1)}, bf16[256,256]{1,0:T(8,128)(2,1)}, u32[]{:S(2)}) copy-start(bf16[256,256]{1,0:T(8,128)(2,1)} %constant.17.clone.back_order_ref) | copy-start | bytes 393220
  3.1 33.5 %copy-start.4 = (bf16[256,256]{1,0:T(8,128)(2,1)S(1)}, bf16[256,256]{1,0:T(8,128)(2,1)}, u32[]{:S(2)}) copy-start(bf16[256,256]{1,0:T(8,128)(2,1)} %constant.16.clone.order_ref) | copy-start | bytes 393220
  36.6 9.4 %copy-start.5 = (bf16[192,192]{1,0:T(8,128)(2,1)S(1)}, bf16[192,192]{1,0:T(8,128)(2,1)}, u32[]{:S(2)}) copy-start(bf16[192,192]{1,0:T(8,128)(2,1)} %constant.18.clone.order_ref) | copy-start | bytes 221188
  42.1 3.9 %collective-permute-start.1 = (bf16[2,384,384]{2,1,0:T(8,128)(2,1)S(1)}, bf16[2,384,384]{2,1,0:T(8,128)(2,1)S(1)}, u32[]{:S(2)}, u32[]{:S(2)}) collective-permute-start(bf16[2,384,384]{2,1,0:T(8,128)(2,1)S(1)} %get-tuple-element.9), channel_id=1, source_target_pairs={{0,256},{256,0},{1,257},{257,1},{2,258},{258,2},{3,259},{259,3},{4... | collective-permute-start | bytes 1769480 | tf_op jit(solution)/shard_map/ppermute | solution.py:270
  47.2 14.3 %copy-start = (bf16[256,192]{1,0:T(8,128)(2,1)S(1)}, bf16[256,192]{1,0:T(8,128)(2,1)}, u32[]{:S(2)}) copy-start(bf16[256,192]{1,0:T(8,128)(2,1)} %constant.19.clone.order_ref) | copy-start | bytes 294916
  47.2 14.3 %all-to-all-start.1 = ((bf16[4,192,384]{2,1,0:T(8,128)(2,1)}), bf16[4,192,384]{2,1,0:T(8,128)(2,1)S(1)}, u32[]{:S(2)}, u32[]{:S(2)}) async-start(bf16[4,192,384]{2,1,0:T(8,128)(2,1)} %shard_map.97), calls=%async_computation.1 | async-start | bytes 1179648 | tf_op jit(solution)/shard_map/all_to_all | solution.py:217
  50.8 14.9 %collective-permute-start = (bf16[32,16,384]{2,1,0:T(8,128)(2,1)S(1)}, bf16[32,16,384]{2,1,0:T(8,128)(2,1)S(1)}, u32[]{:S(2)}, u32[]{:S(2)}) collective-permute-start(bf16[32,16,384]{2,1,0:T(8,128)(2,1)S(1)} %get-tuple-element.7), channel_id=1, source_target_pairs={{32,0},{64,32},{96,64},{128,96},{160,128},{192,160},{224,192},{33,... | collective-permute-start | bytes 1179656 | tf_op jit(solution)/shard_map/ppermute | solution.py:272
  61.8 28.8 %copy-start.1 = (bf16[256,256]{1,0:T(8,128)(2,1)S(1)}, bf16[256,256]{1,0:T(8,128)(2,1)}, u32[]{:S(2)}) copy-start(bf16[256,256]{1,0:T(8,128)(2,1)} %constant.20.clone.order_ref) | copy-start | bytes 393220
